TPU v7x, 128 devices: a whole 4x4x4 slice. The times are simulated.
128 devices in a mesh: wide: 32 (over x, y, z_hi), narrow: 4 (over z_lo, core).
Axes of the slice: x: 4, y: 4, z: 4 (z_hi: 2, z_lo: 2; z = z_hi * 2 + z_lo), core: 2. Of those that a mesh axis runs over, the one named last changes fastest.
Arguments:
- coefficients: float32 [8, 8192, 8192], P(None, 'wide', 'narrow'), may hold values from -0.07 to 0.07
- tensor_blocks: float32 [8, 32, 8192], P(None, 'wide', 'narrow'), may hold values from -6 to 6
- basis_rows: float32 [32, 8192], P(None, ('wide', 'narrow')), may hold values from -1.1 to 1.1, as said below
Outputs:
- new_basis: float32 [32, 8192], P(None, ('wide', 'narrow'))
- projection: float32 [32, 32], replicated
- factor: float32 [32, 32], replicated
Inputs may be any that keep to these rules, and one draw needn't show every extreme that they name: The rows of basis_rows are nearly but not exactly orthonormal: basis_rows basis_rows^T differs from the identity by less than 0.2 in spectral norm.
All inputs are finite; a program needn't handle non-finite values.
Results may differ from a plain program's by a relative error of at most 0.0002.
Values sent between devices are 32-bit elements; how exact they have to be, the bound alone decides.
No kernel may reach another device: no remote copies, remote signals or barrier semaphores. Data moves between devices by JAX's collectives and lax.ppermute only.
A program may use at most 64 MiB of HBM per device.

v0:
```python
import jax
import jax.numpy as jnp
from jax import lax
from jax.sharding import PartitionSpec as P

N = 8192


def in_blocks(value, dim, devices):
    dims = value.shape
    parts = value.reshape(*dims[:dim], devices, dims[dim] // devices, *dims[dim + 1 :])
    return jnp.moveaxis(parts, dim, 0)


def sum_at_owner(value, axis, dim):
    devices = lax.axis_size(axis)
    parts = lax.all_to_all(in_blocks(value, dim, devices), axis, 0, 0, tiled=True)
    return jnp.sum(parts, axis=0)


def total_of_pieces(value, axis):
    parts = lax.all_gather(value, axis)
    return parts.sum(axis=0)


def body(coefficients, tensor_blocks, basis_rows):
    hi = lax.Precision.HIGHEST
    gathered = lax.all_gather(tensor_blocks, "wide", axis=1, tiled=True)
    image = sum_at_owner(
        jnp.einsum("kic,krc->ri", gathered, coefficients, precision=hi), "narrow", 0
    ).T
    local_first = jnp.dot(basis_rows, image.T, precision=hi)
    first = total_of_pieces(local_first, ("wide", "narrow"))
    once = image - jnp.dot(first.T, basis_rows, precision=hi)
    second = total_of_pieces(jnp.dot(basis_rows, once.T, precision=hi), ("wide", "narrow"))
    twice = once - jnp.dot(second.T, basis_rows, precision=hi)
    gram = total_of_pieces(jnp.dot(twice, twice.T, precision=hi), ("wide", "narrow")) / N
    factor = jnp.linalg.cholesky(gram)
    new_basis = lax.linalg.triangular_solve(factor, twice, left_side=True, lower=True)
    return (new_basis, first + second, factor)


def solution(mesh):
    in_specs = (P(None, "wide", "narrow"), P(None, "wide", "narrow"), P(None, ("wide", "narrow")))
    out_specs = (P(None, ("wide", "narrow")), P(), P())
    return jax.shard_map(body, mesh=mesh, in_specs=in_specs, out_specs=out_specs, check_vma=False)
```

profile of v0, /device:TPU:0, one launch (start us, length us, event | category | flops | bytes accessed | tf_op | source)
XLA Modules:
  0.0 234.5 jit_solution(12183286619266672822)
XLA Ops:
  7.2 1.5 copy.8
  8.7 77.1 %all-gather.5.cloned.1.call-done = f32[8,32,2048]{2,0,1:T(8,128)} async-done(((f32[8,1,2048]{2,0,1:T(8,128)}), f32[8,32,2048]{2,0,1:T(8,128)}) %all-gather.5.cloned.1.call-update) | async-done | bytes 2097168 | tf_op jit(solution)/shard_map/all_gather | solution.py:28
  85.8 18.0 %fusion.2 = f32[256,32]{0,1:T(8,128)S(1)} fusion(f32[8,256,2048]{2,1,0:T(8,128)} %param.3, f32[8,32,2048]{2,0,1:T(8,128)} %all-gather.5.cloned.1.call-done), kind=kOutput, calls=%fused_computation.2 | convolution fusion | flops 1610612736 | bytes 18907136 | tf_op jit(solution)/shard_map/kic,krc->ri/dot_general | solution.py:30
  104.0 6.3 %all_to_all.5 = f32[4,1,2048]{2,1,0:T(1,128)S(1)} all-to-all(f32[4,1,2048]{2,1,0:T(1,128)S(1)} %reshape.23), channel_id=1, replica_groups=mesh['wide'=32,'narrow'=4] {'narrow'}, dimensions={0} | all-to-all | bytes 65536 | tf_op jit(solution)/shard_map/all_to_all | solution.py:17
  110.3 0.5 broadcast.50
  110.8 0.7 reduce.6
  111.5 0.1 reshape.24
  111.6 0.1 convolution_bitcast_fusion.1
  111.9 35.0 %all-gather = f32[4096,32]{1,0:T(8,128)S(1)} all-gather(f32[32,32]{1,0:T(8,128)S(1)} %copy.11), channel_id=2, replica_groups=mesh['wide'=32,'narrow'=4] {'wide','narrow'}, dimensions={0}, use_global_device_ids=true | all-gather | bytes 528384 | tf_op jit(solution)/shard_map/all_gather | solution.py:22
  146.9 0.2 reduce_sum.39
  147.1 0.2 convolution_subtract_fusion.1
  147.3 0.1 convolution_bitcast_fusion
  147.5 35.2 %all-gather.1 = f32[4096,32]{1,0:T(8,128)S(1)} all-gather(f32[32,32]{1,0:T(8,128)S(1)} %copy.13), channel_id=3, replica_groups=mesh['wide'=32,'narrow'=4] {'wide','narrow'}, dimensions={0}, use_global_device_ids=true | all-gather | bytes 528384 | tf_op jit(solution)/shard_map/all_gather | solution.py:22
  182.8 0.2 reduce_sum.40
  183.0 0.2 convolution_subtract_fusion
  183.3 0.1 fusion.8
  183.5 35.1 %all-gather.2 = f32[4096,32]{1,0:T(8,128)S(1)} all-gather(f32[32,32]{1,0:T(8,128)S(1)} %fusion.8), channel_id=4, replica_groups=mesh['wide'=32,'narrow'=4] {'wide','narrow'}, dimensions={0}, use_global_device_ids=true | all-gather | bytes 528384 | tf_op jit(solution)/shard_map/all_gather | solution.py:22
  218.6 0.2 reduce_sum.41
  218.8 2.9 %cholesky.16 = f32[32,32]{1,0:T(8,128)S(1)} custom-call(f32[32,32]{1,0:T(8,128)S(1)} %fusion.7), custom_call_target="Cholesky" | custom-call | tf_op jit(solution)/shard_map/jit(cholesky)/cholesky | solution.py:38
  221.8 0.6 compare_reduce_fusion
  222.4 1.3 select_bitcast_fusion
  223.7 2.4 %custom-call.6 = f32[1,32,32]{1,2,0:T(8,128)S(1)} custom-call(f32[1,32,32]{2,1,0:T(8,128)S(1)} %get-tuple-element.6), custom_call_target="InvertDiagBlocksLowerTriangular" | custom-call | tf_op jit(solution)/shard_map/triangular_solve | solution.py:39
  226.1 0.8 fusion.5
  227.0 0.7 copy.16
  (16 shorter events, 0.7 us)
Async XLA Ops:
  7.2 104.5 %copy-start = (f32[32,64]{1,0:T(8,128)S(1)}, f32[32,64]{1,0:T(8,128)}, u32[]{:S(2)}) copy-start(f32[32,64]{1,0:T(8,128)} %param.5) | copy-start | bytes 24580
  7.2 78.6 %all-gather.5.cloned.1.call-start = ((), (), s32[]{:S(2)}) async-start(), calls=%async_computation.1 | async-start | bytes 2162688 | tf_op jit(solution)/shard_map/all_gather | solution.py:28
Sparse Core Ops, SparseCore 0:
  11.0 74.7 all-gather.4
where the time goes:
time: 236 us; the launch traced here: 235 us
  blocking collectives  112 us (47%)
  waiting for transfers between devices  77.1 us (33%)
  matrix products  19.7 us (8%)
  between operations  14.1 us (6%)
  other arithmetic  8.63 us (4%)
  local copies, waits for them, and re-layouts  3.34 us (1%)
    all_gather x3, blocking collectives, total_of_pieces(): parts = lax.all_gather(value, axis)  105 us
    all_gather x1, waiting for transfers between devices, body(): gathered = lax.all_gather(tensor_blocks, 'wide', axis=1, tiled=True)  77.1 us
    dot_general x1, matrix products, body(): jnp.einsum('kic,krc->ri', gathered, coefficients, precision=hi)  18 us
    all_to_all x1, blocking collectives, sum_at_owner(): lax.all_to_all(in_blocks(value, dim, devices), axis, 0, 0, tiled=True)  6.3 us
  transfers between devices with their start and end apart: 1, of which 1 were waited for; matrix products, arithmetic and copies ran while one was open for 0% of the time, Pallas kernels for 0%

commit v1 on v0

v1 whole, which is shorter than its diff:
```python
import functools

import jax
import jax.numpy as jnp
from jax import lax
from jax.experimental import pallas as pl
from jax.experimental.pallas import tpu as pltpu
from jax.sharding import PartitionSpec as P

N = 8192
K = 8
R = 32
XS = 4
YS = 4
HALF = 1024
AXES = ("wide", "narrow")
HI = lax.Precision.HIGHEST
NT = (((1,), (1,)), ((), ()))
NN = (((1,), (0,)), ((), ()))
VM = pl.BlockSpec(memory_space=pltpu.VMEM)


def flat(x, y, zh, zl, core):
    return ((x * YS + y) * 2 + zh) * 4 + zl * 2 + core


def sources(source_of):
    pairs = []
    for x in range(XS):
        for y in range(YS):
            for zh in range(2):
                for zl in range(2):
                    for core in range(2):
                        here = (x, y, zh, zl, core)
                        pairs.append((flat(*source_of(*here)), flat(*here)))
    return pairs


def from_x(step):
    return sources(lambda x, y, zh, zl, core: ((x + step) % XS, y, zh, zl, core))


def from_y(step):
    return sources(lambda x, y, zh, zl, core: (x, (y + step) % YS, zh, zl, core))


FROM_ZH = sources(lambda x, y, zh, zl, core: (x, y, 1 - zh, zl, core))
FROM_ZL = sources(lambda x, y, zh, zl, core: (x, y, zh, 1 - zl, core))
FROM_CORE = sources(lambda x, y, zh, zl, core: (x, y, zh, zl, 1 - core))
FROM_Z = sources(lambda x, y, zh, zl, core: (x, y, 1 - zh, 1 - zl, core))
EVEN = (1, 0, 3, 2)
ODD = (3, 2, 1, 0)


def pair_x(partner):
    return sources(lambda x, y, zh, zl, core: (partner[x], y, zh, zl, core))


def pair_y(partner):
    return sources(lambda x, y, zh, zl, core: (x, partner[y], zh, zl, core))


def move(value, pairs):
    return lax.ppermute(value, AXES, pairs)


def split(value):
    high = value.astype(jnp.bfloat16)
    low = (value - high.astype(jnp.float32)).astype(jnp.bfloat16)
    return high, low


def split_kernel(block_ref, high_ref, low_ref):
    k = pl.program_id(0)
    high, low = split(block_ref[0])
    high_ref[k] = high
    low_ref[k] = low


def split_coefficients(coefficients):
    shape = coefficients.shape
    out = pltpu.VMEM(shape, jnp.bfloat16)
    return pl.pallas_call(
        split_kernel,
        grid=(shape[0],),
        in_specs=[pl.BlockSpec((1, *shape[1:]), lambda k: (k, 0, 0))],
        out_specs=[VM, VM],
        out_shape=[out, out],
        compiler_params=pltpu.CompilerParams(vmem_limit_bytes=10 << 20),
        name="split",
    )(coefficients)


def image_kernel(place_ref, *refs):
    pieces = (refs[0:4], refs[4:8])
    high_ref, low_ref, out_ref, held = refs[8:]
    for half in range(2):
        total = None
        for k in range(K):
            rows = jnp.concatenate([piece[:, k, :] for piece in pieces[half]], axis=0)
            rows_high, rows_low = split(rows)
            both = jnp.concatenate([rows_high, rows_low], axis=0)
            cols = pl.ds(half * HALF, HALF)
            main = lax.dot_general(both, high_ref[k, :, cols], NT, preferred_element_type=jnp.float32)
            rest = lax.dot_general(rows_high, low_ref[k, :, cols], NT, preferred_element_type=jnp.float32)
            part = main[:R] + main[R:] + rest
            total = part if total is None else total + part
        held[half] = total
    x0, y0, zh0 = place_ref[0], place_ref[1], place_ref[2]
    for x in range(XS):
        for y in range(YS):
            for zh in range(2):
                dx = (x - x0 + XS) % XS
                dy = (y - y0 + YS) % YS
                dz = (zh + zh0) % 2
                a = held[0, pl.ds(dy * 8 + dx * 2 + dz, 1), :]
                b = held[1, pl.ds(dx * 8 + dy * 2 + dz, 1), :]
                out_ref[pl.ds((x * YS + y) * 2 + zh, 1), :] = a + b


def image_part(place, pieces, high, low):
    rows = high.shape[1]
    return pl.pallas_call(
        image_kernel,
        in_specs=[pl.BlockSpec(memory_space=pltpu.SMEM)] + [VM] * 10,
        out_specs=VM,
        out_shape=jax.ShapeDtypeStruct((R, rows), jnp.float32),
        scratch_shapes=[pltpu.VMEM((2, R, rows), jnp.float32)],
        compiler_params=pltpu.CompilerParams(vmem_limit_bytes=6 << 20),
        name="image",
    )(place, *pieces, high, low)


def products_kernel(mine_ref, other_ref, basis_ref, image_ref, products_ref):
    image = mine_ref[...] + other_ref[...]
    image_ref[...] = image
    basis = basis_ref[...]
    both = jnp.concatenate([image, basis], axis=0)
    of_image = lax.dot_general(image, both, NT, precision=HI, preferred_element_type=jnp.float32)
    of_basis = lax.dot_general(basis, both, NT, precision=HI, preferred_element_type=jnp.float32)
    products_ref[...] = jnp.concatenate([of_image, of_basis], axis=1)


def products(mine, other, basis):
    return pl.pallas_call(
        products_kernel,
        in_specs=[VM] * 3,
        out_specs=[VM] * 2,
        out_shape=[
            jax.ShapeDtypeStruct(mine.shape, jnp.float32),
            jax.ShapeDtypeStruct((R, 4 * R), jnp.float32),
        ],
        compiler_params=pltpu.CompilerParams(vmem_limit_bytes=2 << 20),
        name="products",
    )(mine, other, basis)


def final_kernel(place_ref, products_ref, image_ref, basis_ref, new_ref, projection_ref, factor_ref):
    dot = functools.partial(lax.dot_general, precision=HI, preferred_element_type=jnp.float32)
    squares = products_ref[:, 0:R]
    first_t = products_ref[:, R : 2 * R]
    first = products_ref[:, 2 * R : 3 * R]
    basis_gram = products_ref[:, 3 * R : 4 * R]
    projection = 2.0 * first - dot(basis_gram, first, NN)
    projection_t = 2.0 * first_t - dot(first_t, basis_gram, NN)
    projection_ref[...] = projection
    left = first - dot(basis_gram, projection, NN)
    gram = (squares - dot(first_t, projection, NN) - dot(projection_t, left, NN)) / N
    narrow = place_ref[3]
    own = image_ref[:, 0:64]
    for n in range(1, 4):
        own = jnp.where(narrow == n, image_ref[:, n * 64 : (n + 1) * 64], own)
    twice = own - dot(projection_t, basis_ref[...], NN)
    work = jnp.concatenate([gram, jnp.zeros((R, R), jnp.float32), twice], axis=1)
    lane = lax.broadcasted_iota(jnp.int32, (1, 4 * R), 1)
    done = []
    for k in range(R):
        row = work[k : k + 1, :]
        column = work[:, k : k + 1]
        scale = 1.0 / jnp.sqrt(work[k : k + 1, k : k + 1])
        unit = row * scale
        done.append(jnp.where(lane >= k, unit, 0.0))
        work = work - (column * scale) * unit
    rows = jnp.concatenate(done, axis=0)
    factor_ref[...] = rows[:, 0:R].T
    new_ref[...] = rows[:, 2 * R : 4 * R]


def final(place, total, image, basis):
    return pl.pallas_call(
        final_kernel,
        in_specs=[pl.BlockSpec(memory_space=pltpu.SMEM)] + [VM] * 3,
        out_specs=[VM] * 3,
        out_shape=[
            jax.ShapeDtypeStruct(basis.shape, jnp.float32),
            jax.ShapeDtypeStruct((R, R), jnp.float32),
            jax.ShapeDtypeStruct((R, R), jnp.float32),
        ],
        compiler_params=pltpu.CompilerParams(vmem_limit_bytes=2 << 20),
        name="final",
    )(place, total, image, basis)


def body(coefficients, tensor_blocks, basis_rows):
    wide = lax.axis_index("wide")
    narrow = lax.axis_index("narrow")
    place = jnp.stack([wide // (2 * YS), (wide // 2) % YS, wide % 2, narrow]).astype(jnp.int32)

    own = tensor_blocks.reshape(K, 2 * HALF)
    across = move(own, FROM_ZH)
    pair = jnp.stack([own, across])
    a, b = pair[:, :, :HALF], pair[:, :, HALF:]
    a = jnp.concatenate([a] + [move(a, from_x(s)) for s in (1, 2, 3)])
    b = jnp.concatenate([b] + [move(b, from_y(s)) for s in (1, 2, 3)])
    pieces_a = [a] + [move(a, from_y(s)) for s in (1, 2, 3)]
    pieces_b = [b] + [move(b, from_x(s)) for s in (1, 2, 3)]

    high, low = split_coefficients(coefficients)

    other = move(basis_rows, FROM_CORE)
    at_core = narrow % 2 == 0
    basis = jnp.concatenate([jnp.where(at_core, basis_rows, other), jnp.where(at_core, other, basis_rows)], axis=1)
    other = move(basis, FROM_ZL)
    at_zl = narrow // 2 == 0
    basis = jnp.concatenate([jnp.where(at_zl, basis, other), jnp.where(at_zl, other, basis)], axis=1)

    part = image_part(place, pieces_a + pieces_b, high, low)
    part = part + move(part, FROM_CORE)
    image, total = products(part, move(part, FROM_ZL), basis)
    for pairs in (FROM_Z, pair_x(EVEN), pair_x(ODD), pair_y(EVEN), pair_y(ODD)):
        total = total + move(total, pairs)
    return tuple(final(place, total, image, basis_rows))


def solution(mesh):
    in_specs = (P(None, "wide", "narrow"), P(None, "wide", "narrow"), P(None, ("wide", "narrow")))
    out_specs = (P(None, ("wide", "narrow")), P(), P())
    return jax.shard_map(body, mesh=mesh, in_specs=in_specs, out_specs=out_specs, check_vma=False)
```

time: 236 us -> 99 us (0.42)
  blocking collectives: 112 us -> 0 us
  waiting for transfers between devices: 77.1 us -> 36.5 us
  starting transfers between devices: 0.04 us -> 26.9 us
  matrix products: 19.7 us -> 0 us
  local copies, waits for them, and re-layouts: 3.34 us -> 19.9 us
  Pallas kernels: 0 us -> 13.5 us
  between operations: 14.1 us -> 0.74 us
  other arithmetic: 8.63 us -> 1.03 us
    all_gather x3 -> x0, blocking collectives: 105 us -> none  [total_of_pieces(): parts = lax.all_gather(value, axis)]
    all_gather x1 -> x0, waiting for transfers between devices: 77.1 us -> none  [body(): gathered = lax.all_gather(tensor_blocks, 'wide', axis=1, tiled=True)]
    ppermute x0 -> x22, waiting for transfers between devices: none -> 36.5 us  [move(): return lax.ppermute(value, AXES, pairs)]
    ppermute x0 -> x22, starting transfers between devices: none -> 26.9 us  [move(): return lax.ppermute(value, AXES, pairs)]
    dot_general x6 -> x0, matrix products: 18.8 us -> none  [the longest x1 18 us: body(): jnp.einsum('kic,krc->ri', gathered, coefficients, precision=hi)]
    unnamed x8 -> x13, local copies, waits for them, and re-layouts: 2.51 us -> 19.9 us
    pallas_call x0 -> x4, Pallas kernels: none -> 13.5 us  [the longest x1 5.79 us: image_part(): pl.pallas_call(image_kernel, in_specs=[pl.BlockSpec(memory_space=pltpu.SM...]
    another operation x5 -> x2, other arithmetic: 7.29 us -> 0.09 us  [the longest x1 0.08 us: body(): jnp.stack([wide // (2 * YS), wide // 2 % YS, wide % 2, narrow])]
  transfers between devices with their start and end apart: 1 -> 22, of which waited for: 1 -> 13; matrix products, arithmetic and copies ran while one was open for 0% -> 1% of each run, Pallas kernels for 0% -> 8%
where the time goes in v1:
time: 99 us; the launch traced here: 98.6 us
  waiting for transfers between devices  36.5 us (37%)
  starting transfers between devices  26.9 us (27%)
  local copies, waits for them, and re-layouts  19.9 us (20%)
  Pallas kernels  13.5 us (14%)
  other arithmetic  1.03 us (1%)
    ppermute x22, waiting for transfers between devices, move(): return lax.ppermute(value, AXES, pairs)  36.5 us
    ppermute x22, starting transfers between devices, move(): return lax.ppermute(value, AXES, pairs)  26.9 us
    unnamed x13, local copies, waits for them, and re-layouts  19.9 us
    pallas_call x1, Pallas kernels, image_part(): pl.pallas_call(image_kernel, in_specs=[pl.BlockSpec(memory_space=pltpu.SM...  5.79 us
    pallas_call x1, Pallas kernels, final(): pl.pallas_call(final_kernel, in_specs=[pl.BlockSpec(memory_space=pltpu.SM...  5.02 us
    pallas_call x1, Pallas kernels, split_coefficients(): pl.pallas_call(split_kernel, grid=(shape[0],), in_specs=[pl.BlockSpec((1,...  2.45 us
  transfers between devices with their start and end apart: 22, of which 13 were waited for; matrix products, arithmetic and copies ran while one was open for 1% of the time, Pallas kernels for 8%

profile of v1, /device:TPU:0, one launch (start us, length us, event | category | flops | bytes accessed | tf_op | source)
XLA Modules:
  0.0 98.6 jit_solution(16984322646755065823)
XLA Ops:
  1.5 4.0 %collective-permute-start = (f32[8,2048]{1,0:T(8,128)S(1)}, f32[8,2048]{1,0:T(8,128)S(1)}, u32[]{:S(2)}, u32[]{:S(2)}) collective-permute-start(f32[8,2048]{1,0:T(8,128)S(1)} %bitcast.10), channel_id=1, source_target_pairs={{4,0},{5,1},{6,2},{7,3},{0,4},{1,5},{2,6},{3,7},{12,8},{13,9},{14,... | collective-permute-start | bytes 196616 | tf_op jit(solution)/shard_map/ppermute | solution.py:64
  5.5 2.2 %collective-permute-done = f32[8,2048]{1,0:T(8,128)S(1)} collective-permute-done((f32[8,2048]{1,0:T(8,128)S(1)}, f32[8,2048]{1,0:T(8,128)S(1)}, u32[]{:S(2)}, u32[]{:S(2)}) %collective-permute-start) | collective-permute-done | bytes 65568 | tf_op jit(solution)/shard_map/ppermute | solution.py:64
  7.8 3.1 %collective-permute-start.7 = (f32[2,8,1024]{2,1,0:T(8,128)S(1)}, f32[2,8,1024]{2,1,0:T(8,128)S(1)}, u32[]{:S(2)}, u32[]{:S(2)}) collective-permute-start(f32[2,8,1024]{2,1,0:T(8,128)S(1)} %get-tuple-element.11), channel_id=1, source_target_pairs={{8,0},{9,1},{10,2},{11,3},{12,4},{13,5},{14,6},{15,7},{16,8},{17,9... | collective-permute-start | bytes 196616 | tf_op jit(solution)/shard_map/ppermute | solution.py:64
  12.8 3.9 %collective-permute-done.8 = f32[2,8,1024]{2,1,0:T(8,128)S(1)} collective-permute-done((f32[2,8,1024]{2,1,0:T(8,128)S(1)}, f32[2,8,1024]{2,1,0:T(8,128)S(1)}, u32[]{:S(2)}, u32[]{:S(2)}) %collective-permute-start.8) | collective-permute-done | bytes 65568 | tf_op jit(solution)/shard_map/ppermute | solution.py:64
  17.4 2.8 %collective-permute-start.10 = (f32[8,8,1024]{2,1,0:T(8,128)S(1)}, f32[8,8,1024]{2,1,0:T(8,128)S(1)}, u32[]{:S(2)}, u32[]{:S(2)}) collective-permute-start(f32[8,8,1024]{2,1,0:T(8,128)S(1)} %pad_maximum_fusion.1.refs_4_), channel_id=1, source_target_pairs={{32,0},{33,1},{34,2},{35,3},{36,4},{37,5},{38,6},{39,7},{40,8},{41... | collective-permute-start | bytes 786440 | tf_op jit(solution)/shard_map/ppermute | solution.py:64
  22.4 3.9 %collective-permute-done.1 = f32[2,8,1024]{2,1,0:T(8,128)S(1)} collective-permute-done((f32[2,8,1024]{2,1,0:T(8,128)S(1)}, f32[2,8,1024]{2,1,0:T(8,128)S(1)}, u32[]{:S(2)}, u32[]{:S(2)}) %collective-permute-start.1) | collective-permute-done | bytes 65568 | tf_op jit(solution)/shard_map/ppermute | solution.py:64
  26.3 2.0 %collective-permute-start.11 = (f32[8,8,1024]{2,1,0:T(8,128)S(1)}, f32[8,8,1024]{2,1,0:T(8,128)S(1)}, u32[]{:S(2)}, u32[]{:S(2)}) collective-permute-start(f32[8,8,1024]{2,1,0:T(8,128)S(1)} %pad_maximum_fusion.1.refs_4_), channel_id=1, source_target_pairs={{64,0},{65,1},{66,2},{67,3},{68,4},{69,5},{70,6},{71,7},{72,8},{73... | collective-permute-start | bytes 786440 | tf_op jit(solution)/shard_map/ppermute | solution.py:64
  28.3 2.5 %collective-permute-start.12 = (f32[8,8,1024]{2,1,0:T(8,128)S(1)}, f32[8,8,1024]{2,1,0:T(8,128)S(1)}, u32[]{:S(2)}, u32[]{:S(2)}) collective-permute-start(f32[8,8,1024]{2,1,0:T(8,128)S(1)} %pad_maximum_fusion.1.refs_4_), channel_id=1, source_target_pairs={{96,0},{97,1},{98,2},{99,3},{100,4},{101,5},{102,6},{103,7},{104,8... | collective-permute-start | bytes 786440 | tf_op jit(solution)/shard_map/ppermute | solution.py:64
  34.2 2.7 %collective-permute-done.11.refs_6_ = f32[8,8,1024]{2,1,0:T(8,128)S(1)} collective-permute-done((f32[8,8,1024]{2,1,0:T(8,128)S(1)}, f32[8,8,1024]{2,1,0:T(8,128)S(1)}, u32[]{:S(2)}, u32[]{:S(2)}) %collective-permute-start.11) | collective-permute-done | bytes 262176 | tf_op jit(solution)/shard_map/ppermute | solution.py:64
  38.4 5.8 %copy-done = f32[8,256,2048]{2,1,0:T(8,128)S(1)} copy-done((f32[8,256,2048]{2,1,0:T(8,128)S(1)}, f32[8,256,2048]{2,1,0:T(8,128)}, u32[]{:S(2)}) %copy-start) | copy-done | bytes 16777240
  44.2 2.4 %split.1 = (bf16[8,256,2048]{2,1,0:T(8,128)(2,1)S(1)}, bf16[8,256,2048]{2,1,0:T(8,128)(2,1)S(1)}) custom-call(f32[8,256,2048]{2,1,0:T(8,128)S(1)} %copy-done), custom_call_target="tpu_custom_call" | custom-call | tf_op jit(solution)/shard_map/split/pallas_call | solution.py:83
  46.7 3.3 %copy-done.1 = bf16[8,256,2048]{2,1,0:T(8,128)(2,1)} copy-done((bf16[8,256,2048]{2,1,0:T(8,128)(2,1)}, bf16[8,256,2048]{2,1,0:T(8,128)(2,1)S(1)}, u32[]{:S(2)}) %copy-start.1) | copy-done | bytes 8388632
  49.9 3.2 %copy-done.3 = bf16[8,256,2048]{2,1,0:T(8,128)(2,1)} copy-done((bf16[8,256,2048]{2,1,0:T(8,128)(2,1)}, bf16[8,256,2048]{2,1,0:T(8,128)(2,1)S(1)}, u32[]{:S(2)}) %copy-start.3) | copy-done | bytes 8388632
  53.2 3.4 %copy-done.2 = bf16[8,256,2048]{2,1,0:T(8,128)(2,1)S(1)} copy-done((bf16[8,256,2048]{2,1,0:T(8,128)(2,1)S(1)}, bf16[8,256,2048]{2,1,0:T(8,128)(2,1)}, u32[]{:S(2)}) %copy-start.2) | copy-done | bytes 8388632
  56.6 3.4 %copy-done.4 = bf16[8,256,2048]{2,1,0:T(8,128)(2,1)S(1)} copy-done((bf16[8,256,2048]{2,1,0:T(8,128)(2,1)S(1)}, bf16[8,256,2048]{2,1,0:T(8,128)(2,1)}, u32[]{:S(2)}) %copy-start.4) | copy-done | bytes 8388632
  59.9 5.8 %image.1 = f32[32,256]{1,0:T(8,128)S(1)} custom-call(s32[4]{0:T(128)S(1)} %pad_add_fusion.place_ref, f32[8,8,1024]{2,1,0:T(8,128)S(1)} %pad_maximum_fusion.refs_0_, f32[8,8,1024]{2,1,0:T(8,128)S(1)} %collective-permute-done.4.refs_1_, f32[8,8,1024]{2,1,0:T(8,128)S(1)} %collective-permute-done.5.refs_2_, f32[8,8,1024]{2,1,0:T(8,128)S(1)} %collective-permute-done.6.refs_3_, ...), custom_call_target="tpu_custom_call" | custom-call | tf_op jit(solution)/shard_map/image/pallas_call | solution.py:123
  67.6 3.3 %collective-permute-done.14.other_ref = f32[32,256]{1,0:T(8,128)S(1)} collective-permute-done((f32[32,256]{1,0:T(8,128)S(1)}, f32[32,256]{1,0:T(8,128)S(1)}, u32[]{:S(2)}, u32[]{:S(2)}) %collective-permute-start.14) | collective-permute-done | bytes 32800 | tf_op jit(solution)/shard_map/ppermute | solution.py:64
  71.2 2.6 %collective-permute-start.17 = (f32[32,128]{1,0:T(8,128)S(1)}, f32[32,128]{1,0:T(8,128)S(1)}, u32[]{:S(2)}, u32[]{:S(2)}) collective-permute-start(f32[32,128]{1,0:T(8,128)S(1)} %get-tuple-element.9), channel_id=1, source_target_pairs={{6,0},{7,1},{4,2},{5,3},{2,4},{3,5},{0,6},{1,7},{14,8},{15,9},{12,... | collective-permute-start | bytes 49160 | tf_op jit(solution)/shard_map/ppermute | solution.py:64
  73.8 2.4 %collective-permute-done.17 = f32[32,128]{1,0:T(8,128)S(1)} collective-permute-done((f32[32,128]{1,0:T(8,128)S(1)}, f32[32,128]{1,0:T(8,128)S(1)}, u32[]{:S(2)}, u32[]{:S(2)}) %collective-permute-start.17) | collective-permute-done | bytes 16416 | tf_op jit(solution)/shard_map/ppermute | solution.py:64
  76.2 3.7 %collective-permute-done.18 = f32[32,128]{1,0:T(8,128)S(1)} collective-permute-done((f32[32,128]{1,0:T(8,128)S(1)}, f32[32,128]{1,0:T(8,128)S(1)}, u32[]{:S(2)}, u32[]{:S(2)}) %collective-permute-start.18) | collective-permute-done | bytes 16416 | tf_op jit(solution)/shard_map/ppermute | solution.py:64
  80.8 4.2 %collective-permute-done.19 = f32[32,128]{1,0:T(8,128)S(1)} collective-permute-done((f32[32,128]{1,0:T(8,128)S(1)}, f32[32,128]{1,0:T(8,128)S(1)}, u32[]{:S(2)}, u32[]{:S(2)}) %collective-permute-start.19) | collective-permute-done | bytes 16416 | tf_op jit(solution)/shard_map/ppermute | solution.py:64
  84.9 3.7 %collective-permute-done.20 = f32[32,128]{1,0:T(8,128)S(1)} collective-permute-done((f32[32,128]{1,0:T(8,128)S(1)}, f32[32,128]{1,0:T(8,128)S(1)}, u32[]{:S(2)}, u32[]{:S(2)}) %collective-permute-start.20) | collective-permute-done | bytes 16416 | tf_op jit(solution)/shard_map/ppermute | solution.py:64
  89.3 4.3 %collective-permute-done.21 = f32[32,128]{1,0:T(8,128)S(1)} collective-permute-done((f32[32,128]{1,0:T(8,128)S(1)}, f32[32,128]{1,0:T(8,128)S(1)}, u32[]{:S(2)}, u32[]{:S(2)}) %collective-permute-start.21) | collective-permute-done | bytes 16416 | tf_op jit(solution)/shard_map/ppermute | solution.py:64
  93.6 5.0 %final.1 = (f32[32,64]{1,0:T(8,128)}, f32[32,32]{1,0:T(8,128)}, f32[32,32]{1,0:T(8,128)}) custom-call(s32[4]{0:T(128)S(1)} %pad_add_fusion.place_ref, f32[32,128]{1,0:T(8,128)S(1)} %add.39.products_ref, f32[32,256]{1,0:T(8,128)S(1)} %get-tuple-element.10.image_ref, f32[32,64]{1,0:T(8,128)S(1)} %copy-done.5), custom_call_target="tpu_custom_call" | custom-call | tf_op jit(solution)/shard_map/final/pallas_call | solution.py:190
  (51 shorter events, 14.2 us)
Async XLA Ops:
  1.5 6.3 %collective-permute-start = (f32[8,2048]{1,0:T(8,128)S(1)}, f32[8,2048]{1,0:T(8,128)S(1)}, u32[]{:S(2)}, u32[]{:S(2)}) collective-permute-start(f32[8,2048]{1,0:T(8,128)S(1)} %bitcast.10), channel_id=1, source_target_pairs={{4,0},{5,1},{6,2},{7,3},{0,4},{1,5},{2,6},{3,7},{12,8},{13,9},{14,... | collective-permute-start | bytes 196616 | tf_op jit(solution)/shard_map/ppermute | solution.py:64
  7.8 5.0 %collective-permute-start.7 = (f32[2,8,1024]{2,1,0:T(8,128)S(1)}, f32[2,8,1024]{2,1,0:T(8,128)S(1)}, u32[]{:S(2)}, u32[]{:S(2)}) collective-permute-start(f32[2,8,1024]{2,1,0:T(8,128)S(1)} %get-tuple-element.11), channel_id=1, source_target_pairs={{8,0},{9,1},{10,2},{11,3},{12,4},{13,5},{14,6},{15,7},{16,8},{17,9... | collective-permute-start | bytes 196616 | tf_op jit(solution)/shard_map/ppermute | solution.py:64
  10.9 5.8 %collective-permute-start.8 = (f32[2,8,1024]{2,1,0:T(8,128)S(1)}, f32[2,8,1024]{2,1,0:T(8,128)S(1)}, u32[]{:S(2)}, u32[]{:S(2)}) collective-permute-start(f32[2,8,1024]{2,1,0:T(8,128)S(1)} %get-tuple-element.11), channel_id=1, source_target_pairs={{16,0},{17,1},{18,2},{19,3},{20,4},{21,5},{22,6},{23,7},{24,8},{25... | collective-permute-start | bytes 196616 | tf_op jit(solution)/shard_map/ppermute | solution.py:64
  11.5 5.8 %collective-permute-start.9 = (f32[2,8,1024]{2,1,0:T(8,128)S(1)}, f32[2,8,1024]{2,1,0:T(8,128)S(1)}, u32[]{:S(2)}, u32[]{:S(2)}) collective-permute-start(f32[2,8,1024]{2,1,0:T(8,128)S(1)} %get-tuple-element.11), channel_id=1, source_target_pairs={{24,0},{25,1},{26,2},{27,3},{28,4},{29,5},{30,6},{31,7},{0,8},{1,9... | collective-permute-start | bytes 196616 | tf_op jit(solution)/shard_map/ppermute | solution.py:64
  17.4 15.0 %collective-permute-start.10 = (f32[8,8,1024]{2,1,0:T(8,128)S(1)}, f32[8,8,1024]{2,1,0:T(8,128)S(1)}, u32[]{:S(2)}, u32[]{:S(2)}) collective-permute-start(f32[8,8,1024]{2,1,0:T(8,128)S(1)} %pad_maximum_fusion.1.refs_4_), channel_id=1, source_target_pairs={{32,0},{33,1},{34,2},{35,3},{36,4},{37,5},{38,6},{39,7},{40,8},{41... | collective-permute-start | bytes 786440 | tf_op jit(solution)/shard_map/ppermute | solution.py:64
  20.2 6.1 %collective-permute-start.1 = (f32[2,8,1024]{2,1,0:T(8,128)S(1)}, f32[2,8,1024]{2,1,0:T(8,128)S(1)}, u32[]{:S(2)}, u32[]{:S(2)}) collective-permute-start(f32[2,8,1024]{2,1,0:T(8,128)S(1)} %get-tuple-element.12), channel_id=1, source_target_pairs={{32,0},{33,1},{34,2},{35,3},{36,4},{37,5},{38,6},{39,7},{40,8},{41... | collective-permute-start | bytes 196616 | tf_op jit(solution)/shard_map/ppermute | solution.py:64
  21.0 7.3 %collective-permute-start.2 = (f32[2,8,1024]{2,1,0:T(8,128)S(1)}, f32[2,8,1024]{2,1,0:T(8,128)S(1)}, u32[]{:S(2)}, u32[]{:S(2)}) collective-permute-start(f32[2,8,1024]{2,1,0:T(8,128)S(1)} %get-tuple-element.12), channel_id=1, source_target_pairs={{64,0},{65,1},{66,2},{67,3},{68,4},{69,5},{70,6},{71,7},{72,8},{73... | collective-permute-start | bytes 196616 | tf_op jit(solution)/shard_map/ppermute | solution.py:64
  21.5 9.3 %collective-permute-start.3 = (f32[2,8,1024]{2,1,0:T(8,128)S(1)}, f32[2,8,1024]{2,1,0:T(8,128)S(1)}, u32[]{:S(2)}, u32[]{:S(2)}) collective-permute-start(f32[2,8,1024]{2,1,0:T(8,128)S(1)} %get-tuple-element.12), channel_id=1, source_target_pairs={{96,0},{97,1},{98,2},{99,3},{100,4},{101,5},{102,6},{103,7},{104,8... | collective-permute-start | bytes 196616 | tf_op jit(solution)/shard_map/ppermute | solution.py:64
  22.4 9.1 %collective-permute-start.15 = (f32[32,64]{1,0:T(8,128)}, f32[32,64]{1,0:T(8,128)S(1)}, u32[]{:S(2)}, u32[]{:S(2)}) collective-permute-start(f32[32,64]{1,0:T(8,128)} %basis_ref.1), channel_id=1, source_target_pairs={{1,0},{0,1},{3,2},{2,3},{5,4},{4,5},{7,6},{6,7},{9,8},{8,9},{11,10... | collective-permute-start | bytes 24584 | tf_op jit(solution)/shard_map/ppermute | solution.py:64
  26.3 10.6 %collective-permute-start.11 = (f32[8,8,1024]{2,1,0:T(8,128)S(1)}, f32[8,8,1024]{2,1,0:T(8,128)S(1)}, u32[]{:S(2)}, u32[]{:S(2)}) collective-permute-start(f32[8,8,1024]{2,1,0:T(8,128)S(1)} %pad_maximum_fusion.1.refs_4_), channel_id=1, source_target_pairs={{64,0},{65,1},{66,2},{67,3},{68,4},{69,5},{70,6},{71,7},{72,8},{73... | collective-permute-start | bytes 786440 | tf_op jit(solution)/shard_map/ppermute | solution.py:64
  28.3 24.8 %collective-permute-start.12 = (f32[8,8,1024]{2,1,0:T(8,128)S(1)}, f32[8,8,1024]{2,1,0:T(8,128)S(1)}, u32[]{:S(2)}, u32[]{:S(2)}) collective-permute-start(f32[8,8,1024]{2,1,0:T(8,128)S(1)} %pad_maximum_fusion.1.refs_4_), channel_id=1, source_target_pairs={{96,0},{97,1},{98,2},{99,3},{100,4},{101,5},{102,6},{103,7},{104,8... | collective-permute-start | bytes 786440 | tf_op jit(solution)/shard_map/ppermute | solution.py:64
  30.9 22.3 %collective-permute-start.4 = (f32[8,8,1024]{2,1,0:T(8,128)S(1)}, f32[8,8,1024]{2,1,0:T(8,128)S(1)}, u32[]{:S(2)}, u32[]{:S(2)}) collective-permute-start(f32[8,8,1024]{2,1,0:T(8,128)S(1)} %pad_maximum_fusion.refs_0_), channel_id=1, source_target_pairs={{8,0},{9,1},{10,2},{11,3},{12,4},{13,5},{14,6},{15,7},{16,8},{17,9... | collective-permute-start | bytes 786440 | tf_op jit(solution)/shard_map/ppermute | solution.py:64
  31.5 21.7 %collective-permute-start.5 = (f32[8,8,1024]{2,1,0:T(8,128)S(1)}, f32[8,8,1024]{2,1,0:T(8,128)S(1)}, u32[]{:S(2)}, u32[]{:S(2)}) collective-permute-start(f32[8,8,1024]{2,1,0:T(8,128)S(1)} %pad_maximum_fusion.refs_0_), channel_id=1, source_target_pairs={{16,0},{17,1},{18,2},{19,3},{20,4},{21,5},{22,6},{23,7},{24,8},{25... | collective-permute-start | bytes 786440 | tf_op jit(solution)/shard_map/ppermute | solution.py:64
  32.3 20.8 %collective-permute-start.6 = (f32[8,8,1024]{2,1,0:T(8,128)S(1)}, f32[8,8,1024]{2,1,0:T(8,128)S(1)}, u32[]{:S(2)}, u32[]{:S(2)}) collective-permute-start(f32[8,8,1024]{2,1,0:T(8,128)S(1)} %pad_maximum_fusion.refs_0_), channel_id=1, source_target_pairs={{24,0},{25,1},{26,2},{27,3},{28,4},{29,5},{30,6},{31,7},{0,8},{1,9... | collective-permute-start | bytes 786440 | tf_op jit(solution)/shard_map/ppermute | solution.py:64
  36.9 29.0 %collective-permute-start.16 = (f32[32,128]{1,0:T(8,128)S(1)}, f32[32,128]{1,0:T(8,128)S(1)}, u32[]{:S(2)}, u32[]{:S(2)}) collective-permute-start(f32[32,128]{1,0:T(8,128)S(1)} %pad_maximum_fusion.4), channel_id=1, source_target_pairs={{2,0},{3,1},{0,2},{1,3},{6,4},{7,5},{4,6},{5,7},{10,8},{11,9},{8,1... | collective-permute-start | bytes 49160 | tf_op jit(solution)/shard_map/ppermute | solution.py:64
  38.4 5.8 %copy-start = (f32[8,256,2048]{2,1,0:T(8,128)S(1)}, f32[8,256,2048]{2,1,0:T(8,128)}, u32[]{:S(2)}) copy-start(f32[8,256,2048]{2,1,0:T(8,128)} %block_ref.1) | copy-start | bytes 50331652
  59.9 33.7 %copy-start.5 = (f32[32,64]{1,0:T(8,128)S(1)}, f32[32,64]{1,0:T(8,128)}, u32[]{:S(2)}) copy-start(f32[32,64]{1,0:T(8,128)} %basis_ref.1) | copy-start | bytes 24580
  65.7 1.3 %collective-permute-start.13 = (f32[32,256]{1,0:T(8,128)S(1)}, f32[32,256]{1,0:T(8,128)S(1)}, u32[]{:S(2)}, u32[]{:S(2)}) collective-permute-start(f32[32,256]{1,0:T(8,128)S(1)} %image.1), channel_id=1, source_target_pairs={{1,0},{0,1},{3,2},{2,3},{5,4},{4,5},{7,6},{6,7},{9,8},{8,9},{11,10... | collective-permute-start | bytes 98312 | tf_op jit(solution)/shard_map/ppermute | solution.py:64
  67.0 3.9 %collective-permute-start.14 = (f32[32,256]{1,0:T(8,128)S(1)}, f32[32,256]{1,0:T(8,128)S(1)}, u32[]{:S(2)}, u32[]{:S(2)}) collective-permute-start(f32[32,256]{1,0:T(8,128)S(1)} %add.33.mine_ref), channel_id=1, source_target_pairs={{2,0},{3,1},{0,2},{1,3},{6,4},{7,5},{4,6},{5,7},{10,8},{11,9},{8,1... | collective-permute-start | bytes 98312 | tf_op jit(solution)/shard_map/ppermute | solution.py:64
  71.2 5.0 %collective-permute-start.17 = (f32[32,128]{1,0:T(8,128)S(1)}, f32[32,128]{1,0:T(8,128)S(1)}, u32[]{:S(2)}, u32[]{:S(2)}) collective-permute-start(f32[32,128]{1,0:T(8,128)S(1)} %get-tuple-element.9), channel_id=1, source_target_pairs={{6,0},{7,1},{4,2},{5,3},{2,4},{3,5},{0,6},{1,7},{14,8},{15,9},{12,... | collective-permute-start | bytes 49160 | tf_op jit(solution)/shard_map/ppermute | solution.py:64
  76.2 3.7 %collective-permute-start.18 = (f32[32,128]{1,0:T(8,128)S(1)}, f32[32,128]{1,0:T(8,128)S(1)}, u32[]{:S(2)}, u32[]{:S(2)}) collective-permute-start(f32[32,128]{1,0:T(8,128)S(1)} %add.35), channel_id=1, source_target_pairs={{32,0},{33,1},{34,2},{35,3},{36,4},{37,5},{38,6},{39,7},{40,8},{41... | collective-permute-start | bytes 49160 | tf_op jit(solution)/shard_map/ppermute | solution.py:64
  80.0 4.9 %collective-permute-start.19 = (f32[32,128]{1,0:T(8,128)S(1)}, f32[32,128]{1,0:T(8,128)S(1)}, u32[]{:S(2)}, u32[]{:S(2)}) collective-permute-start(f32[32,128]{1,0:T(8,128)S(1)} %add.36), channel_id=1, source_target_pairs={{96,0},{97,1},{98,2},{99,3},{100,4},{101,5},{102,6},{103,7},{104,8... | collective-permute-start | bytes 49160 | tf_op jit(solution)/shard_map/ppermute | solution.py:64
  84.9 3.7 %collective-permute-start.20 = (f32[32,128]{1,0:T(8,128)S(1)}, f32[32,128]{1,0:T(8,128)S(1)}, u32[]{:S(2)}, u32[]{:S(2)}) collective-permute-start(f32[32,128]{1,0:T(8,128)S(1)} %add.37), channel_id=1, source_target_pairs={{8,0},{9,1},{10,2},{11,3},{12,4},{13,5},{14,6},{15,7},{0,8},{1,9},... | collective-permute-start | bytes 49160 | tf_op jit(solution)/shard_map/ppermute | solution.py:64
  88.7 4.9 %collective-permute-start.21 = (f32[32,128]{1,0:T(8,128)S(1)}, f32[32,128]{1,0:T(8,128)S(1)}, u32[]{:S(2)}, u32[]{:S(2)}) collective-permute-start(f32[32,128]{1,0:T(8,128)S(1)} %add.38), channel_id=1, source_target_pairs={{24,0},{25,1},{26,2},{27,3},{28,4},{29,5},{30,6},{31,7},{16,8},{17... | collective-permute-start | bytes 49160 | tf_op jit(solution)/shard_map/ppermute | solution.py:64
  (4 other events, 13.3 us)

commit v2 on v1

v2 whole, which is shorter than its diff:
```python
import functools

import jax
import jax.numpy as jnp
from jax import lax
from jax.experimental import pallas as pl
from jax.experimental.pallas import tpu as pltpu
from jax.sharding import Mesh, PartitionSpec as P

N = 8192
K = 8
R = 32
XS = 4
YS = 4
HALF = 1024
ROWS = 256
OWN = 64
AXES = ("x", "y", "zh", "zl", "core")
HI = lax.Precision.HIGHEST
NT = (((1,), (1,)), ((), ()))
NN = (((1,), (0,)), ((), ()))
VM = pl.BlockSpec(memory_space=pltpu.VMEM)
SM = pl.BlockSpec(memory_space=pltpu.SMEM)


def flat(x, y, zh, zl, core):
    return ((x * YS + y) * 2 + zh) * 4 + zl * 2 + core


def sources(source_of):
    pairs = []
    for x in range(XS):
        for y in range(YS):
            for zh in range(2):
                for zl in range(2):
                    for core in range(2):
                        here = (x, y, zh, zl, core)
                        pairs.append((flat(*source_of(*here)), flat(*here)))
    return pairs


def from_x(step):
    return sources(lambda x, y, zh, zl, core: ((x + step) % XS, y, zh, zl, core))


def from_y(step):
    return sources(lambda x, y, zh, zl, core: (x, (y + step) % YS, zh, zl, core))


FROM_ZH = sources(lambda x, y, zh, zl, core: (x, y, 1 - zh, zl, core))
FROM_CORE = sources(lambda x, y, zh, zl, core: (x, y, zh, zl, 1 - core))
FROM_ZL = sources(lambda x, y, zh, zl, core: (x, y, zh, 1 - zl, 1 - core))
FROM_Z = sources(lambda x, y, zh, zl, core: (x, y, 1 - zh, 1 - zl, 1 - core))


def move(value, pairs):
    return lax.ppermute(value, AXES, pairs)


def split(value):
    high = value.astype(jnp.bfloat16)
    low = (value - high.astype(jnp.float32)).astype(jnp.bfloat16)
    return high, low


def load_kernel(source_ref, out_ref, sem):
    copy = pltpu.make_async_copy(source_ref, out_ref, sem)
    copy.start()
    copy.wait()


def load(coefficients):
    return pl.pallas_call(
        load_kernel,
        in_specs=[pl.BlockSpec(memory_space=pltpu.HBM)],
        out_specs=VM,
        out_shape=pltpu.VMEM(coefficients.shape, jnp.float32),
        scratch_shapes=[pltpu.SemaphoreType.DMA],
        compiler_params=pltpu.CompilerParams(vmem_limit_bytes=1 << 20),
        name="load",
    )(coefficients)


def half_image(half, place_ref, pieces, block, held):
    total = None
    for k in range(K):
        rows = jnp.concatenate([piece[:, k, :] for piece in pieces], axis=0)
        rows_high, rows_low = split(rows)
        both = jnp.concatenate([rows_high, rows_low], axis=0)
        high, low = split(block[k, :, half * HALF : (half + 1) * HALF])
        main = lax.dot_general(both, high, NT, preferred_element_type=jnp.float32)
        rest = lax.dot_general(rows_high, low, NT, preferred_element_type=jnp.float32)
        part = main[:R] + main[R:] + rest
        total = part if total is None else total + part
    held[...] = total
    x0, y0, zh0 = place_ref[0], place_ref[1], place_ref[2]
    ordered = []
    for x in range(XS):
        for y in range(YS):
            for zh in range(2):
                dx = (x - x0 + XS) % XS
                dy = (y - y0 + YS) % YS
                dz = (zh + zh0) % 2
                outer, inner = (dy, dx) if half == 0 else (dx, dy)
                ordered.append(held[pl.ds(outer * 8 + inner * 2 + dz, 1), :])
    return ordered


def first_half_kernel(place_ref, *refs):
    pieces, (block, out_ref, held) = refs[:4], refs[4:]
    for i, row in enumerate(half_image(0, place_ref, pieces, block, held)):
        out_ref[i : i + 1, :] = row


def second_half_kernel(place_ref, *refs):
    pieces, (block, first_ref, basis_ref, out_ref, held) = refs[:4], refs[4:]
    for i, row in enumerate(half_image(1, place_ref, pieces, block, held)):
        out_ref[i : i + 1, 0:ROWS] = first_ref[i : i + 1, :] + row
    out_ref[:, ROWS : ROWS + OWN] = basis_ref[...]
    out_ref[:, ROWS + OWN :] = jnp.zeros_like(basis_ref)


def image_call(kernel, name, width, *args):
    return pl.pallas_call(
        kernel,
        in_specs=[SM] + [VM] * (len(args) - 1),
        out_specs=VM,
        out_shape=jax.ShapeDtypeStruct((R, width), jnp.float32),
        scratch_shapes=[pltpu.VMEM((R, ROWS), jnp.float32)],
        compiler_params=pltpu.CompilerParams(vmem_limit_bytes=6 << 20),
        name=name,
    )(*args)


def in_order(second, mine, other):
    return jnp.concatenate([jnp.where(second, other, mine), jnp.where(second, mine, other)], axis=1)


def pair_kernel(place_ref, mine_ref, other_ref, out_ref):
    out_ref[:, 0:ROWS] = mine_ref[:, 0:ROWS] + other_ref[:, 0:ROWS]
    own = slice(ROWS, ROWS + OWN)
    out_ref[:, ROWS:] = in_order(place_ref[4] == 1, mine_ref[:, own], other_ref[:, own])


def pair(place, mine, other):
    return pl.pallas_call(
        pair_kernel,
        in_specs=[SM, VM, VM],
        out_specs=VM,
        out_shape=jax.ShapeDtypeStruct(mine.shape, jnp.float32),
        compiler_params=pltpu.CompilerParams(vmem_limit_bytes=2 << 20),
        name="pair",
    )(place, mine, other)


def products_kernel(place_ref, mine_ref, other_ref, image_ref, products_ref):
    image = mine_ref[:, 0:ROWS] + other_ref[:, 0:ROWS]
    image_ref[...] = image
    basis = in_order(place_ref[3] == 1, mine_ref[:, ROWS:], other_ref[:, ROWS:])
    both = jnp.concatenate([image, basis], axis=0)
    of_image = lax.dot_general(image, both, NT, precision=HI, preferred_element_type=jnp.float32)
    of_basis = lax.dot_general(basis, both, NT, precision=HI, preferred_element_type=jnp.float32)
    products_ref[...] = jnp.concatenate([of_image, of_basis], axis=1)


def products(place, mine, other):
    return pl.pallas_call(
        products_kernel,
        in_specs=[SM, VM, VM],
        out_specs=[VM] * 2,
        out_shape=[
            jax.ShapeDtypeStruct((R, ROWS), jnp.float32),
            jax.ShapeDtypeStruct((R, 4 * R), jnp.float32),
        ],
        compiler_params=pltpu.CompilerParams(vmem_limit_bytes=2 << 20),
        name="products",
    )(place, mine, other)


def final_kernel(place_ref, products_ref, image_ref, basis_ref, new_ref, projection_ref, factor_ref):
    dot = functools.partial(lax.dot_general, precision=HI, preferred_element_type=jnp.float32)
    total = products_ref[0]
    for chip in range(1, XS * YS):
        total = total + products_ref[chip]
    squares = total[:, 0:R]
    first_t = total[:, R : 2 * R]
    first = total[:, 2 * R : 3 * R]
    basis_gram = total[:, 3 * R : 4 * R]
    projection = 2.0 * first - dot(basis_gram, first, NN)
    projection_t = 2.0 * first_t - dot(first_t, basis_gram, NN)
    projection_ref[...] = projection
    left = first - dot(basis_gram, projection, NN)
    gram = (squares - dot(first_t, projection, NN) - dot(projection_t, left, NN)) / N
    narrow = place_ref[3] * 2 + place_ref[4]
    own = image_ref[:, 0:64]
    for n in range(1, 4):
        own = jnp.where(narrow == n, image_ref[:, n * 64 : (n + 1) * 64], own)
    twice = own - dot(projection_t, basis_ref[...], NN)
    work = jnp.concatenate([gram, jnp.zeros((R, R), jnp.float32), twice], axis=1)
    lane = lax.broadcasted_iota(jnp.int32, (1, 4 * R), 1)
    done = []
    for k in range(R):
        row = work[k : k + 1, :]
        column = work[:, k : k + 1]
        scale = 1.0 / jnp.sqrt(work[k : k + 1, k : k + 1])
        unit = row * scale
        done.append(jnp.where(lane >= k, unit, 0.0))
        work = work - (column * scale) * unit
    rows = jnp.concatenate(done, axis=0)
    factor_ref[...] = rows[:, 0:R].T
    new_ref[...] = rows[:, 2 * R : 4 * R]


def final(place, total, image, basis):
    return pl.pallas_call(
        final_kernel,
        in_specs=[SM] + [VM] * 3,
        out_specs=[VM] * 3,
        out_shape=[
            jax.ShapeDtypeStruct(basis.shape, jnp.float32),
            jax.ShapeDtypeStruct((R, R), jnp.float32),
            jax.ShapeDtypeStruct((R, R), jnp.float32),
        ],
        compiler_params=pltpu.CompilerParams(vmem_limit_bytes=2 << 20),
        name="final",
    )(place, total, image, basis)


def body(coefficients, tensor_blocks, basis_rows):
    coefficients = pltpu.with_memory_space_constraint(coefficients, pltpu.HBM)
    place = jnp.stack([lax.axis_index(axis) for axis in AXES]).astype(jnp.int32)

    own = tensor_blocks.reshape(K, 2 * HALF)
    across = move(own, FROM_ZH)
    both = jnp.stack([own, across])
    a, b = both[:, :, :HALF], both[:, :, HALF:]
    moved = [move(a, from_x(s)) for s in (1, 2, 3)] + [move(b, from_y(s)) for s in (1, 2, 3)]
    *moved, coefficients = lax.optimization_barrier((*moved, coefficients))
    loaded = load(coefficients)
    a = jnp.concatenate([a] + moved[:3])
    b = jnp.concatenate([b] + moved[3:])
    pieces_b = {0: b}
    for s in (2, 3, 1):
        pieces_b[s] = move(b, from_x(s))
    pieces_a = {0: a}
    for s in (2, 3, 1):
        pieces_a[s] = move(a, from_y(s))

    part = image_call(first_half_kernel, "image_a", ROWS, place, *[pieces_a[s] for s in range(4)], loaded)
    pieces = [pieces_b[s] for s in range(4)]
    part = image_call(
        second_half_kernel, "image_b", ROWS + 2 * OWN, place, *pieces, loaded, part, basis_rows
    )
    part = pair(place, part, move(part, FROM_CORE))
    image, total = products(place, part, move(part, FROM_ZL))
    total = total + move(total, FROM_Z)
    total = jnp.broadcast_to(total, (XS * YS, *total.shape))
    total = lax.all_to_all(total, ("x", "y"), 0, 0, tiled=True)
    return tuple(final(place, total, image, basis_rows))


def solution(mesh):
    mesh = Mesh(mesh.devices.reshape(XS, YS, 2, 2, 2), AXES)
    wide, narrow = AXES[:3], AXES[3:]
    in_specs = (P(None, wide, narrow), P(None, wide, narrow), P(None, AXES))
    out_specs = (P(None, AXES), P(), P())
    return jax.shard_map(body, mesh=mesh, in_specs=in_specs, out_specs=out_specs, check_vma=False)
```

time: 99 us -> 74.9 us (0.76)
  waiting for transfers between devices: 36.5 us -> 13.4 us
  local copies, waits for them, and re-layouts: 19.9 us -> 0.97 us
  blocking collectives: 0 us -> 14.3 us
  Pallas kernels: 13.5 us -> 19 us
    ppermute x22 -> x16, waiting for transfers between devices: 36.5 us -> 13.4 us  [move(): return lax.ppermute(value, AXES, pairs)]
    unnamed x13 -> x3, local copies, waits for them, and re-layouts: 19.9 us -> 0.87 us
    all_to_all x0 -> x1, blocking collectives: none -> 14.3 us  [body(): total = lax.all_to_all(total, ('x', 'y'), 0, 0, tiled=True)]
    pallas_call x4 -> x6, Pallas kernels: 13.5 us -> 19 us  [the longest x2 6.76 us: image_call(): pl.pallas_call(kernel, in_specs=[SM] + [VM] * (len(args) - 1), out_specs=...]
    ppermute x22 -> x16, starting transfers between devices: 26.9 us -> 26.1 us  [move(): return lax.ppermute(value, AXES, pairs)]
  transfers between devices with their start and end apart: 22 -> 16, of which waited for: 13 -> 9; matrix products, arithmetic and copies ran while one was open for 1% -> 0% of each run, Pallas kernels for 8% -> 12%
where the time goes in v2:
time: 74.9 us; the launch traced here: 74.6 us
  starting transfers between devices  26.1 us (35%)
  Pallas kernels  19 us (25%)
  blocking collectives  14.3 us (19%)
  waiting for transfers between devices  13.4 us (18%)
  local copies, waits for them, and re-layouts  0.97 us (1%)
  between operations  0.75 us (1%)
    ppermute x16, starting transfers between devices, move(): return lax.ppermute(value, AXES, pairs)  26.1 us
    all_to_all x1, blocking collectives, body(): total = lax.all_to_all(total, ('x', 'y'), 0, 0, tiled=True)  14.3 us
    ppermute x16, waiting for transfers between devices, move(): return lax.ppermute(value, AXES, pairs)  13.4 us
    pallas_call x2, Pallas kernels, image_call(): pl.pallas_call(kernel, in_specs=[SM] + [VM] * (len(args) - 1), out_specs=...  6.76 us
    pallas_call x1, Pallas kernels, load(): pl.pallas_call(load_kernel, in_specs=[pl.BlockSpec(memory_space=pltpu.HBM...  5.78 us
    pallas_call x1, Pallas kernels, final(): pl.pallas_call(final_kernel, in_specs=[SM] + [VM] * 3, out_specs=[VM] * 3...  5.04 us
  transfers between devices with their start and end apart: 16, of which 9 were waited for; matrix products, arithmetic and copies ran while one was open for 0% of the time, Pallas kernels for 12%

profile of v2, /device:TPU:0, one launch (start us, length us, event | category | flops | bytes accessed | tf_op | source)
XLA Modules:
  0.0 74.6 jit_solution(12643735900280448982)
XLA Ops:
  0.6 0.9 %copy.10 = f32[8,1,2048]{2,0,1:T(8,128)S(1)} copy(f32[8,1,2048]{2,1,0:T(1,128)} %param.4) | data formatting | bytes 131072
  1.5 4.0 %collective-permute-start = (f32[8,2048]{1,0:T(8,128)S(1)}, f32[8,2048]{1,0:T(8,128)S(1)}, u32[]{:S(2)}, u32[]{:S(2)}) collective-permute-start(f32[8,2048]{1,0:T(8,128)S(1)} %bitcast.11), channel_id=1, source_target_pairs={{4,0},{5,1},{6,2},{7,3},{0,4},{1,5},{2,6},{3,7},{12,8},{13,9},{14,... | collective-permute-start | bytes 196616 | tf_op jit(solution)/shard_map/ppermute | solution.py:57
  5.5 2.2 %collective-permute-done = f32[8,2048]{1,0:T(8,128)S(1)} collective-permute-done((f32[8,2048]{1,0:T(8,128)S(1)}, f32[8,2048]{1,0:T(8,128)S(1)}, u32[]{:S(2)}, u32[]{:S(2)}) %collective-permute-start) | collective-permute-done | bytes 65568 | tf_op jit(solution)/shard_map/ppermute | solution.py:57
  7.8 2.8 %collective-permute-start.1 = (f32[2,8,1024]{2,1,0:T(8,128)S(1)}, f32[2,8,1024]{2,1,0:T(8,128)S(1)}, u32[]{:S(2)}, u32[]{:S(2)}) collective-permute-start(f32[2,8,1024]{2,1,0:T(8,128)S(1)} %get-tuple-element.22), channel_id=1, source_target_pairs={{32,0},{33,1},{34,2},{35,3},{36,4},{37,5},{38,6},{39,7},{40,8},{41... | collective-permute-start | bytes 196616 | tf_op jit(solution)/shard_map/ppermute | solution.py:57
  11.4 0.9 %collective-permute-start.3 = (f32[2,8,1024]{2,1,0:T(8,128)S(1)}, f32[2,8,1024]{2,1,0:T(8,128)S(1)}, u32[]{:S(2)}, u32[]{:S(2)}) collective-permute-start(f32[2,8,1024]{2,1,0:T(8,128)S(1)} %get-tuple-element.22), channel_id=1, source_target_pairs={{96,0},{97,1},{98,2},{99,3},{100,4},{101,5},{102,6},{103,7},{104,8... | collective-permute-start | bytes 196616 | tf_op jit(solution)/shard_map/ppermute | solution.py:57
  12.3 3.0 %collective-permute-start.4 = (f32[2,8,1024]{2,1,0:T(8,128)S(1)}, f32[2,8,1024]{2,1,0:T(8,128)S(1)}, u32[]{:S(2)}, u32[]{:S(2)}) collective-permute-start(f32[2,8,1024]{2,1,0:T(8,128)S(1)} %get-tuple-element.21), channel_id=1, source_target_pairs={{8,0},{9,1},{10,2},{11,3},{12,4},{13,5},{14,6},{15,7},{16,8},{17,9... | collective-permute-start | bytes 196616 | tf_op jit(solution)/shard_map/ppermute | solution.py:57
  16.0 1.0 %collective-permute-start.6 = (f32[2,8,1024]{2,1,0:T(8,128)S(1)}, f32[2,8,1024]{2,1,0:T(8,128)S(1)}, u32[]{:S(2)}, u32[]{:S(2)}) collective-permute-start(f32[2,8,1024]{2,1,0:T(8,128)S(1)} %get-tuple-element.21), channel_id=1, source_target_pairs={{24,0},{25,1},{26,2},{27,3},{28,4},{29,5},{30,6},{31,7},{0,8},{1,9... | collective-permute-start | bytes 196616 | tf_op jit(solution)/shard_map/ppermute | solution.py:57
  17.2 3.9 %collective-permute-done.5 = f32[2,8,1024]{2,1,0:T(8,128)S(1)} collective-permute-done((f32[2,8,1024]{2,1,0:T(8,128)S(1)}, f32[2,8,1024]{2,1,0:T(8,128)S(1)}, u32[]{:S(2)}, u32[]{:S(2)}) %collective-permute-start.5) | collective-permute-done | bytes 65568 | tf_op jit(solution)/shard_map/ppermute | solution.py:57
  22.4 0.9 %collective-permute-start.11 = (f32[8,8,1024]{2,1,0:T(8,128)S(1)}, f32[8,8,1024]{2,1,0:T(8,128)S(1)}, u32[]{:S(2)}, u32[]{:S(2)}) collective-permute-start(f32[8,8,1024]{2,1,0:T(8,128)S(1)} %pad_maximum_fusion.1.refs_0_), channel_id=1, source_target_pairs={{16,0},{17,1},{18,2},{19,3},{20,4},{21,5},{22,6},{23,7},{24,8},{25... | collective-permute-start | bytes 786440 | tf_op jit(solution)/shard_map/ppermute | solution.py:57
  23.4 1.3 %collective-permute-start.12 = (f32[8,8,1024]{2,1,0:T(8,128)S(1)}, f32[8,8,1024]{2,1,0:T(8,128)S(1)}, u32[]{:S(2)}, u32[]{:S(2)}) collective-permute-start(f32[8,8,1024]{2,1,0:T(8,128)S(1)} %pad_maximum_fusion.1.refs_0_), channel_id=1, source_target_pairs={{24,0},{25,1},{26,2},{27,3},{28,4},{29,5},{30,6},{31,7},{0,8},{1,9... | collective-permute-start | bytes 786440 | tf_op jit(solution)/shard_map/ppermute | solution.py:57
  24.7 2.4 %collective-permute-start.7 = (f32[8,8,1024]{2,1,0:T(8,128)S(1)}, f32[8,8,1024]{2,1,0:T(8,128)S(1)}, u32[]{:S(2)}, u32[]{:S(2)}) collective-permute-start(f32[8,8,1024]{2,1,0:T(8,128)S(1)} %pad_maximum_fusion.refs_0_), channel_id=1, source_target_pairs={{32,0},{33,1},{34,2},{35,3},{36,4},{37,5},{38,6},{39,7},{40,8},{41... | collective-permute-start | bytes 786440 | tf_op jit(solution)/shard_map/ppermute | solution.py:57
  27.1 1.5 %collective-permute-start.8 = (f32[8,8,1024]{2,1,0:T(8,128)S(1)}, f32[8,8,1024]{2,1,0:T(8,128)S(1)}, u32[]{:S(2)}, u32[]{:S(2)}) collective-permute-start(f32[8,8,1024]{2,1,0:T(8,128)S(1)} %pad_maximum_fusion.refs_0_), channel_id=1, source_target_pairs={{64,0},{65,1},{66,2},{67,3},{68,4},{69,5},{70,6},{71,7},{72,8},{73... | collective-permute-start | bytes 786440 | tf_op jit(solution)/shard_map/ppermute | solution.py:57
  28.6 1.0 %collective-permute-done.10.refs_1_ = f32[8,8,1024]{2,1,0:T(8,128)S(1)} collective-permute-done((f32[8,8,1024]{2,1,0:T(8,128)S(1)}, f32[8,8,1024]{2,1,0:T(8,128)S(1)}, u32[]{:S(2)}, u32[]{:S(2)}) %collective-permute-start.10) | collective-permute-done | bytes 262176 | tf_op jit(solution)/shard_map/ppermute | solution.py:57
  29.6 1.8 %collective-permute-start.9 = (f32[8,8,1024]{2,1,0:T(8,128)S(1)}, f32[8,8,1024]{2,1,0:T(8,128)S(1)}, u32[]{:S(2)}, u32[]{:S(2)}) collective-permute-start(f32[8,8,1024]{2,1,0:T(8,128)S(1)} %pad_maximum_fusion.refs_0_), channel_id=1, source_target_pairs={{96,0},{97,1},{98,2},{99,3},{100,4},{101,5},{102,6},{103,7},{104,8... | collective-permute-start | bytes 786440 | tf_op jit(solution)/shard_map/ppermute | solution.py:57
  31.5 5.8 %load.1.refs_4_ = f32[8,256,2048]{2,1,0:T(8,128)S(1)} custom-call(f32[8,256,2048]{2,1,0:T(8,128)} %source_ref), custom_call_target="tpu_custom_call" | custom-call | tf_op jit(solution)/shard_map/load/pallas_call | solution.py:73
  37.3 3.4 %image_a.1.refs_5_ = f32[32,256]{1,0:T(8,128)S(1)} custom-call(s32[5]{0:T(128)S(1)} %stack.29.place_ref, f32[8,8,1024]{2,1,0:T(8,128)S(1)} %pad_maximum_fusion.1.refs_0_, f32[8,8,1024]{2,1,0:T(8,128)S(1)} %collective-permute-done.10.refs_1_, f32[8,8,1024]{2,1,0:T(8,128)S(1)} %collective-permute-done.11.refs_2_, ...), custom_call_target="tpu_custom_call" | custom-call | tf_op jit(solution)/shard_map/image_a/pallas_call | solution.py:124
  40.7 3.4 %image_b.1.mine_ref = f32[32,384]{1,0:T(8,128)S(1)} custom-call(s32[5]{0:T(128)S(1)} %stack.29.place_ref, f32[8,8,1024]{2,1,0:T(8,128)S(1)} %pad_maximum_fusion.refs_0_, f32[8,8,1024]{2,1,0:T(8,128)S(1)} %collective-permute-done.7.refs_1_, f32[8,8,1024]{2,1,0:T(8,128)S(1)} %collective-permute-done.8.refs_2_, ...), custom_call_target="tpu_custom_call" | custom-call | tf_op jit(solution)/shard_map/image_b/pallas_call | solution.py:124
  44.2 1.2 %collective-permute-done.13.other_ref = f32[32,384]{1,0:T(8,128)S(1)} collective-permute-done((f32[32,384]{1,0:T(8,128)S(1)}, f32[32,384]{1,0:T(8,128)S(1)}, u32[]{:S(2)}, u32[]{:S(2)}) %collective-permute-start.13) | collective-permute-done | bytes 49184 | tf_op jit(solution)/shard_map/ppermute | solution.py:57
  46.1 1.1 %collective-permute-start.14 = (f32[32,384]{1,0:T(8,128)S(1)}, f32[32,384]{1,0:T(8,128)S(1)}, u32[]{:S(2)}, u32[]{:S(2)}) collective-permute-start(f32[32,384]{1,0:T(8,128)S(1)} %pair.1.mine_ref), channel_id=1, source_target_pairs={{3,0},{2,1},{1,2},{0,3},{7,4},{6,5},{5,6},{4,7},{11,8},{10,9},{9,1... | collective-permute-start | bytes 147464 | tf_op jit(solution)/shard_map/ppermute | solution.py:57
  47.1 2.7 %collective-permute-done.14.other_ref = f32[32,384]{1,0:T(8,128)S(1)} collective-permute-done((f32[32,384]{1,0:T(8,128)S(1)}, f32[32,384]{1,0:T(8,128)S(1)}, u32[]{:S(2)}, u32[]{:S(2)}) %collective-permute-start.14) | collective-permute-done | bytes 49184 | tf_op jit(solution)/shard_map/ppermute | solution.py:57
  50.6 3.2 %collective-permute-start.15 = (f32[32,128]{1,0:T(8,128)S(1)}, f32[32,128]{1,0:T(8,128)S(1)}, u32[]{:S(2)}, u32[]{:S(2)}) collective-permute-start(f32[32,128]{1,0:T(8,128)S(1)} %get-tuple-element.19), channel_id=1, source_target_pairs={{7,0},{6,1},{5,2},{4,3},{3,4},{2,5},{1,6},{0,7},{15,8},{14,9},{13,... | collective-permute-start | bytes 49160 | tf_op jit(solution)/shard_map/ppermute | solution.py:57
  53.8 1.4 %collective-permute-done.15 = f32[32,128]{1,0:T(8,128)S(1)} collective-permute-done((f32[32,128]{1,0:T(8,128)S(1)}, f32[32,128]{1,0:T(8,128)S(1)}, u32[]{:S(2)}, u32[]{:S(2)}) %collective-permute-start.15) | collective-permute-done | bytes 16416 | tf_op jit(solution)/shard_map/ppermute | solution.py:57
  55.3 14.3 %all_to_all.5.products_ref = f32[16,32,128]{2,1,0:T(8,128)S(1)} all-to-all(f32[16,32,128]{2,1,0:T(8,128)S(1)} %broadcast_in_dim.3), channel_id=1, replica_groups=mesh['x'=4,'y'=4,'zh'=2,'zl'=2,'core'=2] {'x','y'}, dimensions={0} | all-to-all | bytes 524288 | tf_op jit(solution)/shard_map/all_to_all | solution.py:258
  69.6 5.0 %final.1 = (f32[32,64]{1,0:T(8,128)}, f32[32,32]{1,0:T(8,128)}, f32[32,32]{1,0:T(8,128)}) custom-call(s32[5]{0:T(128)S(1)} %stack.29.place_ref, f32[16,32,128]{2,1,0:T(8,128)S(1)} %all_to_all.5.products_ref, f32[32,256]{1,0:T(8,128)S(1)} %get-tuple-element.20.image_ref, f32[32,64]{1,0:T(8,128)S(1)} %copy-done), custom_call_target="tpu_custom_call" | custom-call | tf_op jit(solution)/shard_map/final/pallas_call | solution.py:215
  (24 shorter events, 4.7 us)
Async XLA Ops:
  1.5 6.3 %collective-permute-start = (f32[8,2048]{1,0:T(8,128)S(1)}, f32[8,2048]{1,0:T(8,128)S(1)}, u32[]{:S(2)}, u32[]{:S(2)}) collective-permute-start(f32[8,2048]{1,0:T(8,128)S(1)} %bitcast.11), channel_id=1, source_target_pairs={{4,0},{5,1},{6,2},{7,3},{0,4},{1,5},{2,6},{3,7},{12,8},{13,9},{14,... | collective-permute-start | bytes 196616 | tf_op jit(solution)/shard_map/ppermute | solution.py:57
  7.8 8.2 %collective-permute-start.1 = (f32[2,8,1024]{2,1,0:T(8,128)S(1)}, f32[2,8,1024]{2,1,0:T(8,128)S(1)}, u32[]{:S(2)}, u32[]{:S(2)}) collective-permute-start(f32[2,8,1024]{2,1,0:T(8,128)S(1)} %get-tuple-element.22), channel_id=1, source_target_pairs={{32,0},{33,1},{34,2},{35,3},{36,4},{37,5},{38,6},{39,7},{40,8},{41... | collective-permute-start | bytes 196616 | tf_op jit(solution)/shard_map/ppermute | solution.py:57
  10.6 6.3 %collective-permute-start.2 = (f32[2,8,1024]{2,1,0:T(8,128)S(1)}, f32[2,8,1024]{2,1,0:T(8,128)S(1)}, u32[]{:S(2)}, u32[]{:S(2)}) collective-permute-start(f32[2,8,1024]{2,1,0:T(8,128)S(1)} %get-tuple-element.22), channel_id=1, source_target_pairs={{64,0},{65,1},{66,2},{67,3},{68,4},{69,5},{70,6},{71,7},{72,8},{73... | collective-permute-start | bytes 196616 | tf_op jit(solution)/shard_map/ppermute | solution.py:57
  11.4 5.7 %collective-permute-start.3 = (f32[2,8,1024]{2,1,0:T(8,128)S(1)}, f32[2,8,1024]{2,1,0:T(8,128)S(1)}, u32[]{:S(2)}, u32[]{:S(2)}) collective-permute-start(f32[2,8,1024]{2,1,0:T(8,128)S(1)} %get-tuple-element.22), channel_id=1, source_target_pairs={{96,0},{97,1},{98,2},{99,3},{100,4},{101,5},{102,6},{103,7},{104,8... | collective-permute-start | bytes 196616 | tf_op jit(solution)/shard_map/ppermute | solution.py:57
  12.3 4.9 %collective-permute-start.4 = (f32[2,8,1024]{2,1,0:T(8,128)S(1)}, f32[2,8,1024]{2,1,0:T(8,128)S(1)}, u32[]{:S(2)}, u32[]{:S(2)}) collective-permute-start(f32[2,8,1024]{2,1,0:T(8,128)S(1)} %get-tuple-element.21), channel_id=1, source_target_pairs={{8,0},{9,1},{10,2},{11,3},{12,4},{13,5},{14,6},{15,7},{16,8},{17,9... | collective-permute-start | bytes 196616 | tf_op jit(solution)/shard_map/ppermute | solution.py:57
  15.3 5.8 %collective-permute-start.5 = (f32[2,8,1024]{2,1,0:T(8,128)S(1)}, f32[2,8,1024]{2,1,0:T(8,128)S(1)}, u32[]{:S(2)}, u32[]{:S(2)}) collective-permute-start(f32[2,8,1024]{2,1,0:T(8,128)S(1)} %get-tuple-element.21), channel_id=1, source_target_pairs={{16,0},{17,1},{18,2},{19,3},{20,4},{21,5},{22,6},{23,7},{24,8},{25... | collective-permute-start | bytes 196616 | tf_op jit(solution)/shard_map/ppermute | solution.py:57
  16.0 5.8 %collective-permute-start.6 = (f32[2,8,1024]{2,1,0:T(8,128)S(1)}, f32[2,8,1024]{2,1,0:T(8,128)S(1)}, u32[]{:S(2)}, u32[]{:S(2)}) collective-permute-start(f32[2,8,1024]{2,1,0:T(8,128)S(1)} %get-tuple-element.21), channel_id=1, source_target_pairs={{24,0},{25,1},{26,2},{27,3},{28,4},{29,5},{30,6},{31,7},{0,8},{1,9... | collective-permute-start | bytes 196616 | tf_op jit(solution)/shard_map/ppermute | solution.py:57
  21.8 7.8 %collective-permute-start.10 = (f32[8,8,1024]{2,1,0:T(8,128)S(1)}, f32[8,8,1024]{2,1,0:T(8,128)S(1)}, u32[]{:S(2)}, u32[]{:S(2)}) collective-permute-start(f32[8,8,1024]{2,1,0:T(8,128)S(1)} %pad_maximum_fusion.1.refs_0_), channel_id=1, source_target_pairs={{8,0},{9,1},{10,2},{11,3},{12,4},{13,5},{14,6},{15,7},{16,8},{17,9... | collective-permute-start | bytes 786440 | tf_op jit(solution)/shard_map/ppermute | solution.py:57
  22.4 14.8 %collective-permute-start.11 = (f32[8,8,1024]{2,1,0:T(8,128)S(1)}, f32[8,8,1024]{2,1,0:T(8,128)S(1)}, u32[]{:S(2)}, u32[]{:S(2)}) collective-permute-start(f32[8,8,1024]{2,1,0:T(8,128)S(1)} %pad_maximum_fusion.1.refs_0_), channel_id=1, source_target_pairs={{16,0},{17,1},{18,2},{19,3},{20,4},{21,5},{22,6},{23,7},{24,8},{25... | collective-permute-start | bytes 786440 | tf_op jit(solution)/shard_map/ppermute | solution.py:57
  23.4 13.9 %collective-permute-start.12 = (f32[8,8,1024]{2,1,0:T(8,128)S(1)}, f32[8,8,1024]{2,1,0:T(8,128)S(1)}, u32[]{:S(2)}, u32[]{:S(2)}) collective-permute-start(f32[8,8,1024]{2,1,0:T(8,128)S(1)} %pad_maximum_fusion.1.refs_0_), channel_id=1, source_target_pairs={{24,0},{25,1},{26,2},{27,3},{28,4},{29,5},{30,6},{31,7},{0,8},{1,9... | collective-permute-start | bytes 786440 | tf_op jit(solution)/shard_map/ppermute | solution.py:57
  24.7 16.0 %collective-permute-start.7 = (f32[8,8,1024]{2,1,0:T(8,128)S(1)}, f32[8,8,1024]{2,1,0:T(8,128)S(1)}, u32[]{:S(2)}, u32[]{:S(2)}) collective-permute-start(f32[8,8,1024]{2,1,0:T(8,128)S(1)} %pad_maximum_fusion.refs_0_), channel_id=1, source_target_pairs={{32,0},{33,1},{34,2},{35,3},{36,4},{37,5},{38,6},{39,7},{40,8},{41... | collective-permute-start | bytes 786440 | tf_op jit(solution)/shard_map/ppermute | solution.py:57
  27.1 13.6 %collective-permute-start.8 = (f32[8,8,1024]{2,1,0:T(8,128)S(1)}, f32[8,8,1024]{2,1,0:T(8,128)S(1)}, u32[]{:S(2)}, u32[]{:S(2)}) collective-permute-start(f32[8,8,1024]{2,1,0:T(8,128)S(1)} %pad_maximum_fusion.refs_0_), channel_id=1, source_target_pairs={{64,0},{65,1},{66,2},{67,3},{68,4},{69,5},{70,6},{71,7},{72,8},{73... | collective-permute-start | bytes 786440 | tf_op jit(solution)/shard_map/ppermute | solution.py:57
  29.6 11.1 %collective-permute-start.9 = (f32[8,8,1024]{2,1,0:T(8,128)S(1)}, f32[8,8,1024]{2,1,0:T(8,128)S(1)}, u32[]{:S(2)}, u32[]{:S(2)}) collective-permute-start(f32[8,8,1024]{2,1,0:T(8,128)S(1)} %pad_maximum_fusion.refs_0_), channel_id=1, source_target_pairs={{96,0},{97,1},{98,2},{99,3},{100,4},{101,5},{102,6},{103,7},{104,8... | collective-permute-start | bytes 786440 | tf_op jit(solution)/shard_map/ppermute | solution.py:57
  37.3 3.5 %copy-start = (f32[32,64]{1,0:T(8,128)S(1)}, f32[32,64]{1,0:T(8,128)}, u32[]{:S(2)}) copy-start(f32[32,64]{1,0:T(8,128)} %basis_ref.1) | copy-start | bytes 24580
  44.1 1.3 %collective-permute-start.13 = (f32[32,384]{1,0:T(8,128)S(1)}, f32[32,384]{1,0:T(8,128)S(1)}, u32[]{:S(2)}, u32[]{:S(2)}) collective-permute-start(f32[32,384]{1,0:T(8,128)S(1)} %image_b.1.mine_ref), channel_id=1, source_target_pairs={{1,0},{0,1},{3,2},{2,3},{5,4},{4,5},{7,6},{6,7},{9,8},{8,9},{11,10... | collective-permute-start | bytes 147464 | tf_op jit(solution)/shard_map/ppermute | solution.py:57
  46.1 3.7 %collective-permute-start.14 = (f32[32,384]{1,0:T(8,128)S(1)}, f32[32,384]{1,0:T(8,128)S(1)}, u32[]{:S(2)}, u32[]{:S(2)}) collective-permute-start(f32[32,384]{1,0:T(8,128)S(1)} %pair.1.mine_ref), channel_id=1, source_target_pairs={{3,0},{2,1},{1,2},{0,3},{7,4},{6,5},{5,6},{4,7},{11,8},{10,9},{9,1... | collective-permute-start | bytes 147464 | tf_op jit(solution)/shard_map/ppermute | solution.py:57
  50.6 4.7 %collective-permute-start.15 = (f32[32,128]{1,0:T(8,128)S(1)}, f32[32,128]{1,0:T(8,128)S(1)}, u32[]{:S(2)}, u32[]{:S(2)}) collective-permute-start(f32[32,128]{1,0:T(8,128)S(1)} %get-tuple-element.19), channel_id=1, source_target_pairs={{7,0},{6,1},{5,2},{4,3},{3,4},{2,5},{1,6},{0,7},{15,8},{14,9},{13,... | collective-permute-start | bytes 49160 | tf_op jit(solution)/shard_map/ppermute | solution.py:57

commit v3 on v2

--- a/solution.py
+++ b/solution.py
@@ -12,7 +12,7 @@
 R = 32
 XS = 4
 YS = 4
-HALF = 1024
+C = 2048
 ROWS = 256
 OWN = 64
 AXES = ("x", "y", "zh", "zl", "core")
@@ -39,18 +39,24 @@
     return pairs
 
 
-def from_x(step):
-    return sources(lambda x, y, zh, zl, core: ((x + step) % XS, y, zh, zl, core))
-
-
-def from_y(step):
-    return sources(lambda x, y, zh, zl, core: (x, (y + step) % YS, zh, zl, core))
+def ring(step, x_core):
+    def source(x, y, zh, zl, core):
+        if core == x_core:
+            return (x + step) % XS, y, zh, zl, core
+        return x, (y + step) % YS, zh, zl, core
+
+    return sources(source)
 
 
 FROM_ZH = sources(lambda x, y, zh, zl, core: (x, y, 1 - zh, zl, core))
 FROM_CORE = sources(lambda x, y, zh, zl, core: (x, y, zh, zl, 1 - core))
-FROM_ZL = sources(lambda x, y, zh, zl, core: (x, y, zh, 1 - zl, 1 - core))
-FROM_Z = sources(lambda x, y, zh, zl, core: (x, y, 1 - zh, 1 - zl, 1 - core))
+
+def along_z(step):
+    def source(x, y, zh, zl, core):
+        z = (zh * 2 + zl + step) % 4
+        return x, y, z // 2, z % 2, 1 - core
+
+    return sources(source)
 
 
 def move(value, pairs):
@@ -81,55 +87,43 @@
     )(coefficients)
 
 
-def half_image(half, place_ref, pieces, block, held):
+def image_kernel(place_ref, *refs):
+    pieces, (block, basis_ref, out_ref, held) = refs[:8], refs[8:]
     total = None
     for k in range(K):
         rows = jnp.concatenate([piece[:, k, :] for piece in pieces], axis=0)
         rows_high, rows_low = split(rows)
         both = jnp.concatenate([rows_high, rows_low], axis=0)
-        high, low = split(block[k, :, half * HALF : (half + 1) * HALF])
+        high, low = split(block[k])
         main = lax.dot_general(both, high, NT, preferred_element_type=jnp.float32)
         rest = lax.dot_general(rows_high, low, NT, preferred_element_type=jnp.float32)
         part = main[:R] + main[R:] + rest
         total = part if total is None else total + part
     held[...] = total
-    x0, y0, zh0 = place_ref[0], place_ref[1], place_ref[2]
-    ordered = []
+    x0, y0, zh0, core = place_ref[0], place_ref[1], place_ref[2], place_ref[4]
     for x in range(XS):
         for y in range(YS):
             for zh in range(2):
                 dx = (x - x0 + XS) % XS
                 dy = (y - y0 + YS) % YS
                 dz = (zh + zh0) % 2
-                outer, inner = (dy, dx) if half == 0 else (dx, dy)
-                ordered.append(held[pl.ds(outer * 8 + inner * 2 + dz, 1), :])
-    return ordered
-
-
-def first_half_kernel(place_ref, *refs):
-    pieces, (block, out_ref, held) = refs[:4], refs[4:]
-    for i, row in enumerate(half_image(0, place_ref, pieces, block, held)):
-        out_ref[i : i + 1, :] = row
-
-
-def second_half_kernel(place_ref, *refs):
-    pieces, (block, first_ref, basis_ref, out_ref, held) = refs[:4], refs[4:]
-    for i, row in enumerate(half_image(1, place_ref, pieces, block, held)):
-        out_ref[i : i + 1, 0:ROWS] = first_ref[i : i + 1, :] + row
+                slot = dz * 16 + jnp.where(core == 0, dy * 4 + dx, dx * 4 + dy)
+                row = (x * YS + y) * 2 + zh
+                out_ref[row : row + 1, 0:ROWS] = held[pl.ds(slot, 1), :]
     out_ref[:, ROWS : ROWS + OWN] = basis_ref[...]
     out_ref[:, ROWS + OWN :] = jnp.zeros_like(basis_ref)
 
 
-def image_call(kernel, name, width, *args):
-    return pl.pallas_call(
-        kernel,
-        in_specs=[SM] + [VM] * (len(args) - 1),
+def image_part(place, pieces, block, basis):
+    return pl.pallas_call(
+        image_kernel,
+        in_specs=[SM] + [VM] * (len(pieces) + 2),
         out_specs=VM,
-        out_shape=jax.ShapeDtypeStruct((R, width), jnp.float32),
+        out_shape=jax.ShapeDtypeStruct((R, ROWS + 2 * OWN), jnp.float32),
         scratch_shapes=[pltpu.VMEM((R, ROWS), jnp.float32)],
         compiler_params=pltpu.CompilerParams(vmem_limit_bytes=6 << 20),
-        name=name,
-    )(*args)
+        name="image",
+    )(place, *pieces, block, basis)
 
 
 def in_order(second, mine, other):
@@ -153,28 +147,57 @@
     )(place, mine, other)
 
 
-def products_kernel(place_ref, mine_ref, other_ref, image_ref, products_ref):
-    image = mine_ref[:, 0:ROWS] + other_ref[:, 0:ROWS]
-    image_ref[...] = image
-    basis = in_order(place_ref[3] == 1, mine_ref[:, ROWS:], other_ref[:, ROWS:])
+def products_kernel(place_ref, *refs):
+    parts, (image_ref, products_ref, held) = refs[:4], refs[4:]
+    zh = place_ref[2]
+    z = zh * 2 + place_ref[3]
+    for step, part in enumerate(parts):
+        held[pl.ds((z + step) % 4, 1)] = part[...][None]
+    images = [held[2 * h, :, 0:ROWS] + held[2 * h + 1, :, 0:ROWS] for h in range(2)]
+    image_ref[...] = jnp.where(zh == 0, images[0], images[1])
+    image = jnp.concatenate(images, axis=1)
+    basis = jnp.concatenate([held[i, :, ROWS:] for i in range(4)], axis=1)
     both = jnp.concatenate([image, basis], axis=0)
     of_image = lax.dot_general(image, both, NT, precision=HI, preferred_element_type=jnp.float32)
     of_basis = lax.dot_general(basis, both, NT, precision=HI, preferred_element_type=jnp.float32)
     products_ref[...] = jnp.concatenate([of_image, of_basis], axis=1)
 
 
-def products(place, mine, other):
+def products(place, parts):
     return pl.pallas_call(
         products_kernel,
-        in_specs=[SM, VM, VM],
+        in_specs=[SM] + [VM] * 4,
         out_specs=[VM] * 2,
         out_shape=[
             jax.ShapeDtypeStruct((R, ROWS), jnp.float32),
             jax.ShapeDtypeStruct((R, 4 * R), jnp.float32),
         ],
+        scratch_shapes=[pltpu.VMEM((4, *parts[0].shape), jnp.float32)],
         compiler_params=pltpu.CompilerParams(vmem_limit_bytes=2 << 20),
         name="products",
-    )(place, mine, other)
+    )(place, *parts)
+
+
+def eliminate(work):
+    lane = lax.broadcasted_iota(jnp.int32, (1, 4 * R), 1)
+    done = []
+    for k in range(0, R, 8):
+        columns = [jnp.broadcast_to(work[:, k + m : k + m + 1], work.shape) for m in range(8)]
+        rows = [work[k + m : k + m + 1, :] for m in range(8)]
+        update = jnp.zeros_like(work)
+        for m in range(8):
+            at = k + m
+            scale = lax.rsqrt(columns[m][at : at + 1, :])
+            unit = rows[m] * scale
+            column = columns[m] * scale
+            done.append(jnp.where(lane >= at, unit, 0.0))
+            for t in range(m + 1, 8):
+                factor = columns[t][at : at + 1, :] * scale
+                rows[t] = rows[t] - column[k + t : k + t + 1, :] * unit
+                columns[t] = columns[t] - column * factor
+            update = update + column * unit
+        work = work - update
+    return jnp.concatenate(done, axis=0)
 
 
 def final_kernel(place_ref, products_ref, image_ref, basis_ref, new_ref, projection_ref, factor_ref):
@@ -197,16 +220,7 @@
         own = jnp.where(narrow == n, image_ref[:, n * 64 : (n + 1) * 64], own)
     twice = own - dot(projection_t, basis_ref[...], NN)
     work = jnp.concatenate([gram, jnp.zeros((R, R), jnp.float32), twice], axis=1)
-    lane = lax.broadcasted_iota(jnp.int32, (1, 4 * R), 1)
-    done = []
-    for k in range(R):
-        row = work[k : k + 1, :]
-        column = work[:, k : k + 1]
-        scale = 1.0 / jnp.sqrt(work[k : k + 1, k : k + 1])
-        unit = row * scale
-        done.append(jnp.where(lane >= k, unit, 0.0))
-        work = work - (column * scale) * unit
-    rows = jnp.concatenate(done, axis=0)
+    rows = eliminate(work)
     factor_ref[...] = rows[:, 0:R].T
     new_ref[...] = rows[:, 2 * R : 4 * R]
 
@@ -230,30 +244,19 @@
     coefficients = pltpu.with_memory_space_constraint(coefficients, pltpu.HBM)
     place = jnp.stack([lax.axis_index(axis) for axis in AXES]).astype(jnp.int32)
 
-    own = tensor_blocks.reshape(K, 2 * HALF)
-    across = move(own, FROM_ZH)
-    both = jnp.stack([own, across])
-    a, b = both[:, :, :HALF], both[:, :, HALF:]
-    moved = [move(a, from_x(s)) for s in (1, 2, 3)] + [move(b, from_y(s)) for s in (1, 2, 3)]
-    *moved, coefficients = lax.optimization_barrier((*moved, coefficients))
+    own = tensor_blocks.reshape(K, C)
+    moved = [move(own, ring(step, 0)) for step in (1, 2, 3)]
+    row = jnp.stack(lax.optimization_barrier([own, *moved]))
+    across = move(row, FROM_ZH)
+    coefficients, across = lax.optimization_barrier((coefficients, across))
     loaded = load(coefficients)
-    a = jnp.concatenate([a] + moved[:3])
-    b = jnp.concatenate([b] + moved[3:])
-    pieces_b = {0: b}
-    for s in (2, 3, 1):
-        pieces_b[s] = move(b, from_x(s))
-    pieces_a = {0: a}
-    for s in (2, 3, 1):
-        pieces_a[s] = move(a, from_y(s))
-
-    part = image_call(first_half_kernel, "image_a", ROWS, place, *[pieces_a[s] for s in range(4)], loaded)
-    pieces = [pieces_b[s] for s in range(4)]
-    part = image_call(
-        second_half_kernel, "image_b", ROWS + 2 * OWN, place, *pieces, loaded, part, basis_rows
-    )
+    pieces = []
+    for blocks in (row, across):
+        pieces += [blocks] + [move(blocks, ring(step, 1)) for step in (1, 2, 3)]
+
+    part = image_part(place, pieces, loaded, basis_rows)
     part = pair(place, part, move(part, FROM_CORE))
-    image, total = products(place, part, move(part, FROM_ZL))
-    total = total + move(total, FROM_Z)
+    image, total = products(place, [part] + [move(part, along_z(step)) for step in (1, 2, 3)])
     total = jnp.broadcast_to(total, (XS * YS, *total.shape))
     total = lax.all_to_all(total, ("x", "y"), 0, 0, tiled=True)
     return tuple(final(place, total, image, basis_rows))

time: 74.9 us -> 65.6 us (0.88)
  waiting for transfers between devices: 13.4 us -> 8.15 us
  Pallas kernels: 19 us -> 15.9 us
  starting transfers between devices: 26.1 us -> 24.5 us
  blocking collectives: 14.3 us -> 15.1 us
    ppermute x16 -> x14, waiting for transfers between devices: 13.4 us -> 8.15 us  [move(): return lax.ppermute(value, AXES, pairs)]
    pallas_call x1, Pallas kernels: 5.04 us -> 2.75 us  [final(): pl.pallas_call(final_kernel, in_specs=[SM] + [VM] * 3, out_specs=[VM] * 3...]
    ppermute x16 -> x14, starting transfers between devices: 26.1 us -> 24.5 us  [move(): return lax.ppermute(value, AXES, pairs)]
    pallas_call x3 -> x2, Pallas kernels: 7.58 us -> 6.74 us  [the longest x1 5.79 us: image_part(): pl.pallas_call(image_kernel, in_specs=[SM] + [VM] * (len(pieces) + 2), ou...]
    all_to_all x1, blocking collectives: 14.3 us -> 15.1 us  [body(): total = lax.all_to_all(total, ('x', 'y'), 0, 0, tiled=True)]
  transfers between devices with their start and end apart: 16 -> 14, of which waited for: 9 -> 7; matrix products, arithmetic and copies ran while one was open for 0% -> 0% of each run, Pallas kernels for 12% -> 9%
where the time goes in v3:
time: 65.6 us; the launch traced here: 65.4 us
  starting transfers between devices  24.5 us (37%)
  Pallas kernels  15.9 us (24%)
  blocking collectives  15.1 us (23%)
  waiting for transfers between devices  8.15 us (12%)
  local copies, waits for them, and re-layouts  0.99 us (2%)
  between operations  0.71 us (1%)
    ppermute x14, starting transfers between devices, move(): return lax.ppermute(value, AXES, pairs)  24.5 us
    all_to_all x1, blocking collectives, body(): total = lax.all_to_all(total, ('x', 'y'), 0, 0, tiled=True)  15.1 us
    ppermute x14, waiting for transfers between devices, move(): return lax.ppermute(value, AXES, pairs)  8.15 us
    pallas_call x1, Pallas kernels, image_part(): pl.pallas_call(image_kernel, in_specs=[SM] + [VM] * (len(pieces) + 2), ou...  5.79 us
    pallas_call x1, Pallas kernels, load(): pl.pallas_call(load_kernel, in_specs=[pl.BlockSpec(memory_space=pltpu.HBM...  5.79 us
    pallas_call x1, Pallas kernels, final(): pl.pallas_call(final_kernel, in_specs=[SM] + [VM] * 3, out_specs=[VM] * 3...  2.75 us
  transfers between devices with their start and end apart: 14, of which 7 were waited for; matrix products, arithmetic and copies ran while one was open for 0% of the time, Pallas kernels for 9%

profile of v3, /device:TPU:0, one launch (start us, length us, event | category | flops | bytes accessed | tf_op | source)
XLA Modules:
  0.0 65.4 jit_solution(15843580044785781366)
XLA Ops:
  0.6 0.9 %copy.8 = f32[8,1,2048]{2,0,1:T(8,128)S(1)} copy(f32[8,1,2048]{2,1,0:T(1,128)} %param.4) | data formatting | bytes 131072
  1.5 1.6 %collective-permute-start.2 = (f32[8,2048]{1,0:T(8,128)S(1)}, f32[8,2048]{1,0:T(8,128)S(1)}, u32[]{:S(2)}, u32[]{:S(2)}) collective-permute-start(f32[8,2048]{1,0:T(8,128)S(1)} %bitcast.12), channel_id=1, source_target_pairs={{96,0},{25,1},{98,2},{27,3},{100,4},{29,5},{102,6},{31,7},{104,8},... | collective-permute-start | bytes 196616 | tf_op jit(solution)/shard_map/ppermute | solution.py:63
  3.1 2.7 %collective-permute-start.1 = (f32[8,2048]{1,0:T(8,128)S(1)}, f32[8,2048]{1,0:T(8,128)S(1)}, u32[]{:S(2)}, u32[]{:S(2)}) collective-permute-start(f32[8,2048]{1,0:T(8,128)S(1)} %bitcast.13), channel_id=1, source_target_pairs={{64,0},{17,1},{66,2},{19,3},{68,4},{21,5},{70,6},{23,7},{72,8},{25... | collective-permute-start | bytes 196616 | tf_op jit(solution)/shard_map/ppermute | solution.py:63
  5.9 1.4 %collective-permute-start = (f32[8,2048]{1,0:T(8,128)S(1)}, f32[8,2048]{1,0:T(8,128)S(1)}, u32[]{:S(2)}, u32[]{:S(2)}) collective-permute-start(f32[8,2048]{1,0:T(8,128)S(1)} %bitcast.14), channel_id=1, source_target_pairs={{32,0},{9,1},{34,2},{11,3},{36,4},{13,5},{38,6},{15,7},{40,8},{17,... | collective-permute-start | bytes 196616 | tf_op jit(solution)/shard_map/ppermute | solution.py:63
  7.3 1.6 %collective-permute-done.1 = f32[8,2048]{1,0:T(8,128)S(1)} collective-permute-done((f32[8,2048]{1,0:T(8,128)S(1)}, f32[8,2048]{1,0:T(8,128)S(1)}, u32[]{:S(2)}, u32[]{:S(2)}) %collective-permute-start.1) | collective-permute-done | bytes 65568 | tf_op jit(solution)/shard_map/ppermute | solution.py:63
  8.9 1.2 %collective-permute-done = f32[8,2048]{1,0:T(8,128)S(1)} collective-permute-done((f32[8,2048]{1,0:T(8,128)S(1)}, f32[8,2048]{1,0:T(8,128)S(1)}, u32[]{:S(2)}, u32[]{:S(2)}) %collective-permute-start) | collective-permute-done | bytes 65568 | tf_op jit(solution)/shard_map/ppermute | solution.py:63
  10.2 4.0 %collective-permute-start.6 = (f32[4,8,2048]{2,1,0:T(8,128)S(1)}, f32[4,8,2048]{2,1,0:T(8,128)S(1)}, u32[]{:S(2)}, u32[]{:S(2)}) collective-permute-start(f32[4,8,2048]{2,1,0:T(8,128)S(1)} %pad_maximum_fusion.refs_0_), channel_id=1, source_target_pairs={{4,0},{5,1},{6,2},{7,3},{0,4},{1,5},{2,6},{3,7},{12,8},{13,9},{14,... | collective-permute-start | bytes 786440 | tf_op jit(solution)/shard_map/ppermute | solution.py:63
  14.1 1.6 %collective-permute-start.5 = (f32[4,8,2048]{2,1,0:T(8,128)S(1)}, f32[4,8,2048]{2,1,0:T(8,128)S(1)}, u32[]{:S(2)}, u32[]{:S(2)}) collective-permute-start(f32[4,8,2048]{2,1,0:T(8,128)S(1)} %pad_maximum_fusion.refs_0_), channel_id=1, source_target_pairs={{24,0},{97,1},{26,2},{99,3},{28,4},{101,5},{30,6},{103,7},{0,8},{1... | collective-permute-start | bytes 786440 | tf_op jit(solution)/shard_map/ppermute | solution.py:63
  15.7 2.9 %collective-permute-start.4 = (f32[4,8,2048]{2,1,0:T(8,128)S(1)}, f32[4,8,2048]{2,1,0:T(8,128)S(1)}, u32[]{:S(2)}, u32[]{:S(2)}) collective-permute-start(f32[4,8,2048]{2,1,0:T(8,128)S(1)} %pad_maximum_fusion.refs_0_), channel_id=1, source_target_pairs={{16,0},{65,1},{18,2},{67,3},{20,4},{69,5},{22,6},{71,7},{24,8},{73... | collective-permute-start | bytes 786440 | tf_op jit(solution)/shard_map/ppermute | solution.py:63
  18.6 1.3 %collective-permute-start.3 = (f32[4,8,2048]{2,1,0:T(8,128)S(1)}, f32[4,8,2048]{2,1,0:T(8,128)S(1)}, u32[]{:S(2)}, u32[]{:S(2)}) collective-permute-start(f32[4,8,2048]{2,1,0:T(8,128)S(1)} %pad_maximum_fusion.refs_0_), channel_id=1, source_target_pairs={{8,0},{33,1},{10,2},{35,3},{12,4},{37,5},{14,6},{39,7},{16,8},{41,... | collective-permute-start | bytes 786440 | tf_op jit(solution)/shard_map/ppermute | solution.py:63
  20.6 2.7 %collective-permute-start.8 = (f32[4,8,2048]{2,1,0:T(8,128)S(1)}, f32[4,8,2048]{2,1,0:T(8,128)S(1)}, u32[]{:S(2)}, u32[]{:S(2)}) collective-permute-start(f32[4,8,2048]{2,1,0:T(8,128)S(1)} %collective-permute-done.6.refs_4_), channel_id=1, source_target_pairs={{16,0},{65,1},{18,2},{67,3},{20,4},{69,5},{22,6},{71,7},{24,8},{73... | collective-permute-start | bytes 786440 | tf_op jit(solution)/shard_map/ppermute | solution.py:63
  23.3 1.0 %collective-permute-start.7 = (f32[4,8,2048]{2,1,0:T(8,128)S(1)}, f32[4,8,2048]{2,1,0:T(8,128)S(1)}, u32[]{:S(2)}, u32[]{:S(2)}) collective-permute-start(f32[4,8,2048]{2,1,0:T(8,128)S(1)} %collective-permute-done.6.refs_4_), channel_id=1, source_target_pairs={{8,0},{33,1},{10,2},{35,3},{12,4},{37,5},{14,6},{39,7},{16,8},{41,... | collective-permute-start | bytes 786440 | tf_op jit(solution)/shard_map/ppermute | solution.py:63
  24.4 5.8 %load.1.refs_8_ = f32[8,256,2048]{2,1,0:T(8,128)S(1)} custom-call(f32[8,256,2048]{2,1,0:T(8,128)} %source_ref), custom_call_target="tpu_custom_call" | custom-call | tf_op jit(solution)/shard_map/load/pallas_call | solution.py:79
  30.2 1.2 %collective-permute-done.8.refs_6_ = f32[4,8,2048]{2,1,0:T(8,128)S(1)} collective-permute-done((f32[4,8,2048]{2,1,0:T(8,128)S(1)}, f32[4,8,2048]{2,1,0:T(8,128)S(1)}, u32[]{:S(2)}, u32[]{:S(2)}) %collective-permute-start.8) | collective-permute-done | bytes 262176 | tf_op jit(solution)/shard_map/ppermute | solution.py:63
  31.4 5.8 %image.1.mine_ref = f32[32,384]{1,0:T(8,128)S(1)} custom-call(s32[5]{0:T(128)S(1)} %stack.38.place_ref, f32[4,8,2048]{2,1,0:T(8,128)S(1)} %pad_maximum_fusion.refs_0_, f32[4,8,2048]{2,1,0:T(8,128)S(1)} %collective-permute-done.3.refs_1_, f32[4,8,2048]{2,1,0:T(8,128)S(1)} %collective-permute-done.4.refs_2_, f32[4,8,2048]{2,1,0:T(8,128)S(1)} %collective-permute-done.5.refs_3_, ...), custom_call_target="tpu_custom_call" | custom-call | tf_op jit(solution)/shard_map/image/pallas_call | solution.py:118
  37.3 1.2 %collective-permute-done.10.other_ref = f32[32,384]{1,0:T(8,128)S(1)} collective-permute-done((f32[32,384]{1,0:T(8,128)S(1)}, f32[32,384]{1,0:T(8,128)S(1)}, u32[]{:S(2)}, u32[]{:S(2)}) %collective-permute-start.10) | collective-permute-done | bytes 49184 | tf_op jit(solution)/shard_map/ppermute | solution.py:63
  39.1 0.8 %collective-permute-start.13 = (f32[32,384]{1,0:T(8,128)S(1)}, f32[32,384]{1,0:T(8,128)S(1)}, u32[]{:S(2)}, u32[]{:S(2)}) collective-permute-start(f32[32,384]{1,0:T(8,128)S(1)} %pair.1.refs_0_), channel_id=1, source_target_pairs={{7,0},{6,1},{1,2},{0,3},{3,4},{2,5},{5,6},{4,7},{15,8},{14,9},{9,1... | collective-permute-start | bytes 147464 | tf_op jit(solution)/shard_map/ppermute | solution.py:63
  39.9 3.0 %collective-permute-start.12 = (f32[32,384]{1,0:T(8,128)S(1)}, f32[32,384]{1,0:T(8,128)S(1)}, u32[]{:S(2)}, u32[]{:S(2)}) collective-permute-start(f32[32,384]{1,0:T(8,128)S(1)} %pair.1.refs_0_), channel_id=1, source_target_pairs={{5,0},{4,1},{7,2},{6,3},{1,4},{0,5},{3,6},{2,7},{13,8},{12,9},{15,... | collective-permute-start | bytes 147464 | tf_op jit(solution)/shard_map/ppermute | solution.py:63
  42.8 0.8 %collective-permute-start.11 = (f32[32,384]{1,0:T(8,128)S(1)}, f32[32,384]{1,0:T(8,128)S(1)}, u32[]{:S(2)}, u32[]{:S(2)}) collective-permute-start(f32[32,384]{1,0:T(8,128)S(1)} %pair.1.refs_0_), channel_id=1, source_target_pairs={{3,0},{2,1},{5,2},{4,3},{7,4},{6,5},{1,6},{0,7},{11,8},{10,9},{13,... | collective-permute-start | bytes 147464 | tf_op jit(solution)/shard_map/ppermute | solution.py:63
  44.0 1.8 %collective-permute-done.12.refs_2_ = f32[32,384]{1,0:T(8,128)S(1)} collective-permute-done((f32[32,384]{1,0:T(8,128)S(1)}, f32[32,384]{1,0:T(8,128)S(1)}, u32[]{:S(2)}, u32[]{:S(2)}) %collective-permute-start.12) | collective-permute-done | bytes 49184 | tf_op jit(solution)/shard_map/ppermute | solution.py:63
  45.9 0.7 %collective-permute-done.11.refs_1_ = f32[32,384]{1,0:T(8,128)S(1)} collective-permute-done((f32[32,384]{1,0:T(8,128)S(1)}, f32[32,384]{1,0:T(8,128)S(1)}, u32[]{:S(2)}, u32[]{:S(2)}) %collective-permute-start.11) | collective-permute-done | bytes 49184 | tf_op jit(solution)/shard_map/ppermute | solution.py:63
  46.5 1.0 %products.1 = (f32[32,256]{1,0:T(8,128)S(1)}, f32[32,128]{1,0:T(8,128)S(1)}) custom-call(s32[5]{0:T(128)S(1)} %stack.38.place_ref, f32[32,384]{1,0:T(8,128)S(1)} %pair.1.refs_0_, f32[32,384]{1,0:T(8,128)S(1)} %collective-permute-done.11.refs_1_, f32[32,384]{1,0:T(8,128)S(1)} %collective-permute-done.12.refs_2_, f32[32,384]{1,0:T(8,128)S(1)} %collective-permute-done.13.refs_3_), custom_call_target="tpu_custom_call" | custom-call | tf_op jit(solution)/shard_map/products/pallas_call | solution.py:167
  47.5 15.1 %all_to_all.5.products_ref = f32[16,32,128]{2,1,0:T(8,128)S(1)} all-to-all(f32[16,32,128]{2,1,0:T(8,128)S(1)} %broadcast_in_dim.3), channel_id=1, replica_groups=mesh['x'=4,'y'=4,'zh'=2,'zl'=2,'core'=2] {'x','y'}, dimensions={0} | all-to-all | bytes 524288 | tf_op jit(solution)/shard_map/all_to_all | solution.py:261
  62.7 2.8 %final.1 = (f32[32,64]{1,0:T(8,128)}, f32[32,32]{1,0:T(8,128)}, f32[32,32]{1,0:T(8,128)}) custom-call(s32[5]{0:T(128)S(1)} %stack.38.place_ref, f32[16,32,128]{2,1,0:T(8,128)S(1)} %all_to_all.5.products_ref, f32[32,256]{1,0:T(8,128)S(1)} %get-tuple-element.18.image_ref, f32[32,64]{1,0:T(8,128)S(1)} %copy-done), custom_call_target="tpu_custom_call" | custom-call | tf_op jit(solution)/shard_map/final/pallas_call | solution.py:229
  (16 shorter events, 1.9 us)
Async XLA Ops:
  1.5 5.8 %collective-permute-start.2 = (f32[8,2048]{1,0:T(8,128)S(1)}, f32[8,2048]{1,0:T(8,128)S(1)}, u32[]{:S(2)}, u32[]{:S(2)}) collective-permute-start(f32[8,2048]{1,0:T(8,128)S(1)} %bitcast.12), channel_id=1, source_target_pairs={{96,0},{25,1},{98,2},{27,3},{100,4},{29,5},{102,6},{31,7},{104,8},... | collective-permute-start | bytes 196616 | tf_op jit(solution)/shard_map/ppermute | solution.py:63
  3.1 5.8 %collective-permute-start.1 = (f32[8,2048]{1,0:T(8,128)S(1)}, f32[8,2048]{1,0:T(8,128)S(1)}, u32[]{:S(2)}, u32[]{:S(2)}) collective-permute-start(f32[8,2048]{1,0:T(8,128)S(1)} %bitcast.13), channel_id=1, source_target_pairs={{64,0},{17,1},{66,2},{19,3},{68,4},{21,5},{70,6},{23,7},{72,8},{25... | collective-permute-start | bytes 196616 | tf_op jit(solution)/shard_map/ppermute | solution.py:63
  5.9 4.3 %collective-permute-start = (f32[8,2048]{1,0:T(8,128)S(1)}, f32[8,2048]{1,0:T(8,128)S(1)}, u32[]{:S(2)}, u32[]{:S(2)}) collective-permute-start(f32[8,2048]{1,0:T(8,128)S(1)} %bitcast.14), channel_id=1, source_target_pairs={{32,0},{9,1},{34,2},{11,3},{36,4},{13,5},{38,6},{15,7},{40,8},{17,... | collective-permute-start | bytes 196616 | tf_op jit(solution)/shard_map/ppermute | solution.py:63
  10.2 9.8 %collective-permute-start.6 = (f32[4,8,2048]{2,1,0:T(8,128)S(1)}, f32[4,8,2048]{2,1,0:T(8,128)S(1)}, u32[]{:S(2)}, u32[]{:S(2)}) collective-permute-start(f32[4,8,2048]{2,1,0:T(8,128)S(1)} %pad_maximum_fusion.refs_0_), channel_id=1, source_target_pairs={{4,0},{5,1},{6,2},{7,3},{0,4},{1,5},{2,6},{3,7},{12,8},{13,9},{14,... | collective-permute-start | bytes 786440 | tf_op jit(solution)/shard_map/ppermute | solution.py:63
  14.1 9.2 %collective-permute-start.5 = (f32[4,8,2048]{2,1,0:T(8,128)S(1)}, f32[4,8,2048]{2,1,0:T(8,128)S(1)}, u32[]{:S(2)}, u32[]{:S(2)}) collective-permute-start(f32[4,8,2048]{2,1,0:T(8,128)S(1)} %pad_maximum_fusion.refs_0_), channel_id=1, source_target_pairs={{24,0},{97,1},{26,2},{99,3},{28,4},{101,5},{30,6},{103,7},{0,8},{1... | collective-permute-start | bytes 786440 | tf_op jit(solution)/shard_map/ppermute | solution.py:63
  15.7 14.5 %collective-permute-start.4 = (f32[4,8,2048]{2,1,0:T(8,128)S(1)}, f32[4,8,2048]{2,1,0:T(8,128)S(1)}, u32[]{:S(2)}, u32[]{:S(2)}) collective-permute-start(f32[4,8,2048]{2,1,0:T(8,128)S(1)} %pad_maximum_fusion.refs_0_), channel_id=1, source_target_pairs={{16,0},{65,1},{18,2},{67,3},{20,4},{69,5},{22,6},{71,7},{24,8},{73... | collective-permute-start | bytes 786440 | tf_op jit(solution)/shard_map/ppermute | solution.py:63
  18.6 11.6 %collective-permute-start.3 = (f32[4,8,2048]{2,1,0:T(8,128)S(1)}, f32[4,8,2048]{2,1,0:T(8,128)S(1)}, u32[]{:S(2)}, u32[]{:S(2)}) collective-permute-start(f32[4,8,2048]{2,1,0:T(8,128)S(1)} %pad_maximum_fusion.refs_0_), channel_id=1, source_target_pairs={{8,0},{33,1},{10,2},{35,3},{12,4},{37,5},{14,6},{39,7},{16,8},{41,... | collective-permute-start | bytes 786440 | tf_op jit(solution)/shard_map/ppermute | solution.py:63
  19.9 10.3 %collective-permute-start.9 = (f32[4,8,2048]{2,1,0:T(8,128)S(1)}, f32[4,8,2048]{2,1,0:T(8,128)S(1)}, u32[]{:S(2)}, u32[]{:S(2)}) collective-permute-start(f32[4,8,2048]{2,1,0:T(8,128)S(1)} %collective-permute-done.6.refs_4_), channel_id=1, source_target_pairs={{24,0},{97,1},{26,2},{99,3},{28,4},{101,5},{30,6},{103,7},{0,8},{1... | collective-permute-start | bytes 786440 | tf_op jit(solution)/shard_map/ppermute | solution.py:63
  20.6 10.7 %collective-permute-start.8 = (f32[4,8,2048]{2,1,0:T(8,128)S(1)}, f32[4,8,2048]{2,1,0:T(8,128)S(1)}, u32[]{:S(2)}, u32[]{:S(2)}) collective-permute-start(f32[4,8,2048]{2,1,0:T(8,128)S(1)} %collective-permute-done.6.refs_4_), channel_id=1, source_target_pairs={{16,0},{65,1},{18,2},{67,3},{20,4},{69,5},{22,6},{71,7},{24,8},{73... | collective-permute-start | bytes 786440 | tf_op jit(solution)/shard_map/ppermute | solution.py:63
  23.3 8.1 %collective-permute-start.7 = (f32[4,8,2048]{2,1,0:T(8,128)S(1)}, f32[4,8,2048]{2,1,0:T(8,128)S(1)}, u32[]{:S(2)}, u32[]{:S(2)}) collective-permute-start(f32[4,8,2048]{2,1,0:T(8,128)S(1)} %collective-permute-done.6.refs_4_), channel_id=1, source_target_pairs={{8,0},{33,1},{10,2},{35,3},{12,4},{37,5},{14,6},{39,7},{16,8},{41,... | collective-permute-start | bytes 786440 | tf_op jit(solution)/shard_map/ppermute | solution.py:63
  24.4 7.0 %copy-start = (f32[32,64]{1,0:T(8,128)S(1)}, f32[32,64]{1,0:T(8,128)}, u32[]{:S(2)}) copy-start(f32[32,64]{1,0:T(8,128)} %basis_ref.1) | copy-start | bytes 24580
  37.2 1.3 %collective-permute-start.10 = (f32[32,384]{1,0:T(8,128)S(1)}, f32[32,384]{1,0:T(8,128)S(1)}, u32[]{:S(2)}, u32[]{:S(2)}) collective-permute-start(f32[32,384]{1,0:T(8,128)S(1)} %image.1.mine_ref), channel_id=1, source_target_pairs={{1,0},{0,1},{3,2},{2,3},{5,4},{4,5},{7,6},{6,7},{9,8},{8,9},{11,10... | collective-permute-start | bytes 147464 | tf_op jit(solution)/shard_map/ppermute | solution.py:63
  39.1 4.9 %collective-permute-start.13 = (f32[32,384]{1,0:T(8,128)S(1)}, f32[32,384]{1,0:T(8,128)S(1)}, u32[]{:S(2)}, u32[]{:S(2)}) collective-permute-start(f32[32,384]{1,0:T(8,128)S(1)} %pair.1.refs_0_), channel_id=1, source_target_pairs={{7,0},{6,1},{1,2},{0,3},{3,4},{2,5},{5,6},{4,7},{15,8},{14,9},{9,1... | collective-permute-start | bytes 147464 | tf_op jit(solution)/shard_map/ppermute | solution.py:63
  39.9 6.0 %collective-permute-start.12 = (f32[32,384]{1,0:T(8,128)S(1)}, f32[32,384]{1,0:T(8,128)S(1)}, u32[]{:S(2)}, u32[]{:S(2)}) collective-permute-start(f32[32,384]{1,0:T(8,128)S(1)} %pair.1.refs_0_), channel_id=1, source_target_pairs={{5,0},{4,1},{7,2},{6,3},{1,4},{0,5},{3,6},{2,7},{13,8},{12,9},{15,... | collective-permute-start | bytes 147464 | tf_op jit(solution)/shard_map/ppermute | solution.py:63
  42.8 3.7 %collective-permute-start.11 = (f32[32,384]{1,0:T(8,128)S(1)}, f32[32,384]{1,0:T(8,128)S(1)}, u32[]{:S(2)}, u32[]{:S(2)}) collective-permute-start(f32[32,384]{1,0:T(8,128)S(1)} %pair.1.refs_0_), channel_id=1, source_target_pairs={{3,0},{2,1},{5,2},{4,3},{7,4},{6,5},{1,6},{0,7},{11,8},{10,9},{13,... | collective-permute-start | bytes 147464 | tf_op jit(solution)/shard_map/ppermute | solution.py:63

commit v4 on v3

--- a/solution.py
+++ b/solution.py
@@ -14,6 +14,7 @@
 YS = 4
 C = 2048
 ROWS = 256
+RB = 128
 OWN = 64
 AXES = ("x", "y", "zh", "zl", "core")
 HI = lax.Precision.HIGHEST
@@ -88,26 +89,27 @@
 
 
 def image_kernel(place_ref, *refs):
-    pieces, (block, basis_ref, out_ref, held) = refs[:8], refs[8:]
-    total = None
+    pieces, (block, basis_ref, out_ref, held, split_rows) = refs[:8], refs[8:]
     for k in range(K):
-        rows = jnp.concatenate([piece[:, k, :] for piece in pieces], axis=0)
-        rows_high, rows_low = split(rows)
-        both = jnp.concatenate([rows_high, rows_low], axis=0)
-        high, low = split(block[k])
-        main = lax.dot_general(both, high, NT, preferred_element_type=jnp.float32)
-        rest = lax.dot_general(rows_high, low, NT, preferred_element_type=jnp.float32)
-        part = main[:R] + main[R:] + rest
-        total = part if total is None else total + part
-    held[...] = total
+        high, low = split(jnp.concatenate([piece[:, k, :] for piece in pieces], axis=0))
+        split_rows[0:R, k * C : (k + 1) * C] = high
+        split_rows[R : 2 * R, k * C : (k + 1) * C] = low
+    for r in range(0, ROWS, RB):
+        total = None
+        for k in range(K):
+            high, low = split(block[k, r : r + RB, :])
+            both = jnp.concatenate([high, low], axis=0)
+            part = lax.dot_general(both, split_rows[:, k * C : (k + 1) * C], NT, preferred_element_type=jnp.float32)
+            total = part if total is None else total + part
+        total = total.T
+        held[:, r : r + RB] = (total[:R, :RB] + total[R:, RB:]) + (total[R:, :RB] + total[:R, RB:])
     x0, y0, zh0, core = place_ref[0], place_ref[1], place_ref[2], place_ref[4]
     for x in range(XS):
         for y in range(YS):
             for zh in range(2):
                 dx = (x - x0 + XS) % XS
                 dy = (y - y0 + YS) % YS
-                dz = (zh + zh0) % 2
-                slot = dz * 16 + jnp.where(core == 0, dy * 4 + dx, dx * 4 + dy)
+                slot = (zh ^ zh0) * 16 + jnp.where(core == 0, dy * 4 + dx, dx * 4 + dy)
                 row = (x * YS + y) * 2 + zh
                 out_ref[row : row + 1, 0:ROWS] = held[pl.ds(slot, 1), :]
     out_ref[:, ROWS : ROWS + OWN] = basis_ref[...]
@@ -120,8 +122,8 @@
         in_specs=[SM] + [VM] * (len(pieces) + 2),
         out_specs=VM,
         out_shape=jax.ShapeDtypeStruct((R, ROWS + 2 * OWN), jnp.float32),
-        scratch_shapes=[pltpu.VMEM((R, ROWS), jnp.float32)],
-        compiler_params=pltpu.CompilerParams(vmem_limit_bytes=6 << 20),
+        scratch_shapes=[pltpu.VMEM((R, ROWS), jnp.float32), pltpu.VMEM((2 * R, K * C), jnp.bfloat16)],
+        compiler_params=pltpu.CompilerParams(vmem_limit_bytes=8 << 20),
         name="image",
     )(place, *pieces, block, basis)
 
@@ -130,21 +132,10 @@
     return jnp.concatenate([jnp.where(second, other, mine), jnp.where(second, mine, other)], axis=1)
 
 
-def pair_kernel(place_ref, mine_ref, other_ref, out_ref):
-    out_ref[:, 0:ROWS] = mine_ref[:, 0:ROWS] + other_ref[:, 0:ROWS]
+def pair(second, mine, other):
     own = slice(ROWS, ROWS + OWN)
-    out_ref[:, ROWS:] = in_order(place_ref[4] == 1, mine_ref[:, own], other_ref[:, own])
-
-
-def pair(place, mine, other):
-    return pl.pallas_call(
-        pair_kernel,
-        in_specs=[SM, VM, VM],
-        out_specs=VM,
-        out_shape=jax.ShapeDtypeStruct(mine.shape, jnp.float32),
-        compiler_params=pltpu.CompilerParams(vmem_limit_bytes=2 << 20),
-        name="pair",
-    )(place, mine, other)
+    image = mine[:, :ROWS] + other[:, :ROWS]
+    return jnp.concatenate([image, in_order(second, mine[:, own], other[:, own])], axis=1)
 
 
 def products_kernel(place_ref, *refs):
@@ -255,7 +246,7 @@
         pieces += [blocks] + [move(blocks, ring(step, 1)) for step in (1, 2, 3)]
 
     part = image_part(place, pieces, loaded, basis_rows)
-    part = pair(place, part, move(part, FROM_CORE))
+    part = pair(place[4] == 1, part, move(part, FROM_CORE))
     image, total = products(place, [part] + [move(part, along_z(step)) for step in (1, 2, 3)])
     total = jnp.broadcast_to(total, (XS * YS, *total.shape))
     total = lax.all_to_all(total, ("x", "y"), 0, 0, tiled=True)

time: 65.6 us -> 64.5 us (0.983)
  Pallas kernels: 15.9 us -> 14.7 us
where the time goes in v4:
time: 64.5 us; the launch traced here: 64.3 us
  starting transfers between devices  24.5 us (38%)
  blocking collectives  15.1 us (23%)
  Pallas kernels  14.7 us (23%)
  waiting for transfers between devices  8.16 us (13%)
  local copies, waits for them, and re-layouts  0.99 us (2%)
  between operations  0.71 us (1%)
    ppermute x14, starting transfers between devices, move(): return lax.ppermute(value, AXES, pairs)  24.5 us
    all_to_all x1, blocking collectives, body(): total = lax.all_to_all(total, ('x', 'y'), 0, 0, tiled=True)  15.1 us
    ppermute x14, waiting for transfers between devices, move(): return lax.ppermute(value, AXES, pairs)  8.16 us
    pallas_call x1, Pallas kernels, load(): pl.pallas_call(load_kernel, in_specs=[pl.BlockSpec(memory_space=pltpu.HBM...  5.79 us
    pallas_call x1, Pallas kernels, image_part(): pl.pallas_call(image_kernel, in_specs=[SM] + [VM] * (len(pieces) + 2), ou...  5.18 us
    pallas_call x1, Pallas kernels, final(): pl.pallas_call(final_kernel, in_specs=[SM] + [VM] * 3, out_specs=[VM] * 3...  2.75 us
  transfers between devices with their start and end apart: 14, of which 7 were waited for; matrix products, arithmetic and copies ran while one was open for 0% of the time, Pallas kernels for 9%

profile of v4, /device:TPU:0, one launch (start us, length us, event | category | flops | bytes accessed | tf_op | source)
XLA Modules:
  0.0 64.3 jit_solution(7530217688222854633)
XLA Ops:
  0.6 0.9 %copy.8 = f32[8,1,2048]{2,0,1:T(8,128)S(1)} copy(f32[8,1,2048]{2,1,0:T(1,128)} %param.4) | data formatting | bytes 131072
  1.5 1.6 %collective-permute-start.2 = (f32[8,2048]{1,0:T(8,128)S(1)}, f32[8,2048]{1,0:T(8,128)S(1)}, u32[]{:S(2)}, u32[]{:S(2)}) collective-permute-start(f32[8,2048]{1,0:T(8,128)S(1)} %bitcast.12), channel_id=1, source_target_pairs={{96,0},{25,1},{98,2},{27,3},{100,4},{29,5},{102,6},{31,7},{104,8},... | collective-permute-start | bytes 196616 | tf_op jit(solution)/shard_map/ppermute | solution.py:64
  3.1 2.7 %collective-permute-start.1 = (f32[8,2048]{1,0:T(8,128)S(1)}, f32[8,2048]{1,0:T(8,128)S(1)}, u32[]{:S(2)}, u32[]{:S(2)}) collective-permute-start(f32[8,2048]{1,0:T(8,128)S(1)} %bitcast.13), channel_id=1, source_target_pairs={{64,0},{17,1},{66,2},{19,3},{68,4},{21,5},{70,6},{23,7},{72,8},{25... | collective-permute-start | bytes 196616 | tf_op jit(solution)/shard_map/ppermute | solution.py:64
  5.9 1.4 %collective-permute-start = (f32[8,2048]{1,0:T(8,128)S(1)}, f32[8,2048]{1,0:T(8,128)S(1)}, u32[]{:S(2)}, u32[]{:S(2)}) collective-permute-start(f32[8,2048]{1,0:T(8,128)S(1)} %bitcast.14), channel_id=1, source_target_pairs={{32,0},{9,1},{34,2},{11,3},{36,4},{13,5},{38,6},{15,7},{40,8},{17,... | collective-permute-start | bytes 196616 | tf_op jit(solution)/shard_map/ppermute | solution.py:64
  7.3 1.6 %collective-permute-done.1 = f32[8,2048]{1,0:T(8,128)S(1)} collective-permute-done((f32[8,2048]{1,0:T(8,128)S(1)}, f32[8,2048]{1,0:T(8,128)S(1)}, u32[]{:S(2)}, u32[]{:S(2)}) %collective-permute-start.1) | collective-permute-done | bytes 65568 | tf_op jit(solution)/shard_map/ppermute | solution.py:64
  8.9 1.2 %collective-permute-done = f32[8,2048]{1,0:T(8,128)S(1)} collective-permute-done((f32[8,2048]{1,0:T(8,128)S(1)}, f32[8,2048]{1,0:T(8,128)S(1)}, u32[]{:S(2)}, u32[]{:S(2)}) %collective-permute-start) | collective-permute-done | bytes 65568 | tf_op jit(solution)/shard_map/ppermute | solution.py:64
  10.2 4.0 %collective-permute-start.6 = (f32[4,8,2048]{2,1,0:T(8,128)S(1)}, f32[4,8,2048]{2,1,0:T(8,128)S(1)}, u32[]{:S(2)}, u32[]{:S(2)}) collective-permute-start(f32[4,8,2048]{2,1,0:T(8,128)S(1)} %pad_maximum_fusion.refs_0_), channel_id=1, source_target_pairs={{4,0},{5,1},{6,2},{7,3},{0,4},{1,5},{2,6},{3,7},{12,8},{13,9},{14,... | collective-permute-start | bytes 786440 | tf_op jit(solution)/shard_map/ppermute | solution.py:64
  14.1 1.6 %collective-permute-start.5 = (f32[4,8,2048]{2,1,0:T(8,128)S(1)}, f32[4,8,2048]{2,1,0:T(8,128)S(1)}, u32[]{:S(2)}, u32[]{:S(2)}) collective-permute-start(f32[4,8,2048]{2,1,0:T(8,128)S(1)} %pad_maximum_fusion.refs_0_), channel_id=1, source_target_pairs={{24,0},{97,1},{26,2},{99,3},{28,4},{101,5},{30,6},{103,7},{0,8},{1... | collective-permute-start | bytes 786440 | tf_op jit(solution)/shard_map/ppermute | solution.py:64
  15.7 2.9 %collective-permute-start.4 = (f32[4,8,2048]{2,1,0:T(8,128)S(1)}, f32[4,8,2048]{2,1,0:T(8,128)S(1)}, u32[]{:S(2)}, u32[]{:S(2)}) collective-permute-start(f32[4,8,2048]{2,1,0:T(8,128)S(1)} %pad_maximum_fusion.refs_0_), channel_id=1, source_target_pairs={{16,0},{65,1},{18,2},{67,3},{20,4},{69,5},{22,6},{71,7},{24,8},{73... | collective-permute-start | bytes 786440 | tf_op jit(solution)/shard_map/ppermute | solution.py:64
  18.6 1.3 %collective-permute-start.3 = (f32[4,8,2048]{2,1,0:T(8,128)S(1)}, f32[4,8,2048]{2,1,0:T(8,128)S(1)}, u32[]{:S(2)}, u32[]{:S(2)}) collective-permute-start(f32[4,8,2048]{2,1,0:T(8,128)S(1)} %pad_maximum_fusion.refs_0_), channel_id=1, source_target_pairs={{8,0},{33,1},{10,2},{35,3},{12,4},{37,5},{14,6},{39,7},{16,8},{41,... | collective-permute-start | bytes 786440 | tf_op jit(solution)/shard_map/ppermute | solution.py:64
  20.6 2.7 %collective-permute-start.8 = (f32[4,8,2048]{2,1,0:T(8,128)S(1)}, f32[4,8,2048]{2,1,0:T(8,128)S(1)}, u32[]{:S(2)}, u32[]{:S(2)}) collective-permute-start(f32[4,8,2048]{2,1,0:T(8,128)S(1)} %collective-permute-done.6.refs_4_), channel_id=1, source_target_pairs={{16,0},{65,1},{18,2},{67,3},{20,4},{69,5},{22,6},{71,7},{24,8},{73... | collective-permute-start | bytes 786440 | tf_op jit(solution)/shard_map/ppermute | solution.py:64
  23.3 1.0 %collective-permute-start.7 = (f32[4,8,2048]{2,1,0:T(8,128)S(1)}, f32[4,8,2048]{2,1,0:T(8,128)S(1)}, u32[]{:S(2)}, u32[]{:S(2)}) collective-permute-start(f32[4,8,2048]{2,1,0:T(8,128)S(1)} %collective-permute-done.6.refs_4_), channel_id=1, source_target_pairs={{8,0},{33,1},{10,2},{35,3},{12,4},{37,5},{14,6},{39,7},{16,8},{41,... | collective-permute-start | bytes 786440 | tf_op jit(solution)/shard_map/ppermute | solution.py:64
  24.4 5.8 %load.1.refs_8_ = f32[8,256,2048]{2,1,0:T(8,128)S(1)} custom-call(f32[8,256,2048]{2,1,0:T(8,128)} %source_ref), custom_call_target="tpu_custom_call" | custom-call | tf_op jit(solution)/shard_map/load/pallas_call | solution.py:80
  30.2 1.2 %collective-permute-done.8.refs_6_ = f32[4,8,2048]{2,1,0:T(8,128)S(1)} collective-permute-done((f32[4,8,2048]{2,1,0:T(8,128)S(1)}, f32[4,8,2048]{2,1,0:T(8,128)S(1)}, u32[]{:S(2)}, u32[]{:S(2)}) %collective-permute-start.8) | collective-permute-done | bytes 262176 | tf_op jit(solution)/shard_map/ppermute | solution.py:64
  31.4 5.2 %image.1 = f32[32,384]{1,0:T(8,128)S(1)} custom-call(s32[5]{0:T(128)S(1)} %stack.38.place_ref, f32[4,8,2048]{2,1,0:T(8,128)S(1)} %pad_maximum_fusion.refs_0_, f32[4,8,2048]{2,1,0:T(8,128)S(1)} %collective-permute-done.3.refs_1_, f32[4,8,2048]{2,1,0:T(8,128)S(1)} %collective-permute-done.4.refs_2_, f32[4,8,2048]{2,1,0:T(8,128)S(1)} %collective-permute-done.5.refs_3_, ...), custom_call_target="tpu_custom_call" | custom-call | tf_op jit(solution)/shard_map/image/pallas_call | solution.py:120
  36.6 1.2 %collective-permute-done.10 = f32[32,384]{1,0:T(8,128)S(1)} collective-permute-done((f32[32,384]{1,0:T(8,128)S(1)}, f32[32,384]{1,0:T(8,128)S(1)}, u32[]{:S(2)}, u32[]{:S(2)}) %collective-permute-start.10) | collective-permute-done | bytes 49184 | tf_op jit(solution)/shard_map/ppermute | solution.py:64
  38.0 0.8 %collective-permute-start.13 = (f32[32,384]{1,0:T(8,128)S(1)}, f32[32,384]{1,0:T(8,128)S(1)}, u32[]{:S(2)}, u32[]{:S(2)}) collective-permute-start(f32[32,384]{1,0:T(8,128)S(1)} %pad_maximum_fusion.1.refs_0_), channel_id=1, source_target_pairs={{7,0},{6,1},{1,2},{0,3},{3,4},{2,5},{5,6},{4,7},{15,8},{14,9},{9,1... | collective-permute-start | bytes 147464 | tf_op jit(solution)/shard_map/ppermute | solution.py:64
  38.8 3.0 %collective-permute-start.12 = (f32[32,384]{1,0:T(8,128)S(1)}, f32[32,384]{1,0:T(8,128)S(1)}, u32[]{:S(2)}, u32[]{:S(2)}) collective-permute-start(f32[32,384]{1,0:T(8,128)S(1)} %pad_maximum_fusion.1.refs_0_), channel_id=1, source_target_pairs={{5,0},{4,1},{7,2},{6,3},{1,4},{0,5},{3,6},{2,7},{13,8},{12,9},{15,... | collective-permute-start | bytes 147464 | tf_op jit(solution)/shard_map/ppermute | solution.py:64
  41.7 0.8 %collective-permute-start.11 = (f32[32,384]{1,0:T(8,128)S(1)}, f32[32,384]{1,0:T(8,128)S(1)}, u32[]{:S(2)}, u32[]{:S(2)}) collective-permute-start(f32[32,384]{1,0:T(8,128)S(1)} %pad_maximum_fusion.1.refs_0_), channel_id=1, source_target_pairs={{3,0},{2,1},{5,2},{4,3},{7,4},{6,5},{1,6},{0,7},{11,8},{10,9},{13,... | collective-permute-start | bytes 147464 | tf_op jit(solution)/shard_map/ppermute | solution.py:64
  42.9 1.8 %collective-permute-done.12.refs_2_ = f32[32,384]{1,0:T(8,128)S(1)} collective-permute-done((f32[32,384]{1,0:T(8,128)S(1)}, f32[32,384]{1,0:T(8,128)S(1)}, u32[]{:S(2)}, u32[]{:S(2)}) %collective-permute-start.12) | collective-permute-done | bytes 49184 | tf_op jit(solution)/shard_map/ppermute | solution.py:64
  44.7 0.7 %collective-permute-done.11.refs_1_ = f32[32,384]{1,0:T(8,128)S(1)} collective-permute-done((f32[32,384]{1,0:T(8,128)S(1)}, f32[32,384]{1,0:T(8,128)S(1)}, u32[]{:S(2)}, u32[]{:S(2)}) %collective-permute-start.11) | collective-permute-done | bytes 49184 | tf_op jit(solution)/shard_map/ppermute | solution.py:64
  45.4 1.0 %products.1 = (f32[32,256]{1,0:T(8,128)S(1)}, f32[32,128]{1,0:T(8,128)S(1)}) custom-call(s32[5]{0:T(128)S(1)} %stack.38.place_ref, f32[32,384]{1,0:T(8,128)S(1)} %pad_maximum_fusion.1.refs_0_, f32[32,384]{1,0:T(8,128)S(1)} %collective-permute-done.11.refs_1_, f32[32,384]{1,0:T(8,128)S(1)} %collective-permute-done.12.refs_2_, ...), custom_call_target="tpu_custom_call" | custom-call | tf_op jit(solution)/shard_map/products/pallas_call | solution.py:158
  46.4 15.1 %all_to_all.5.products_ref = f32[16,32,128]{2,1,0:T(8,128)S(1)} all-to-all(f32[16,32,128]{2,1,0:T(8,128)S(1)} %broadcast_in_dim.3), channel_id=1, replica_groups=mesh['x'=4,'y'=4,'zh'=2,'zl'=2,'core'=2] {'x','y'}, dimensions={0} | all-to-all | bytes 524288 | tf_op jit(solution)/shard_map/all_to_all | solution.py:252
  61.5 2.8 %final.1 = (f32[32,64]{1,0:T(8,128)}, f32[32,32]{1,0:T(8,128)}, f32[32,32]{1,0:T(8,128)}) custom-call(s32[5]{0:T(128)S(1)} %stack.38.place_ref, f32[16,32,128]{2,1,0:T(8,128)S(1)} %all_to_all.5.products_ref, f32[32,256]{1,0:T(8,128)S(1)} %get-tuple-element.18.image_ref, f32[32,64]{1,0:T(8,128)S(1)} %copy-done), custom_call_target="tpu_custom_call" | custom-call | tf_op jit(solution)/shard_map/final/pallas_call | solution.py:220
  (18 shorter events, 1.4 us)
Async XLA Ops:
  1.5 5.8 %collective-permute-start.2 = (f32[8,2048]{1,0:T(8,128)S(1)}, f32[8,2048]{1,0:T(8,128)S(1)}, u32[]{:S(2)}, u32[]{:S(2)}) collective-permute-start(f32[8,2048]{1,0:T(8,128)S(1)} %bitcast.12), channel_id=1, source_target_pairs={{96,0},{25,1},{98,2},{27,3},{100,4},{29,5},{102,6},{31,7},{104,8},... | collective-permute-start | bytes 196616 | tf_op jit(solution)/shard_map/ppermute | solution.py:64
  3.1 5.8 %collective-permute-start.1 = (f32[8,2048]{1,0:T(8,128)S(1)}, f32[8,2048]{1,0:T(8,128)S(1)}, u32[]{:S(2)}, u32[]{:S(2)}) collective-permute-start(f32[8,2048]{1,0:T(8,128)S(1)} %bitcast.13), channel_id=1, source_target_pairs={{64,0},{17,1},{66,2},{19,3},{68,4},{21,5},{70,6},{23,7},{72,8},{25... | collective-permute-start | bytes 196616 | tf_op jit(solution)/shard_map/ppermute | solution.py:64
  5.9 4.3 %collective-permute-start = (f32[8,2048]{1,0:T(8,128)S(1)}, f32[8,2048]{1,0:T(8,128)S(1)}, u32[]{:S(2)}, u32[]{:S(2)}) collective-permute-start(f32[8,2048]{1,0:T(8,128)S(1)} %bitcast.14), channel_id=1, source_target_pairs={{32,0},{9,1},{34,2},{11,3},{36,4},{13,5},{38,6},{15,7},{40,8},{17,... | collective-permute-start | bytes 196616 | tf_op jit(solution)/shard_map/ppermute | solution.py:64
  10.2 9.8 %collective-permute-start.6 = (f32[4,8,2048]{2,1,0:T(8,128)S(1)}, f32[4,8,2048]{2,1,0:T(8,128)S(1)}, u32[]{:S(2)}, u32[]{:S(2)}) collective-permute-start(f32[4,8,2048]{2,1,0:T(8,128)S(1)} %pad_maximum_fusion.refs_0_), channel_id=1, source_target_pairs={{4,0},{5,1},{6,2},{7,3},{0,4},{1,5},{2,6},{3,7},{12,8},{13,9},{14,... | collective-permute-start | bytes 786440 | tf_op jit(solution)/shard_map/ppermute | solution.py:64
  14.1 9.2 %collective-permute-start.5 = (f32[4,8,2048]{2,1,0:T(8,128)S(1)}, f32[4,8,2048]{2,1,0:T(8,128)S(1)}, u32[]{:S(2)}, u32[]{:S(2)}) collective-permute-start(f32[4,8,2048]{2,1,0:T(8,128)S(1)} %pad_maximum_fusion.refs_0_), channel_id=1, source_target_pairs={{24,0},{97,1},{26,2},{99,3},{28,4},{101,5},{30,6},{103,7},{0,8},{1... | collective-permute-start | bytes 786440 | tf_op jit(solution)/shard_map/ppermute | solution.py:64
  15.7 14.5 %collective-permute-start.4 = (f32[4,8,2048]{2,1,0:T(8,128)S(1)}, f32[4,8,2048]{2,1,0:T(8,128)S(1)}, u32[]{:S(2)}, u32[]{:S(2)}) collective-permute-start(f32[4,8,2048]{2,1,0:T(8,128)S(1)} %pad_maximum_fusion.refs_0_), channel_id=1, source_target_pairs={{16,0},{65,1},{18,2},{67,3},{20,4},{69,5},{22,6},{71,7},{24,8},{73... | collective-permute-start | bytes 786440 | tf_op jit(solution)/shard_map/ppermute | solution.py:64
  18.6 11.6 %collective-permute-start.3 = (f32[4,8,2048]{2,1,0:T(8,128)S(1)}, f32[4,8,2048]{2,1,0:T(8,128)S(1)}, u32[]{:S(2)}, u32[]{:S(2)}) collective-permute-start(f32[4,8,2048]{2,1,0:T(8,128)S(1)} %pad_maximum_fusion.refs_0_), channel_id=1, source_target_pairs={{8,0},{33,1},{10,2},{35,3},{12,4},{37,5},{14,6},{39,7},{16,8},{41,... | collective-permute-start | bytes 786440 | tf_op jit(solution)/shard_map/ppermute | solution.py:64
  19.9 10.3 %collective-permute-start.9 = (f32[4,8,2048]{2,1,0:T(8,128)S(1)}, f32[4,8,2048]{2,1,0:T(8,128)S(1)}, u32[]{:S(2)}, u32[]{:S(2)}) collective-permute-start(f32[4,8,2048]{2,1,0:T(8,128)S(1)} %collective-permute-done.6.refs_4_), channel_id=1, source_target_pairs={{24,0},{97,1},{26,2},{99,3},{28,4},{101,5},{30,6},{103,7},{0,8},{1... | collective-permute-start | bytes 786440 | tf_op jit(solution)/shard_map/ppermute | solution.py:64
  20.6 10.7 %collective-permute-start.8 = (f32[4,8,2048]{2,1,0:T(8,128)S(1)}, f32[4,8,2048]{2,1,0:T(8,128)S(1)}, u32[]{:S(2)}, u32[]{:S(2)}) collective-permute-start(f32[4,8,2048]{2,1,0:T(8,128)S(1)} %collective-permute-done.6.refs_4_), channel_id=1, source_target_pairs={{16,0},{65,1},{18,2},{67,3},{20,4},{69,5},{22,6},{71,7},{24,8},{73... | collective-permute-start | bytes 786440 | tf_op jit(solution)/shard_map/ppermute | solution.py:64
  23.3 8.1 %collective-permute-start.7 = (f32[4,8,2048]{2,1,0:T(8,128)S(1)}, f32[4,8,2048]{2,1,0:T(8,128)S(1)}, u32[]{:S(2)}, u32[]{:S(2)}) collective-permute-start(f32[4,8,2048]{2,1,0:T(8,128)S(1)} %collective-permute-done.6.refs_4_), channel_id=1, source_target_pairs={{8,0},{33,1},{10,2},{35,3},{12,4},{37,5},{14,6},{39,7},{16,8},{41,... | collective-permute-start | bytes 786440 | tf_op jit(solution)/shard_map/ppermute | solution.py:64
  24.4 7.0 %copy-start = (f32[32,64]{1,0:T(8,128)S(1)}, f32[32,64]{1,0:T(8,128)}, u32[]{:S(2)}) copy-start(f32[32,64]{1,0:T(8,128)} %basis_ref.1) | copy-start | bytes 24580
  36.6 1.3 %collective-permute-start.10 = (f32[32,384]{1,0:T(8,128)S(1)}, f32[32,384]{1,0:T(8,128)S(1)}, u32[]{:S(2)}, u32[]{:S(2)}) collective-permute-start(f32[32,384]{1,0:T(8,128)S(1)} %image.1), channel_id=1, source_target_pairs={{1,0},{0,1},{3,2},{2,3},{5,4},{4,5},{7,6},{6,7},{9,8},{8,9},{11,10... | collective-permute-start | bytes 147464 | tf_op jit(solution)/shard_map/ppermute | solution.py:64
  38.0 4.9 %collective-permute-start.13 = (f32[32,384]{1,0:T(8,128)S(1)}, f32[32,384]{1,0:T(8,128)S(1)}, u32[]{:S(2)}, u32[]{:S(2)}) collective-permute-start(f32[32,384]{1,0:T(8,128)S(1)} %pad_maximum_fusion.1.refs_0_), channel_id=1, source_target_pairs={{7,0},{6,1},{1,2},{0,3},{3,4},{2,5},{5,6},{4,7},{15,8},{14,9},{9,1... | collective-permute-start | bytes 147464 | tf_op jit(solution)/shard_map/ppermute | solution.py:64
  38.8 6.0 %collective-permute-start.12 = (f32[32,384]{1,0:T(8,128)S(1)}, f32[32,384]{1,0:T(8,128)S(1)}, u32[]{:S(2)}, u32[]{:S(2)}) collective-permute-start(f32[32,384]{1,0:T(8,128)S(1)} %pad_maximum_fusion.1.refs_0_), channel_id=1, source_target_pairs={{5,0},{4,1},{7,2},{6,3},{1,4},{0,5},{3,6},{2,7},{13,8},{12,9},{15,... | collective-permute-start | bytes 147464 | tf_op jit(solution)/shard_map/ppermute | solution.py:64
  41.7 3.7 %collective-permute-start.11 = (f32[32,384]{1,0:T(8,128)S(1)}, f32[32,384]{1,0:T(8,128)S(1)}, u32[]{:S(2)}, u32[]{:S(2)}) collective-permute-start(f32[32,384]{1,0:T(8,128)S(1)} %pad_maximum_fusion.1.refs_0_), channel_id=1, source_target_pairs={{3,0},{2,1},{5,2},{4,3},{7,4},{6,5},{1,6},{0,7},{11,8},{10,9},{13,... | collective-permute-start | bytes 147464 | tf_op jit(solution)/shard_map/ppermute | solution.py:64

commit v5 on v4

--- a/solution.py
+++ b/solution.py
@@ -236,14 +236,18 @@
     place = jnp.stack([lax.axis_index(axis) for axis in AXES]).astype(jnp.int32)
 
     own = tensor_blocks.reshape(K, C)
+    own_across = move(own, FROM_ZH)
     moved = [move(own, ring(step, 0)) for step in (1, 2, 3)]
-    row = jnp.stack(lax.optimization_barrier([own, *moved]))
-    across = move(row, FROM_ZH)
+    own, *moved = lax.optimization_barrier([own, *moved])
+    row = jnp.stack([own, *moved])
+    across = move(jnp.stack(moved), FROM_ZH)
+    far, one, three = [move(row, ring(step, 1)) for step in (2, 1, 3)]
+    across = jnp.concatenate([own_across[None], across])
+    far_across = move(far, FROM_ZH)
     coefficients, across = lax.optimization_barrier((coefficients, across))
     loaded = load(coefficients)
-    pieces = []
-    for blocks in (row, across):
-        pieces += [blocks] + [move(blocks, ring(step, 1)) for step in (1, 2, 3)]
+    one_across, three_across = [move(across, ring(step, 1)) for step in (1, 3)]
+    pieces = [row, one, far, three, across, one_across, far_across, three_across]
 
     part = image_part(place, pieces, loaded, basis_rows)
     part = pair(place[4] == 1, part, move(part, FROM_CORE))

time: 64.5 us -> 62.6 us (0.971)
  waiting for transfers between devices: 8.16 us -> 5.39 us
  starting transfers between devices: 24.5 us -> 26.9 us
  blocking collectives: 15.1 us -> 13.5 us
    ppermute x14 -> x15, waiting for transfers between devices: 8.16 us -> 5.39 us  [move(): return lax.ppermute(value, AXES, pairs)]
    ppermute x14 -> x15, starting transfers between devices: 24.5 us -> 26.9 us  [move(): return lax.ppermute(value, AXES, pairs)]
    all_to_all x1, blocking collectives: 15.1 us -> 13.5 us  [body(): total = lax.all_to_all(total, ('x', 'y'), 0, 0, tiled=True)]
  transfers between devices with their start and end apart: 14 -> 15, of which waited for: 7 -> 5; matrix products, arithmetic and copies ran while one was open for 0% -> 0% of each run, Pallas kernels for 9% -> 9%
where the time goes in v5:
time: 62.6 us; the launch traced here: 62.4 us
  starting transfers between devices  26.9 us (43%)
  Pallas kernels  14.7 us (23%)
  blocking collectives  13.5 us (22%)
  waiting for transfers between devices  5.39 us (9%)
  local copies, waits for them, and re-layouts  0.99 us (2%)
  between operations  0.74 us (1%)
    ppermute x15, starting transfers between devices, move(): return lax.ppermute(value, AXES, pairs)  26.9 us
    all_to_all x1, blocking collectives, body(): total = lax.all_to_all(total, ('x', 'y'), 0, 0, tiled=True)  13.5 us
    pallas_call x1, Pallas kernels, load(): pl.pallas_call(load_kernel, in_specs=[pl.BlockSpec(memory_space=pltpu.HBM...  5.79 us
    ppermute x15, waiting for transfers between devices, move(): return lax.ppermute(value, AXES, pairs)  5.39 us
    pallas_call x1, Pallas kernels, image_part(): pl.pallas_call(image_kernel, in_specs=[SM] + [VM] * (len(pieces) + 2), ou...  5.18 us
    pallas_call x1, Pallas kernels, final(): pl.pallas_call(final_kernel, in_specs=[SM] + [VM] * 3, out_specs=[VM] * 3...  2.75 us
  transfers between devices with their start and end apart: 15, of which 5 were waited for; matrix products, arithmetic and copies ran while one was open for 0% of the time, Pallas kernels for 9%

profile of v5, /device:TPU:0, one launch (start us, length us, event | category | flops | bytes accessed | tf_op | source)
XLA Modules:
  0.0 62.4 jit_solution(7265746945982763685)
XLA Ops:
  0.6 0.9 %copy.8 = f32[8,1,2048]{2,0,1:T(8,128)S(1)} copy(f32[8,1,2048]{2,1,0:T(1,128)} %param.4) | data formatting | bytes 131072
  1.5 1.6 %collective-permute-start.2 = (f32[8,2048]{1,0:T(8,128)S(1)}, f32[8,2048]{1,0:T(8,128)S(1)}, u32[]{:S(2)}, u32[]{:S(2)}) collective-permute-start(f32[8,2048]{1,0:T(8,128)S(1)} %bitcast.13), channel_id=1, source_target_pairs={{96,0},{25,1},{98,2},{27,3},{100,4},{29,5},{102,6},{31,7},{104,8},... | collective-permute-start | bytes 196616 | tf_op jit(solution)/shard_map/ppermute | solution.py:64
  3.1 2.7 %collective-permute-start.1 = (f32[8,2048]{1,0:T(8,128)S(1)}, f32[8,2048]{1,0:T(8,128)S(1)}, u32[]{:S(2)}, u32[]{:S(2)}) collective-permute-start(f32[8,2048]{1,0:T(8,128)S(1)} %bitcast.14), channel_id=1, source_target_pairs={{64,0},{17,1},{66,2},{19,3},{68,4},{21,5},{70,6},{23,7},{72,8},{25... | collective-permute-start | bytes 196616 | tf_op jit(solution)/shard_map/ppermute | solution.py:64
  5.9 1.4 %collective-permute-start = (f32[8,2048]{1,0:T(8,128)S(1)}, f32[8,2048]{1,0:T(8,128)S(1)}, u32[]{:S(2)}, u32[]{:S(2)}) collective-permute-start(f32[8,2048]{1,0:T(8,128)S(1)} %bitcast.15), channel_id=1, source_target_pairs={{32,0},{9,1},{34,2},{11,3},{36,4},{13,5},{38,6},{15,7},{40,8},{17,... | collective-permute-start | bytes 196616 | tf_op jit(solution)/shard_map/ppermute | solution.py:64
  7.3 3.9 %collective-permute-start.6 = (f32[8,2048]{1,0:T(8,128)S(1)}, f32[8,2048]{1,0:T(8,128)S(1)}, u32[]{:S(2)}, u32[]{:S(2)}) collective-permute-start(f32[8,2048]{1,0:T(8,128)S(1)} %bitcast.16), channel_id=1, source_target_pairs={{4,0},{5,1},{6,2},{7,3},{0,4},{1,5},{2,6},{3,7},{12,8},{13,9},{14,... | collective-permute-start | bytes 196616 | tf_op jit(solution)/shard_map/ppermute | solution.py:64
  11.2 2.9 %collective-permute-start.7 = (f32[3,8,2048]{2,1,0:T(8,128)S(1)}, f32[3,8,2048]{2,1,0:T(8,128)S(1)}, u32[]{:S(2)}, u32[]{:S(2)}) collective-permute-start(f32[3,8,2048]{2,1,0:T(8,128)S(1)} %pad_maximum_fusion.2), channel_id=1, source_target_pairs={{4,0},{5,1},{6,2},{7,3},{0,4},{1,5},{2,6},{3,7},{12,8},{13,9},{14,... | collective-permute-start | bytes 589832 | tf_op jit(solution)/shard_map/ppermute | solution.py:64
  14.1 3.3 %collective-permute-start.4 = (f32[4,8,2048]{2,1,0:T(8,128)S(1)}, f32[4,8,2048]{2,1,0:T(8,128)S(1)}, u32[]{:S(2)}, u32[]{:S(2)}) collective-permute-start(f32[4,8,2048]{2,1,0:T(8,128)S(1)} %pad_maximum_fusion.refs_0_), channel_id=1, source_target_pairs={{16,0},{65,1},{18,2},{67,3},{20,4},{69,5},{22,6},{71,7},{24,8},{73... | collective-permute-start | bytes 786440 | tf_op jit(solution)/shard_map/ppermute | solution.py:64
  17.4 0.7 %collective-permute-start.5 = (f32[4,8,2048]{2,1,0:T(8,128)S(1)}, f32[4,8,2048]{2,1,0:T(8,128)S(1)}, u32[]{:S(2)}, u32[]{:S(2)}) collective-permute-start(f32[4,8,2048]{2,1,0:T(8,128)S(1)} %pad_maximum_fusion.refs_0_), channel_id=1, source_target_pairs={{24,0},{97,1},{26,2},{99,3},{28,4},{101,5},{30,6},{103,7},{0,8},{1... | collective-permute-start | bytes 786440 | tf_op jit(solution)/shard_map/ppermute | solution.py:64
  18.1 2.6 %collective-permute-start.3 = (f32[4,8,2048]{2,1,0:T(8,128)S(1)}, f32[4,8,2048]{2,1,0:T(8,128)S(1)}, u32[]{:S(2)}, u32[]{:S(2)}) collective-permute-start(f32[4,8,2048]{2,1,0:T(8,128)S(1)} %pad_maximum_fusion.refs_0_), channel_id=1, source_target_pairs={{8,0},{33,1},{10,2},{35,3},{12,4},{37,5},{14,6},{39,7},{16,8},{41,... | collective-permute-start | bytes 786440 | tf_op jit(solution)/shard_map/ppermute | solution.py:64
  20.8 3.2 %collective-permute-start.8 = (f32[4,8,2048]{2,1,0:T(8,128)S(1)}, f32[4,8,2048]{2,1,0:T(8,128)S(1)}, u32[]{:S(2)}, u32[]{:S(2)}) collective-permute-start(f32[4,8,2048]{2,1,0:T(8,128)S(1)} %pad_maximum_fusion.1.refs_4_), channel_id=1, source_target_pairs={{8,0},{33,1},{10,2},{35,3},{12,4},{37,5},{14,6},{39,7},{16,8},{41,... | collective-permute-start | bytes 786440 | tf_op jit(solution)/shard_map/ppermute | solution.py:64
  24.0 0.7 %collective-permute-start.9 = (f32[4,8,2048]{2,1,0:T(8,128)S(1)}, f32[4,8,2048]{2,1,0:T(8,128)S(1)}, u32[]{:S(2)}, u32[]{:S(2)}) collective-permute-start(f32[4,8,2048]{2,1,0:T(8,128)S(1)} %collective-permute-done.4.refs_2_), channel_id=1, source_target_pairs={{4,0},{5,1},{6,2},{7,3},{0,4},{1,5},{2,6},{3,7},{12,8},{13,9},{14,... | collective-permute-start | bytes 786440 | tf_op jit(solution)/shard_map/ppermute | solution.py:64
  24.8 5.8 %load.1.refs_8_ = f32[8,256,2048]{2,1,0:T(8,128)S(1)} custom-call(f32[8,256,2048]{2,1,0:T(8,128)} %source_ref), custom_call_target="tpu_custom_call" | custom-call | tf_op jit(solution)/shard_map/load/pallas_call | solution.py:80
  30.6 1.2 %collective-permute-done.9.refs_6_ = f32[4,8,2048]{2,1,0:T(8,128)S(1)} collective-permute-done((f32[4,8,2048]{2,1,0:T(8,128)S(1)}, f32[4,8,2048]{2,1,0:T(8,128)S(1)}, u32[]{:S(2)}, u32[]{:S(2)}) %collective-permute-start.9) | collective-permute-done | bytes 262176 | tf_op jit(solution)/shard_map/ppermute | solution.py:64
  31.9 5.2 %image.1 = f32[32,384]{1,0:T(8,128)S(1)} custom-call(s32[5]{0:T(128)S(1)} %stack.44.place_ref, f32[4,8,2048]{2,1,0:T(8,128)S(1)} %pad_maximum_fusion.refs_0_, f32[4,8,2048]{2,1,0:T(8,128)S(1)} %collective-permute-done.3.refs_1_, f32[4,8,2048]{2,1,0:T(8,128)S(1)} %collective-permute-done.4.refs_2_, f32[4,8,2048]{2,1,0:T(8,128)S(1)} %collective-permute-done.5.refs_3_, ...), custom_call_target="tpu_custom_call" | custom-call | tf_op jit(solution)/shard_map/image/pallas_call | solution.py:120
  37.1 1.2 %collective-permute-done.11 = f32[32,384]{1,0:T(8,128)S(1)} collective-permute-done((f32[32,384]{1,0:T(8,128)S(1)}, f32[32,384]{1,0:T(8,128)S(1)}, u32[]{:S(2)}, u32[]{:S(2)}) %collective-permute-start.11) | collective-permute-done | bytes 49184 | tf_op jit(solution)/shard_map/ppermute | solution.py:64
  38.5 0.8 %collective-permute-start.14 = (f32[32,384]{1,0:T(8,128)S(1)}, f32[32,384]{1,0:T(8,128)S(1)}, u32[]{:S(2)}, u32[]{:S(2)}) collective-permute-start(f32[32,384]{1,0:T(8,128)S(1)} %pad_maximum_fusion.3.refs_0_), channel_id=1, source_target_pairs={{7,0},{6,1},{1,2},{0,3},{3,4},{2,5},{5,6},{4,7},{15,8},{14,9},{9,1... | collective-permute-start | bytes 147464 | tf_op jit(solution)/shard_map/ppermute | solution.py:64
  39.2 2.2 %collective-permute-start.13 = (f32[32,384]{1,0:T(8,128)S(1)}, f32[32,384]{1,0:T(8,128)S(1)}, u32[]{:S(2)}, u32[]{:S(2)}) collective-permute-start(f32[32,384]{1,0:T(8,128)S(1)} %pad_maximum_fusion.3.refs_0_), channel_id=1, source_target_pairs={{5,0},{4,1},{7,2},{6,3},{1,4},{0,5},{3,6},{2,7},{13,8},{12,9},{15,... | collective-permute-start | bytes 147464 | tf_op jit(solution)/shard_map/ppermute | solution.py:64
  41.4 0.8 %collective-permute-start.12 = (f32[32,384]{1,0:T(8,128)S(1)}, f32[32,384]{1,0:T(8,128)S(1)}, u32[]{:S(2)}, u32[]{:S(2)}) collective-permute-start(f32[32,384]{1,0:T(8,128)S(1)} %pad_maximum_fusion.3.refs_0_), channel_id=1, source_target_pairs={{3,0},{2,1},{5,2},{4,3},{7,4},{6,5},{1,6},{0,7},{11,8},{10,9},{13,... | collective-permute-start | bytes 147464 | tf_op jit(solution)/shard_map/ppermute | solution.py:64
  42.2 1.2 %collective-permute-done.14.refs_3_ = f32[32,384]{1,0:T(8,128)S(1)} collective-permute-done((f32[32,384]{1,0:T(8,128)S(1)}, f32[32,384]{1,0:T(8,128)S(1)}, u32[]{:S(2)}, u32[]{:S(2)}) %collective-permute-start.14) | collective-permute-done | bytes 49184 | tf_op jit(solution)/shard_map/ppermute | solution.py:64
  43.4 0.9 %collective-permute-done.13.refs_2_ = f32[32,384]{1,0:T(8,128)S(1)} collective-permute-done((f32[32,384]{1,0:T(8,128)S(1)}, f32[32,384]{1,0:T(8,128)S(1)}, u32[]{:S(2)}, u32[]{:S(2)}) %collective-permute-start.13) | collective-permute-done | bytes 49184 | tf_op jit(solution)/shard_map/ppermute | solution.py:64
  44.3 0.8 %collective-permute-done.12.refs_1_ = f32[32,384]{1,0:T(8,128)S(1)} collective-permute-done((f32[32,384]{1,0:T(8,128)S(1)}, f32[32,384]{1,0:T(8,128)S(1)}, u32[]{:S(2)}, u32[]{:S(2)}) %collective-permute-start.12) | collective-permute-done | bytes 49184 | tf_op jit(solution)/shard_map/ppermute | solution.py:64
  45.1 1.0 %products.1 = (f32[32,256]{1,0:T(8,128)S(1)}, f32[32,128]{1,0:T(8,128)S(1)}) custom-call(s32[5]{0:T(128)S(1)} %stack.44.place_ref, f32[32,384]{1,0:T(8,128)S(1)} %pad_maximum_fusion.3.refs_0_, f32[32,384]{1,0:T(8,128)S(1)} %collective-permute-done.12.refs_1_, f32[32,384]{1,0:T(8,128)S(1)} %collective-permute-done.13.refs_2_, ...), custom_call_target="tpu_custom_call" | custom-call | tf_op jit(solution)/shard_map/products/pallas_call | solution.py:158
  46.1 13.5 %all_to_all.5.products_ref = f32[16,32,128]{2,1,0:T(8,128)S(1)} all-to-all(f32[16,32,128]{2,1,0:T(8,128)S(1)} %broadcast_in_dim.7), channel_id=1, replica_groups=mesh['x'=4,'y'=4,'zh'=2,'zl'=2,'core'=2] {'x','y'}, dimensions={0} | all-to-all | bytes 524288 | tf_op jit(solution)/shard_map/all_to_all | solution.py:256
  59.6 2.8 %final.1 = (f32[32,64]{1,0:T(8,128)}, f32[32,32]{1,0:T(8,128)}, f32[32,32]{1,0:T(8,128)}) custom-call(s32[5]{0:T(128)S(1)} %stack.44.place_ref, f32[16,32,128]{2,1,0:T(8,128)S(1)} %all_to_all.5.products_ref, f32[32,256]{1,0:T(8,128)S(1)} %get-tuple-element.18.image_ref, f32[32,64]{1,0:T(8,128)S(1)} %copy-done), custom_call_target="tpu_custom_call" | custom-call | tf_op jit(solution)/shard_map/final/pallas_call | solution.py:220
  (22 shorter events, 0.5 us)
Async XLA Ops:
  1.5 9.7 %collective-permute-start.2 = (f32[8,2048]{1,0:T(8,128)S(1)}, f32[8,2048]{1,0:T(8,128)S(1)}, u32[]{:S(2)}, u32[]{:S(2)}) collective-permute-start(f32[8,2048]{1,0:T(8,128)S(1)} %bitcast.13), channel_id=1, source_target_pairs={{96,0},{25,1},{98,2},{27,3},{100,4},{29,5},{102,6},{31,7},{104,8},... | collective-permute-start | bytes 196616 | tf_op jit(solution)/shard_map/ppermute | solution.py:64
  3.1 8.0 %collective-permute-start.1 = (f32[8,2048]{1,0:T(8,128)S(1)}, f32[8,2048]{1,0:T(8,128)S(1)}, u32[]{:S(2)}, u32[]{:S(2)}) collective-permute-start(f32[8,2048]{1,0:T(8,128)S(1)} %bitcast.14), channel_id=1, source_target_pairs={{64,0},{17,1},{66,2},{19,3},{68,4},{21,5},{70,6},{23,7},{72,8},{25... | collective-permute-start | bytes 196616 | tf_op jit(solution)/shard_map/ppermute | solution.py:64
  5.9 5.3 %collective-permute-start = (f32[8,2048]{1,0:T(8,128)S(1)}, f32[8,2048]{1,0:T(8,128)S(1)}, u32[]{:S(2)}, u32[]{:S(2)}) collective-permute-start(f32[8,2048]{1,0:T(8,128)S(1)} %bitcast.15), channel_id=1, source_target_pairs={{32,0},{9,1},{34,2},{11,3},{36,4},{13,5},{38,6},{15,7},{40,8},{17,... | collective-permute-start | bytes 196616 | tf_op jit(solution)/shard_map/ppermute | solution.py:64
  7.3 13.3 %collective-permute-start.6 = (f32[8,2048]{1,0:T(8,128)S(1)}, f32[8,2048]{1,0:T(8,128)S(1)}, u32[]{:S(2)}, u32[]{:S(2)}) collective-permute-start(f32[8,2048]{1,0:T(8,128)S(1)} %bitcast.16), channel_id=1, source_target_pairs={{4,0},{5,1},{6,2},{7,3},{0,4},{1,5},{2,6},{3,7},{12,8},{13,9},{14,... | collective-permute-start | bytes 196616 | tf_op jit(solution)/shard_map/ppermute | solution.py:64
  11.2 9.4 %collective-permute-start.7 = (f32[3,8,2048]{2,1,0:T(8,128)S(1)}, f32[3,8,2048]{2,1,0:T(8,128)S(1)}, u32[]{:S(2)}, u32[]{:S(2)}) collective-permute-start(f32[3,8,2048]{2,1,0:T(8,128)S(1)} %pad_maximum_fusion.2), channel_id=1, source_target_pairs={{4,0},{5,1},{6,2},{7,3},{0,4},{1,5},{2,6},{3,7},{12,8},{13,9},{14,... | collective-permute-start | bytes 589832 | tf_op jit(solution)/shard_map/ppermute | solution.py:64
  14.1 9.8 %collective-permute-start.4 = (f32[4,8,2048]{2,1,0:T(8,128)S(1)}, f32[4,8,2048]{2,1,0:T(8,128)S(1)}, u32[]{:S(2)}, u32[]{:S(2)}) collective-permute-start(f32[4,8,2048]{2,1,0:T(8,128)S(1)} %pad_maximum_fusion.refs_0_), channel_id=1, source_target_pairs={{16,0},{65,1},{18,2},{67,3},{20,4},{69,5},{22,6},{71,7},{24,8},{73... | collective-permute-start | bytes 786440 | tf_op jit(solution)/shard_map/ppermute | solution.py:64
  17.4 13.2 %collective-permute-start.5 = (f32[4,8,2048]{2,1,0:T(8,128)S(1)}, f32[4,8,2048]{2,1,0:T(8,128)S(1)}, u32[]{:S(2)}, u32[]{:S(2)}) collective-permute-start(f32[4,8,2048]{2,1,0:T(8,128)S(1)} %pad_maximum_fusion.refs_0_), channel_id=1, source_target_pairs={{24,0},{97,1},{26,2},{99,3},{28,4},{101,5},{30,6},{103,7},{0,8},{1... | collective-permute-start | bytes 786440 | tf_op jit(solution)/shard_map/ppermute | solution.py:64
  18.1 12.5 %collective-permute-start.3 = (f32[4,8,2048]{2,1,0:T(8,128)S(1)}, f32[4,8,2048]{2,1,0:T(8,128)S(1)}, u32[]{:S(2)}, u32[]{:S(2)}) collective-permute-start(f32[4,8,2048]{2,1,0:T(8,128)S(1)} %pad_maximum_fusion.refs_0_), channel_id=1, source_target_pairs={{8,0},{33,1},{10,2},{35,3},{12,4},{37,5},{14,6},{39,7},{16,8},{41,... | collective-permute-start | bytes 786440 | tf_op jit(solution)/shard_map/ppermute | solution.py:64
  20.7 9.9 %collective-permute-start.10 = (f32[4,8,2048]{2,1,0:T(8,128)S(1)}, f32[4,8,2048]{2,1,0:T(8,128)S(1)}, u32[]{:S(2)}, u32[]{:S(2)}) collective-permute-start(f32[4,8,2048]{2,1,0:T(8,128)S(1)} %pad_maximum_fusion.1.refs_4_), channel_id=1, source_target_pairs={{24,0},{97,1},{26,2},{99,3},{28,4},{101,5},{30,6},{103,7},{0,8},{1... | collective-permute-start | bytes 786440 | tf_op jit(solution)/shard_map/ppermute | solution.py:64
  20.8 9.9 %collective-permute-start.8 = (f32[4,8,2048]{2,1,0:T(8,128)S(1)}, f32[4,8,2048]{2,1,0:T(8,128)S(1)}, u32[]{:S(2)}, u32[]{:S(2)}) collective-permute-start(f32[4,8,2048]{2,1,0:T(8,128)S(1)} %pad_maximum_fusion.1.refs_4_), channel_id=1, source_target_pairs={{8,0},{33,1},{10,2},{35,3},{12,4},{37,5},{14,6},{39,7},{16,8},{41,... | collective-permute-start | bytes 786440 | tf_op jit(solution)/shard_map/ppermute | solution.py:64
  24.0 7.9 %collective-permute-start.9 = (f32[4,8,2048]{2,1,0:T(8,128)S(1)}, f32[4,8,2048]{2,1,0:T(8,128)S(1)}, u32[]{:S(2)}, u32[]{:S(2)}) collective-permute-start(f32[4,8,2048]{2,1,0:T(8,128)S(1)} %collective-permute-done.4.refs_2_), channel_id=1, source_target_pairs={{4,0},{5,1},{6,2},{7,3},{0,4},{1,5},{2,6},{3,7},{12,8},{13,9},{14,... | collective-permute-start | bytes 786440 | tf_op jit(solution)/shard_map/ppermute | solution.py:64
  24.8 7.1 %copy-start = (f32[32,64]{1,0:T(8,128)S(1)}, f32[32,64]{1,0:T(8,128)}, u32[]{:S(2)}) copy-start(f32[32,64]{1,0:T(8,128)} %basis_ref.1) | copy-start | bytes 24580
  37.0 1.3 %collective-permute-start.11 = (f32[32,384]{1,0:T(8,128)S(1)}, f32[32,384]{1,0:T(8,128)S(1)}, u32[]{:S(2)}, u32[]{:S(2)}) collective-permute-start(f32[32,384]{1,0:T(8,128)S(1)} %image.1), channel_id=1, source_target_pairs={{1,0},{0,1},{3,2},{2,3},{5,4},{4,5},{7,6},{6,7},{9,8},{8,9},{11,10... | collective-permute-start | bytes 147464 | tf_op jit(solution)/shard_map/ppermute | solution.py:64
  38.5 4.9 %collective-permute-start.14 = (f32[32,384]{1,0:T(8,128)S(1)}, f32[32,384]{1,0:T(8,128)S(1)}, u32[]{:S(2)}, u32[]{:S(2)}) collective-permute-start(f32[32,384]{1,0:T(8,128)S(1)} %pad_maximum_fusion.3.refs_0_), channel_id=1, source_target_pairs={{7,0},{6,1},{1,2},{0,3},{3,4},{2,5},{5,6},{4,7},{15,8},{14,9},{9,1... | collective-permute-start | bytes 147464 | tf_op jit(solution)/shard_map/ppermute | solution.py:64
  39.2 5.0 %collective-permute-start.13 = (f32[32,384]{1,0:T(8,128)S(1)}, f32[32,384]{1,0:T(8,128)S(1)}, u32[]{:S(2)}, u32[]{:S(2)}) collective-permute-start(f32[32,384]{1,0:T(8,128)S(1)} %pad_maximum_fusion.3.refs_0_), channel_id=1, source_target_pairs={{5,0},{4,1},{7,2},{6,3},{1,4},{0,5},{3,6},{2,7},{13,8},{12,9},{15,... | collective-permute-start | bytes 147464 | tf_op jit(solution)/shard_map/ppermute | solution.py:64
  41.4 3.7 %collective-permute-start.12 = (f32[32,384]{1,0:T(8,128)S(1)}, f32[32,384]{1,0:T(8,128)S(1)}, u32[]{:S(2)}, u32[]{:S(2)}) collective-permute-start(f32[32,384]{1,0:T(8,128)S(1)} %pad_maximum_fusion.3.refs_0_), channel_id=1, source_target_pairs={{3,0},{2,1},{5,2},{4,3},{7,4},{6,5},{1,6},{0,7},{11,8},{10,9},{13,... | collective-permute-start | bytes 147464 | tf_op jit(solution)/shard_map/ppermute | solution.py:64

commit v6 on v4

--- a/solution.py
+++ b/solution.py
@@ -13,6 +13,7 @@
 XS = 4
 YS = 4
 C = 2048
+LANES = 16
 ROWS = 256
 RB = 128
 OWN = 64
@@ -70,6 +71,24 @@
     return high, low
 
 
+def hold_kernel(source_ref, out_ref, sem):
+    copy = pltpu.make_async_copy(source_ref, out_ref, sem)
+    copy.start()
+    copy.wait()
+
+
+def hold(block):
+    return pl.pallas_call(
+        hold_kernel,
+        in_specs=[pl.BlockSpec(memory_space=pltpu.HBM)],
+        out_specs=VM,
+        out_shape=jax.ShapeDtypeStruct(block.shape, jnp.float32),
+        scratch_shapes=[pltpu.SemaphoreType.DMA],
+        compiler_params=pltpu.CompilerParams(vmem_limit_bytes=1 << 20),
+        name="hold",
+    )(block)
+
+
 def load_kernel(source_ref, out_ref, sem):
     copy = pltpu.make_async_copy(source_ref, out_ref, sem)
     copy.start()
@@ -91,9 +110,11 @@
 def image_kernel(place_ref, *refs):
     pieces, (block, basis_ref, out_ref, held, split_rows) = refs[:8], refs[8:]
     for k in range(K):
-        high, low = split(jnp.concatenate([piece[:, k, :] for piece in pieces], axis=0))
-        split_rows[0:R, k * C : (k + 1) * C] = high
-        split_rows[R : 2 * R, k * C : (k + 1) * C] = low
+        for j in range(LANES):
+            at = k * LANES + j
+            rows = [piece[:, at, :] for piece in pieces]
+            high, low = split(jnp.concatenate(rows, axis=0))
+            split_rows[:, at * 128 : (at + 1) * 128] = jnp.concatenate([high, low], axis=0)
     for r in range(0, ROWS, RB):
         total = None
         for k in range(K):
@@ -109,7 +130,7 @@
             for zh in range(2):
                 dx = (x - x0 + XS) % XS
                 dy = (y - y0 + YS) % YS
-                slot = (zh ^ zh0) * 16 + jnp.where(core == 0, dy * 4 + dx, dx * 4 + dy)
+                slot = (zh ^ zh0) * 16 + jnp.where(core == 1, dy * 4 + dx, dx * 4 + dy)
                 row = (x * YS + y) * 2 + zh
                 out_ref[row : row + 1, 0:ROWS] = held[pl.ds(slot, 1), :]
     out_ref[:, ROWS : ROWS + OWN] = basis_ref[...]
@@ -149,9 +170,8 @@
     image = jnp.concatenate(images, axis=1)
     basis = jnp.concatenate([held[i, :, ROWS:] for i in range(4)], axis=1)
     both = jnp.concatenate([image, basis], axis=0)
-    of_image = lax.dot_general(image, both, NT, precision=HI, preferred_element_type=jnp.float32)
-    of_basis = lax.dot_general(basis, both, NT, precision=HI, preferred_element_type=jnp.float32)
-    products_ref[...] = jnp.concatenate([of_image, of_basis], axis=1)
+    total = lax.dot_general(both, both, NT, precision=HI, preferred_element_type=jnp.float32)
+    products_ref[...] = jnp.concatenate([total[:R], total[R:]], axis=1)
 
 
 def products(place, parts):
@@ -235,15 +255,18 @@
     coefficients = pltpu.with_memory_space_constraint(coefficients, pltpu.HBM)
     place = jnp.stack([lax.axis_index(axis) for axis in AXES]).astype(jnp.int32)
 
-    own = tensor_blocks.reshape(K, C)
-    moved = [move(own, ring(step, 0)) for step in (1, 2, 3)]
-    row = jnp.stack(lax.optimization_barrier([own, *moved]))
+    own = tensor_blocks.reshape(K * LANES, C // LANES)
+    held_own = hold(own)
+    moved = [move(own, ring(step, 1)) for step in (1, 2, 3)]
+    held_own, *moved = lax.optimization_barrier([held_own, *moved])
+    row = jnp.stack([held_own, *moved])
     across = move(row, FROM_ZH)
+    far, one, three = [move(row, ring(step, 0)) for step in (2, 1, 3)]
+    far_across = move(far, FROM_ZH)
     coefficients, across = lax.optimization_barrier((coefficients, across))
     loaded = load(coefficients)
-    pieces = []
-    for blocks in (row, across):
-        pieces += [blocks] + [move(blocks, ring(step, 1)) for step in (1, 2, 3)]
+    one_across, three_across = [move(across, ring(step, 0)) for step in (1, 3)]
+    pieces = [row, one, far, three, across, one_across, far_across, three_across]
 
     part = image_part(place, pieces, loaded, basis_rows)
     part = pair(place[4] == 1, part, move(part, FROM_CORE))

time: 64.5 us -> 62.4 us (0.967)
  waiting for transfers between devices: 8.16 us -> 6.68 us
  blocking collectives: 15.1 us -> 13.9 us
    ppermute x14, waiting for transfers between devices: 8.16 us -> 6.68 us  [move(): return lax.ppermute(value, AXES, pairs)]
    all_to_all x1, blocking collectives: 15.1 us -> 13.9 us  [body(): total = lax.all_to_all(total, ('x', 'y'), 0, 0, tiled=True)]
where the time goes in v6:
time: 62.4 us; the launch traced here: 62.2 us
  starting transfers between devices  24.9 us (40%)
  Pallas kernels  14.9 us (24%)
  blocking collectives  13.9 us (22%)
  waiting for transfers between devices  6.68 us (11%)
  local copies, waits for them, and re-layouts  0.98 us (2%)
  between operations  0.73 us (1%)
    ppermute x14, starting transfers between devices, move(): return lax.ppermute(value, AXES, pairs)  24.9 us
    all_to_all x1, blocking collectives, body(): total = lax.all_to_all(total, ('x', 'y'), 0, 0, tiled=True)  13.9 us
    ppermute x14, waiting for transfers between devices, move(): return lax.ppermute(value, AXES, pairs)  6.68 us
    pallas_call x1, Pallas kernels, load(): pl.pallas_call(load_kernel, in_specs=[pl.BlockSpec(memory_space=pltpu.HBM...  5.79 us
    pallas_call x1, Pallas kernels, image_part(): pl.pallas_call(image_kernel, in_specs=[SM] + [VM] * (len(pieces) + 2), ou...  5.4 us
    pallas_call x1, Pallas kernels, final(): pl.pallas_call(final_kernel, in_specs=[SM] + [VM] * 3, out_specs=[VM] * 3...  2.75 us
  transfers between devices with their start and end apart: 14, of which 7 were waited for; matrix products, arithmetic and copies ran while one was open for 0% of the time, Pallas kernels for 9%

profile of v6, /device:TPU:0, one launch (start us, length us, event | category | flops | bytes accessed | tf_op | source)
XLA Modules:
  0.0 62.2 jit_solution(9542648339989677029)
XLA Ops:
  0.6 1.7 %collective-permute-start.2 = (f32[128,128]{1,0:T(8,128)}, f32[128,128]{1,0:T(8,128)S(1)}, u32[]{:S(2)}, u32[]{:S(2)}) collective-permute-start(f32[128,128]{1,0:T(8,128)} %bitcast.11), channel_id=1, source_target_pairs={{24,0},{97,1},{26,2},{99,3},{28,4},{101,5},{30,6},{103,7},{0,8},{1... | collective-permute-start | bytes 196616 | tf_op jit(solution)/shard_map/ppermute | solution.py:65
  2.4 2.9 %collective-permute-start.1 = (f32[128,128]{1,0:T(8,128)}, f32[128,128]{1,0:T(8,128)S(1)}, u32[]{:S(2)}, u32[]{:S(2)}) collective-permute-start(f32[128,128]{1,0:T(8,128)} %bitcast.12), channel_id=1, source_target_pairs={{16,0},{65,1},{18,2},{67,3},{20,4},{69,5},{22,6},{71,7},{24,8},{73... | collective-permute-start | bytes 196616 | tf_op jit(solution)/shard_map/ppermute | solution.py:65
  5.3 1.3 %collective-permute-start = (f32[128,128]{1,0:T(8,128)}, f32[128,128]{1,0:T(8,128)S(1)}, u32[]{:S(2)}, u32[]{:S(2)}) collective-permute-start(f32[128,128]{1,0:T(8,128)} %bitcast.13), channel_id=1, source_target_pairs={{8,0},{33,1},{10,2},{35,3},{12,4},{37,5},{14,6},{39,7},{16,8},{41,... | collective-permute-start | bytes 196616 | tf_op jit(solution)/shard_map/ppermute | solution.py:65
  6.6 0.9 %copy-done = f32[8,1,2048]{2,1,0:T(1,128)S(1)} copy-done((f32[8,1,2048]{2,1,0:T(1,128)S(1)}, f32[8,1,2048]{2,1,0:T(1,128)}, u32[]{:S(2)}) %copy-start) | copy-done | bytes 65560
  7.6 0.9 %collective-permute-done.1 = f32[128,128]{1,0:T(8,128)S(1)} collective-permute-done((f32[128,128]{1,0:T(8,128)}, f32[128,128]{1,0:T(8,128)S(1)}, u32[]{:S(2)}, u32[]{:S(2)}) %collective-permute-start.1) | collective-permute-done | bytes 65568 | tf_op jit(solution)/shard_map/ppermute | solution.py:65
  8.4 1.3 %collective-permute-done = f32[128,128]{1,0:T(8,128)S(1)} collective-permute-done((f32[128,128]{1,0:T(8,128)}, f32[128,128]{1,0:T(8,128)S(1)}, u32[]{:S(2)}, u32[]{:S(2)}) %collective-permute-start) | collective-permute-done | bytes 65568 | tf_op jit(solution)/shard_map/ppermute | solution.py:65
  9.8 4.0 %collective-permute-start.6 = (f32[4,128,128]{2,1,0:T(8,128)S(1)}, f32[4,128,128]{2,1,0:T(8,128)S(1)}, u32[]{:S(2)}, u32[]{:S(2)}) collective-permute-start(f32[4,128,128]{2,1,0:T(8,128)S(1)} %pad_maximum_fusion.refs_0_), channel_id=1, source_target_pairs={{4,0},{5,1},{6,2},{7,3},{0,4},{1,5},{2,6},{3,7},{12,8},{13,9},{14,... | collective-permute-start | bytes 786440 | tf_op jit(solution)/shard_map/ppermute | solution.py:65
  13.7 3.0 %collective-permute-start.4 = (f32[4,128,128]{2,1,0:T(8,128)S(1)}, f32[4,128,128]{2,1,0:T(8,128)S(1)}, u32[]{:S(2)}, u32[]{:S(2)}) collective-permute-start(f32[4,128,128]{2,1,0:T(8,128)S(1)} %pad_maximum_fusion.refs_0_), channel_id=1, source_target_pairs={{64,0},{17,1},{66,2},{19,3},{68,4},{21,5},{70,6},{23,7},{72,8},{25... | collective-permute-start | bytes 786440 | tf_op jit(solution)/shard_map/ppermute | solution.py:65
  16.7 0.6 collective-permute-start.5
  17.3 2.6 %collective-permute-start.3 = (f32[4,128,128]{2,1,0:T(8,128)S(1)}, f32[4,128,128]{2,1,0:T(8,128)S(1)}, u32[]{:S(2)}, u32[]{:S(2)}) collective-permute-start(f32[4,128,128]{2,1,0:T(8,128)S(1)} %pad_maximum_fusion.refs_0_), channel_id=1, source_target_pairs={{32,0},{9,1},{34,2},{11,3},{36,4},{13,5},{38,6},{15,7},{40,8},{17,... | collective-permute-start | bytes 786440 | tf_op jit(solution)/shard_map/ppermute | solution.py:65
  20.0 3.2 %collective-permute-start.7 = (f32[4,128,128]{2,1,0:T(8,128)S(1)}, f32[4,128,128]{2,1,0:T(8,128)S(1)}, u32[]{:S(2)}, u32[]{:S(2)}) collective-permute-start(f32[4,128,128]{2,1,0:T(8,128)S(1)} %collective-permute-done.6.refs_4_), channel_id=1, source_target_pairs={{32,0},{9,1},{34,2},{11,3},{36,4},{13,5},{38,6},{15,7},{40,8},{17,... | collective-permute-start | bytes 786440 | tf_op jit(solution)/shard_map/ppermute | solution.py:65
  23.2 1.6 %collective-permute-start.8 = (f32[4,128,128]{2,1,0:T(8,128)S(1)}, f32[4,128,128]{2,1,0:T(8,128)S(1)}, u32[]{:S(2)}, u32[]{:S(2)}) collective-permute-start(f32[4,128,128]{2,1,0:T(8,128)S(1)} %collective-permute-done.4.refs_2_), channel_id=1, source_target_pairs={{4,0},{5,1},{6,2},{7,3},{0,4},{1,5},{2,6},{3,7},{12,8},{13,9},{14,... | collective-permute-start | bytes 786440 | tf_op jit(solution)/shard_map/ppermute | solution.py:65
  24.9 5.8 %load.1.refs_8_ = f32[8,256,2048]{2,1,0:T(8,128)S(1)} custom-call(f32[8,256,2048]{2,1,0:T(8,128)} %source_ref), custom_call_target="tpu_custom_call" | custom-call | tf_op jit(solution)/shard_map/load/pallas_call | solution.py:99
  31.1 5.4 %image.1 = f32[32,384]{1,0:T(8,128)S(1)} custom-call(s32[5]{0:T(128)S(1)} %stack.38.place_ref, f32[4,128,128]{2,1,0:T(8,128)S(1)} %pad_maximum_fusion.refs_0_, f32[4,128,128]{2,1,0:T(8,128)S(1)} %collective-permute-done.3.refs_1_, f32[4,128,128]{2,1,0:T(8,128)S(1)} %collective-permute-done.4.refs_2_, f32[4,128,128]{2,1,0:T(8,128)S(1)} %collective-permute-done.5.refs_3_, ...), custom_call_target="tpu_custom_call" | custom-call | tf_op jit(solution)/shard_map/image/pallas_call | solution.py:141
  36.6 1.2 %collective-permute-done.10 = f32[32,384]{1,0:T(8,128)S(1)} collective-permute-done((f32[32,384]{1,0:T(8,128)S(1)}, f32[32,384]{1,0:T(8,128)S(1)}, u32[]{:S(2)}, u32[]{:S(2)}) %collective-permute-start.10) | collective-permute-done | bytes 49184 | tf_op jit(solution)/shard_map/ppermute | solution.py:65
  37.9 0.8 %collective-permute-start.13 = (f32[32,384]{1,0:T(8,128)S(1)}, f32[32,384]{1,0:T(8,128)S(1)}, u32[]{:S(2)}, u32[]{:S(2)}) collective-permute-start(f32[32,384]{1,0:T(8,128)S(1)} %pad_maximum_fusion.1.refs_0_), channel_id=1, source_target_pairs={{7,0},{6,1},{1,2},{0,3},{3,4},{2,5},{5,6},{4,7},{15,8},{14,9},{9,1... | collective-permute-start | bytes 147464 | tf_op jit(solution)/shard_map/ppermute | solution.py:65
  38.7 2.2 %collective-permute-start.12 = (f32[32,384]{1,0:T(8,128)S(1)}, f32[32,384]{1,0:T(8,128)S(1)}, u32[]{:S(2)}, u32[]{:S(2)}) collective-permute-start(f32[32,384]{1,0:T(8,128)S(1)} %pad_maximum_fusion.1.refs_0_), channel_id=1, source_target_pairs={{5,0},{4,1},{7,2},{6,3},{1,4},{0,5},{3,6},{2,7},{13,8},{12,9},{15,... | collective-permute-start | bytes 147464 | tf_op jit(solution)/shard_map/ppermute | solution.py:65
  40.9 0.8 %collective-permute-start.11 = (f32[32,384]{1,0:T(8,128)S(1)}, f32[32,384]{1,0:T(8,128)S(1)}, u32[]{:S(2)}, u32[]{:S(2)}) collective-permute-start(f32[32,384]{1,0:T(8,128)S(1)} %pad_maximum_fusion.1.refs_0_), channel_id=1, source_target_pairs={{3,0},{2,1},{5,2},{4,3},{7,4},{6,5},{1,6},{0,7},{11,8},{10,9},{13,... | collective-permute-start | bytes 147464 | tf_op jit(solution)/shard_map/ppermute | solution.py:65
  41.6 1.2 %collective-permute-done.13.refs_3_ = f32[32,384]{1,0:T(8,128)S(1)} collective-permute-done((f32[32,384]{1,0:T(8,128)S(1)}, f32[32,384]{1,0:T(8,128)S(1)}, u32[]{:S(2)}, u32[]{:S(2)}) %collective-permute-start.13) | collective-permute-done | bytes 49184 | tf_op jit(solution)/shard_map/ppermute | solution.py:65
  42.8 0.9 %collective-permute-done.12.refs_2_ = f32[32,384]{1,0:T(8,128)S(1)} collective-permute-done((f32[32,384]{1,0:T(8,128)S(1)}, f32[32,384]{1,0:T(8,128)S(1)}, u32[]{:S(2)}, u32[]{:S(2)}) %collective-permute-start.12) | collective-permute-done | bytes 49184 | tf_op jit(solution)/shard_map/ppermute | solution.py:65
  43.7 0.9 %collective-permute-done.11.refs_1_ = f32[32,384]{1,0:T(8,128)S(1)} collective-permute-done((f32[32,384]{1,0:T(8,128)S(1)}, f32[32,384]{1,0:T(8,128)S(1)}, u32[]{:S(2)}, u32[]{:S(2)}) %collective-permute-start.11) | collective-permute-done | bytes 49184 | tf_op jit(solution)/shard_map/ppermute | solution.py:65
  44.6 0.9 %products.1 = (f32[32,256]{1,0:T(8,128)S(1)}, f32[32,128]{1,0:T(8,128)S(1)}) custom-call(s32[5]{0:T(128)S(1)} %stack.38.place_ref, f32[32,384]{1,0:T(8,128)S(1)} %pad_maximum_fusion.1.refs_0_, f32[32,384]{1,0:T(8,128)S(1)} %collective-permute-done.11.refs_1_, f32[32,384]{1,0:T(8,128)S(1)} %collective-permute-done.12.refs_2_, ...), custom_call_target="tpu_custom_call" | custom-call | tf_op jit(solution)/shard_map/products/pallas_call | solution.py:178
  45.5 13.9 %all_to_all.5.products_ref = f32[16,32,128]{2,1,0:T(8,128)S(1)} all-to-all(f32[16,32,128]{2,1,0:T(8,128)S(1)} %broadcast_in_dim.3), channel_id=1, replica_groups=mesh['x'=4,'y'=4,'zh'=2,'zl'=2,'core'=2] {'x','y'}, dimensions={0} | all-to-all | bytes 524288 | tf_op jit(solution)/shard_map/all_to_all | solution.py:275
  59.4 2.8 %final.1 = (f32[32,64]{1,0:T(8,128)}, f32[32,32]{1,0:T(8,128)}, f32[32,32]{1,0:T(8,128)}) custom-call(s32[5]{0:T(128)S(1)} %stack.38.place_ref, f32[16,32,128]{2,1,0:T(8,128)S(1)} %all_to_all.5.products_ref, f32[32,256]{1,0:T(8,128)S(1)} %get-tuple-element.18.image_ref, f32[32,64]{1,0:T(8,128)S(1)} %copy-done.1), custom_call_target="tpu_custom_call" | custom-call | tf_op jit(solution)/shard_map/final/pallas_call | solution.py:240
  (20 shorter events, 0.7 us)
Async XLA Ops:
  0.6 6.9 %collective-permute-start.2 = (f32[128,128]{1,0:T(8,128)}, f32[128,128]{1,0:T(8,128)S(1)}, u32[]{:S(2)}, u32[]{:S(2)}) collective-permute-start(f32[128,128]{1,0:T(8,128)} %bitcast.11), channel_id=1, source_target_pairs={{24,0},{97,1},{26,2},{99,3},{28,4},{101,5},{30,6},{103,7},{0,8},{1... | collective-permute-start | bytes 196616 | tf_op jit(solution)/shard_map/ppermute | solution.py:65
  2.4 6.1 %collective-permute-start.1 = (f32[128,128]{1,0:T(8,128)}, f32[128,128]{1,0:T(8,128)S(1)}, u32[]{:S(2)}, u32[]{:S(2)}) collective-permute-start(f32[128,128]{1,0:T(8,128)} %bitcast.12), channel_id=1, source_target_pairs={{16,0},{65,1},{18,2},{67,3},{20,4},{69,5},{22,6},{71,7},{24,8},{73... | collective-permute-start | bytes 196616 | tf_op jit(solution)/shard_map/ppermute | solution.py:65
  5.3 4.5 %collective-permute-start = (f32[128,128]{1,0:T(8,128)}, f32[128,128]{1,0:T(8,128)S(1)}, u32[]{:S(2)}, u32[]{:S(2)}) collective-permute-start(f32[128,128]{1,0:T(8,128)} %bitcast.13), channel_id=1, source_target_pairs={{8,0},{33,1},{10,2},{35,3},{12,4},{37,5},{14,6},{39,7},{16,8},{41,... | collective-permute-start | bytes 196616 | tf_op jit(solution)/shard_map/ppermute | solution.py:65
  6.6 0.9 %copy-start = (f32[8,1,2048]{2,1,0:T(1,128)S(1)}, f32[8,1,2048]{2,1,0:T(1,128)}, u32[]{:S(2)}) copy-start(f32[8,1,2048]{2,1,0:T(1,128)} %param.4) | copy-start | bytes 196612
  9.8 10.2 %collective-permute-start.6 = (f32[4,128,128]{2,1,0:T(8,128)S(1)}, f32[4,128,128]{2,1,0:T(8,128)S(1)}, u32[]{:S(2)}, u32[]{:S(2)}) collective-permute-start(f32[4,128,128]{2,1,0:T(8,128)S(1)} %pad_maximum_fusion.refs_0_), channel_id=1, source_target_pairs={{4,0},{5,1},{6,2},{7,3},{0,4},{1,5},{2,6},{3,7},{12,8},{13,9},{14,... | collective-permute-start | bytes 786440 | tf_op jit(solution)/shard_map/ppermute | solution.py:65
  13.7 9.5 %collective-permute-start.4 = (f32[4,128,128]{2,1,0:T(8,128)S(1)}, f32[4,128,128]{2,1,0:T(8,128)S(1)}, u32[]{:S(2)}, u32[]{:S(2)}) collective-permute-start(f32[4,128,128]{2,1,0:T(8,128)S(1)} %pad_maximum_fusion.refs_0_), channel_id=1, source_target_pairs={{64,0},{17,1},{66,2},{19,3},{68,4},{21,5},{70,6},{23,7},{72,8},{25... | collective-permute-start | bytes 786440 | tf_op jit(solution)/shard_map/ppermute | solution.py:65
  16.7 14.0 %collective-permute-start.5 = (f32[4,128,128]{2,1,0:T(8,128)S(1)}, f32[4,128,128]{2,1,0:T(8,128)S(1)}, u32[]{:S(2)}, u32[]{:S(2)}) collective-permute-start(f32[4,128,128]{2,1,0:T(8,128)S(1)} %pad_maximum_fusion.refs_0_), channel_id=1, source_target_pairs={{96,0},{25,1},{98,2},{27,3},{100,4},{29,5},{102,6},{31,7},{104,8},... | collective-permute-start | bytes 786440 | tf_op jit(solution)/shard_map/ppermute | solution.py:65
  17.3 13.4 %collective-permute-start.3 = (f32[4,128,128]{2,1,0:T(8,128)S(1)}, f32[4,128,128]{2,1,0:T(8,128)S(1)}, u32[]{:S(2)}, u32[]{:S(2)}) collective-permute-start(f32[4,128,128]{2,1,0:T(8,128)S(1)} %pad_maximum_fusion.refs_0_), channel_id=1, source_target_pairs={{32,0},{9,1},{34,2},{11,3},{36,4},{13,5},{38,6},{15,7},{40,8},{17,... | collective-permute-start | bytes 786440 | tf_op jit(solution)/shard_map/ppermute | solution.py:65
  20.0 10.8 %collective-permute-start.9 = (f32[4,128,128]{2,1,0:T(8,128)S(1)}, f32[4,128,128]{2,1,0:T(8,128)S(1)}, u32[]{:S(2)}, u32[]{:S(2)}) collective-permute-start(f32[4,128,128]{2,1,0:T(8,128)S(1)} %collective-permute-done.6.refs_4_), channel_id=1, source_target_pairs={{96,0},{25,1},{98,2},{27,3},{100,4},{29,5},{102,6},{31,7},{104,8},... | collective-permute-start | bytes 786440 | tf_op jit(solution)/shard_map/ppermute | solution.py:65
  20.0 10.8 %collective-permute-start.7 = (f32[4,128,128]{2,1,0:T(8,128)S(1)}, f32[4,128,128]{2,1,0:T(8,128)S(1)}, u32[]{:S(2)}, u32[]{:S(2)}) collective-permute-start(f32[4,128,128]{2,1,0:T(8,128)S(1)} %collective-permute-done.6.refs_4_), channel_id=1, source_target_pairs={{32,0},{9,1},{34,2},{11,3},{36,4},{13,5},{38,6},{15,7},{40,8},{17,... | collective-permute-start | bytes 786440 | tf_op jit(solution)/shard_map/ppermute | solution.py:65
  23.2 7.9 %collective-permute-start.8 = (f32[4,128,128]{2,1,0:T(8,128)S(1)}, f32[4,128,128]{2,1,0:T(8,128)S(1)}, u32[]{:S(2)}, u32[]{:S(2)}) collective-permute-start(f32[4,128,128]{2,1,0:T(8,128)S(1)} %collective-permute-done.4.refs_2_), channel_id=1, source_target_pairs={{4,0},{5,1},{6,2},{7,3},{0,4},{1,5},{2,6},{3,7},{12,8},{13,9},{14,... | collective-permute-start | bytes 786440 | tf_op jit(solution)/shard_map/ppermute | solution.py:65
  24.9 6.2 %copy-start.1 = (f32[32,64]{1,0:T(8,128)S(1)}, f32[32,64]{1,0:T(8,128)}, u32[]{:S(2)}) copy-start(f32[32,64]{1,0:T(8,128)} %basis_ref.1) | copy-start | bytes 24580
  36.5 1.3 %collective-permute-start.10 = (f32[32,384]{1,0:T(8,128)S(1)}, f32[32,384]{1,0:T(8,128)S(1)}, u32[]{:S(2)}, u32[]{:S(2)}) collective-permute-start(f32[32,384]{1,0:T(8,128)S(1)} %image.1), channel_id=1, source_target_pairs={{1,0},{0,1},{3,2},{2,3},{5,4},{4,5},{7,6},{6,7},{9,8},{8,9},{11,10... | collective-permute-start | bytes 147464 | tf_op jit(solution)/shard_map/ppermute | solution.py:65
  37.9 4.9 %collective-permute-start.13 = (f32[32,384]{1,0:T(8,128)S(1)}, f32[32,384]{1,0:T(8,128)S(1)}, u32[]{:S(2)}, u32[]{:S(2)}) collective-permute-start(f32[32,384]{1,0:T(8,128)S(1)} %pad_maximum_fusion.1.refs_0_), channel_id=1, source_target_pairs={{7,0},{6,1},{1,2},{0,3},{3,4},{2,5},{5,6},{4,7},{15,8},{14,9},{9,1... | collective-permute-start | bytes 147464 | tf_op jit(solution)/shard_map/ppermute | solution.py:65
  38.7 5.0 %collective-permute-start.12 = (f32[32,384]{1,0:T(8,128)S(1)}, f32[32,384]{1,0:T(8,128)S(1)}, u32[]{:S(2)}, u32[]{:S(2)}) collective-permute-start(f32[32,384]{1,0:T(8,128)S(1)} %pad_maximum_fusion.1.refs_0_), channel_id=1, source_target_pairs={{5,0},{4,1},{7,2},{6,3},{1,4},{0,5},{3,6},{2,7},{13,8},{12,9},{15,... | collective-permute-start | bytes 147464 | tf_op jit(solution)/shard_map/ppermute | solution.py:65
  40.9 3.7 %collective-permute-start.11 = (f32[32,384]{1,0:T(8,128)S(1)}, f32[32,384]{1,0:T(8,128)S(1)}, u32[]{:S(2)}, u32[]{:S(2)}) collective-permute-start(f32[32,384]{1,0:T(8,128)S(1)} %pad_maximum_fusion.1.refs_0_), channel_id=1, source_target_pairs={{3,0},{2,1},{5,2},{4,3},{7,4},{6,5},{1,6},{0,7},{11,8},{10,9},{13,... | collective-permute-start | bytes 147464 | tf_op jit(solution)/shard_map/ppermute | solution.py:65

commit v7 on v6

--- a/solution.py
+++ b/solution.py
@@ -110,11 +110,12 @@
 def image_kernel(place_ref, *refs):
     pieces, (block, basis_ref, out_ref, held, split_rows) = refs[:8], refs[8:]
     for k in range(K):
-        for j in range(LANES):
-            at = k * LANES + j
-            rows = [piece[:, at, :] for piece in pieces]
-            high, low = split(jnp.concatenate(rows, axis=0))
-            split_rows[:, at * 128 : (at + 1) * 128] = jnp.concatenate([high, low], axis=0)
+        tiles = []
+        for at in range(k * LANES, (k + 1) * LANES):
+            tiles.append(jnp.concatenate([piece[:, at, :] for piece in pieces], axis=0))
+        high, low = split(jnp.concatenate(tiles, axis=1))
+        split_rows[0:R, k * C : (k + 1) * C] = high
+        split_rows[R : 2 * R, k * C : (k + 1) * C] = low
     for r in range(0, ROWS, RB):
         total = None
         for k in range(K):

time: 62.4 us -> 62.1 us (level)
  no operation moved by 1% of the time
where the time goes in v7:
time: 62.1 us; the launch traced here: 61.9 us
  starting transfers between devices  24.9 us (40%)
  Pallas kernels  14.6 us (24%)
  blocking collectives  13.9 us (22%)
  waiting for transfers between devices  6.68 us (11%)
  local copies, waits for them, and re-layouts  0.98 us (2%)
  between operations  0.73 us (1%)
    ppermute x14, starting transfers between devices, move(): return lax.ppermute(value, AXES, pairs)  24.9 us
    all_to_all x1, blocking collectives, body(): total = lax.all_to_all(total, ('x', 'y'), 0, 0, tiled=True)  13.9 us
    ppermute x14, waiting for transfers between devices, move(): return lax.ppermute(value, AXES, pairs)  6.68 us
    pallas_call x1, Pallas kernels, load(): pl.pallas_call(load_kernel, in_specs=[pl.BlockSpec(memory_space=pltpu.HBM...  5.79 us
    pallas_call x1, Pallas kernels, image_part(): pl.pallas_call(image_kernel, in_specs=[SM] + [VM] * (len(pieces) + 2), ou...  5.16 us
    pallas_call x1, Pallas kernels, final(): pl.pallas_call(final_kernel, in_specs=[SM] + [VM] * 3, out_specs=[VM] * 3...  2.75 us
  transfers between devices with their start and end apart: 14, of which 7 were waited for; matrix products, arithmetic and copies ran while one was open for 0% of the time, Pallas kernels for 9%

profile of v7, /device:TPU:0, one launch (start us, length us, event | category | flops | bytes accessed | tf_op | source)
XLA Modules:
  0.0 61.9 jit_solution(11286891966768627535)
XLA Ops:
  0.6 1.7 %collective-permute-start.2 = (f32[128,128]{1,0:T(8,128)}, f32[128,128]{1,0:T(8,128)S(1)}, u32[]{:S(2)}, u32[]{:S(2)}) collective-permute-start(f32[128,128]{1,0:T(8,128)} %bitcast.11), channel_id=1, source_target_pairs={{24,0},{97,1},{26,2},{99,3},{28,4},{101,5},{30,6},{103,7},{0,8},{1... | collective-permute-start | bytes 196616 | tf_op jit(solution)/shard_map/ppermute | solution.py:65
  2.4 2.9 %collective-permute-start.1 = (f32[128,128]{1,0:T(8,128)}, f32[128,128]{1,0:T(8,128)S(1)}, u32[]{:S(2)}, u32[]{:S(2)}) collective-permute-start(f32[128,128]{1,0:T(8,128)} %bitcast.12), channel_id=1, source_target_pairs={{16,0},{65,1},{18,2},{67,3},{20,4},{69,5},{22,6},{71,7},{24,8},{73... | collective-permute-start | bytes 196616 | tf_op jit(solution)/shard_map/ppermute | solution.py:65
  5.3 1.3 %collective-permute-start = (f32[128,128]{1,0:T(8,128)}, f32[128,128]{1,0:T(8,128)S(1)}, u32[]{:S(2)}, u32[]{:S(2)}) collective-permute-start(f32[128,128]{1,0:T(8,128)} %bitcast.13), channel_id=1, source_target_pairs={{8,0},{33,1},{10,2},{35,3},{12,4},{37,5},{14,6},{39,7},{16,8},{41,... | collective-permute-start | bytes 196616 | tf_op jit(solution)/shard_map/ppermute | solution.py:65
  6.6 0.9 %copy-done = f32[8,1,2048]{2,1,0:T(1,128)S(1)} copy-done((f32[8,1,2048]{2,1,0:T(1,128)S(1)}, f32[8,1,2048]{2,1,0:T(1,128)}, u32[]{:S(2)}) %copy-start) | copy-done | bytes 65560
  7.6 0.9 %collective-permute-done.1 = f32[128,128]{1,0:T(8,128)S(1)} collective-permute-done((f32[128,128]{1,0:T(8,128)}, f32[128,128]{1,0:T(8,128)S(1)}, u32[]{:S(2)}, u32[]{:S(2)}) %collective-permute-start.1) | collective-permute-done | bytes 65568 | tf_op jit(solution)/shard_map/ppermute | solution.py:65
  8.4 1.3 %collective-permute-done = f32[128,128]{1,0:T(8,128)S(1)} collective-permute-done((f32[128,128]{1,0:T(8,128)}, f32[128,128]{1,0:T(8,128)S(1)}, u32[]{:S(2)}, u32[]{:S(2)}) %collective-permute-start) | collective-permute-done | bytes 65568 | tf_op jit(solution)/shard_map/ppermute | solution.py:65
  9.8 4.0 %collective-permute-start.6 = (f32[4,128,128]{2,1,0:T(8,128)S(1)}, f32[4,128,128]{2,1,0:T(8,128)S(1)}, u32[]{:S(2)}, u32[]{:S(2)}) collective-permute-start(f32[4,128,128]{2,1,0:T(8,128)S(1)} %pad_maximum_fusion.refs_0_), channel_id=1, source_target_pairs={{4,0},{5,1},{6,2},{7,3},{0,4},{1,5},{2,6},{3,7},{12,8},{13,9},{14,... | collective-permute-start | bytes 786440 | tf_op jit(solution)/shard_map/ppermute | solution.py:65
  13.7 3.0 %collective-permute-start.4 = (f32[4,128,128]{2,1,0:T(8,128)S(1)}, f32[4,128,128]{2,1,0:T(8,128)S(1)}, u32[]{:S(2)}, u32[]{:S(2)}) collective-permute-start(f32[4,128,128]{2,1,0:T(8,128)S(1)} %pad_maximum_fusion.refs_0_), channel_id=1, source_target_pairs={{64,0},{17,1},{66,2},{19,3},{68,4},{21,5},{70,6},{23,7},{72,8},{25... | collective-permute-start | bytes 786440 | tf_op jit(solution)/shard_map/ppermute | solution.py:65
  16.7 0.6 collective-permute-start.5
  17.3 2.6 %collective-permute-start.3 = (f32[4,128,128]{2,1,0:T(8,128)S(1)}, f32[4,128,128]{2,1,0:T(8,128)S(1)}, u32[]{:S(2)}, u32[]{:S(2)}) collective-permute-start(f32[4,128,128]{2,1,0:T(8,128)S(1)} %pad_maximum_fusion.refs_0_), channel_id=1, source_target_pairs={{32,0},{9,1},{34,2},{11,3},{36,4},{13,5},{38,6},{15,7},{40,8},{17,... | collective-permute-start | bytes 786440 | tf_op jit(solution)/shard_map/ppermute | solution.py:65
  20.0 3.2 %collective-permute-start.7 = (f32[4,128,128]{2,1,0:T(8,128)S(1)}, f32[4,128,128]{2,1,0:T(8,128)S(1)}, u32[]{:S(2)}, u32[]{:S(2)}) collective-permute-start(f32[4,128,128]{2,1,0:T(8,128)S(1)} %collective-permute-done.6.refs_4_), channel_id=1, source_target_pairs={{32,0},{9,1},{34,2},{11,3},{36,4},{13,5},{38,6},{15,7},{40,8},{17,... | collective-permute-start | bytes 786440 | tf_op jit(solution)/shard_map/ppermute | solution.py:65
  23.2 1.6 %collective-permute-start.8 = (f32[4,128,128]{2,1,0:T(8,128)S(1)}, f32[4,128,128]{2,1,0:T(8,128)S(1)}, u32[]{:S(2)}, u32[]{:S(2)}) collective-permute-start(f32[4,128,128]{2,1,0:T(8,128)S(1)} %collective-permute-done.4.refs_2_), channel_id=1, source_target_pairs={{4,0},{5,1},{6,2},{7,3},{0,4},{1,5},{2,6},{3,7},{12,8},{13,9},{14,... | collective-permute-start | bytes 786440 | tf_op jit(solution)/shard_map/ppermute | solution.py:65
  24.9 5.8 %load.1.refs_8_ = f32[8,256,2048]{2,1,0:T(8,128)S(1)} custom-call(f32[8,256,2048]{2,1,0:T(8,128)} %source_ref), custom_call_target="tpu_custom_call" | custom-call | tf_op jit(solution)/shard_map/load/pallas_call | solution.py:99
  31.1 5.2 %image.1 = f32[32,384]{1,0:T(8,128)S(1)} custom-call(s32[5]{0:T(128)S(1)} %stack.38.place_ref, f32[4,128,128]{2,1,0:T(8,128)S(1)} %pad_maximum_fusion.refs_0_, f32[4,128,128]{2,1,0:T(8,128)S(1)} %collective-permute-done.3.refs_1_, f32[4,128,128]{2,1,0:T(8,128)S(1)} %collective-permute-done.4.refs_2_, f32[4,128,128]{2,1,0:T(8,128)S(1)} %collective-permute-done.5.refs_3_, ...), custom_call_target="tpu_custom_call" | custom-call | tf_op jit(solution)/shard_map/image/pallas_call | solution.py:142
  36.4 1.2 %collective-permute-done.10 = f32[32,384]{1,0:T(8,128)S(1)} collective-permute-done((f32[32,384]{1,0:T(8,128)S(1)}, f32[32,384]{1,0:T(8,128)S(1)}, u32[]{:S(2)}, u32[]{:S(2)}) %collective-permute-start.10) | collective-permute-done | bytes 49184 | tf_op jit(solution)/shard_map/ppermute | solution.py:65
  37.7 0.8 %collective-permute-start.13 = (f32[32,384]{1,0:T(8,128)S(1)}, f32[32,384]{1,0:T(8,128)S(1)}, u32[]{:S(2)}, u32[]{:S(2)}) collective-permute-start(f32[32,384]{1,0:T(8,128)S(1)} %pad_maximum_fusion.1.refs_0_), channel_id=1, source_target_pairs={{7,0},{6,1},{1,2},{0,3},{3,4},{2,5},{5,6},{4,7},{15,8},{14,9},{9,1... | collective-permute-start | bytes 147464 | tf_op jit(solution)/shard_map/ppermute | solution.py:65
  38.5 2.2 %collective-permute-start.12 = (f32[32,384]{1,0:T(8,128)S(1)}, f32[32,384]{1,0:T(8,128)S(1)}, u32[]{:S(2)}, u32[]{:S(2)}) collective-permute-start(f32[32,384]{1,0:T(8,128)S(1)} %pad_maximum_fusion.1.refs_0_), channel_id=1, source_target_pairs={{5,0},{4,1},{7,2},{6,3},{1,4},{0,5},{3,6},{2,7},{13,8},{12,9},{15,... | collective-permute-start | bytes 147464 | tf_op jit(solution)/shard_map/ppermute | solution.py:65
  40.6 0.8 %collective-permute-start.11 = (f32[32,384]{1,0:T(8,128)S(1)}, f32[32,384]{1,0:T(8,128)S(1)}, u32[]{:S(2)}, u32[]{:S(2)}) collective-permute-start(f32[32,384]{1,0:T(8,128)S(1)} %pad_maximum_fusion.1.refs_0_), channel_id=1, source_target_pairs={{3,0},{2,1},{5,2},{4,3},{7,4},{6,5},{1,6},{0,7},{11,8},{10,9},{13,... | collective-permute-start | bytes 147464 | tf_op jit(solution)/shard_map/ppermute | solution.py:65
  41.4 1.2 %collective-permute-done.13.refs_3_ = f32[32,384]{1,0:T(8,128)S(1)} collective-permute-done((f32[32,384]{1,0:T(8,128)S(1)}, f32[32,384]{1,0:T(8,128)S(1)}, u32[]{:S(2)}, u32[]{:S(2)}) %collective-permute-start.13) | collective-permute-done | bytes 49184 | tf_op jit(solution)/shard_map/ppermute | solution.py:65
  42.6 0.9 %collective-permute-done.12.refs_2_ = f32[32,384]{1,0:T(8,128)S(1)} collective-permute-done((f32[32,384]{1,0:T(8,128)S(1)}, f32[32,384]{1,0:T(8,128)S(1)}, u32[]{:S(2)}, u32[]{:S(2)}) %collective-permute-start.12) | collective-permute-done | bytes 49184 | tf_op jit(solution)/shard_map/ppermute | solution.py:65
  43.5 0.9 %collective-permute-done.11.refs_1_ = f32[32,384]{1,0:T(8,128)S(1)} collective-permute-done((f32[32,384]{1,0:T(8,128)S(1)}, f32[32,384]{1,0:T(8,128)S(1)}, u32[]{:S(2)}, u32[]{:S(2)}) %collective-permute-start.11) | collective-permute-done | bytes 49184 | tf_op jit(solution)/shard_map/ppermute | solution.py:65
  44.3 0.9 %products.1 = (f32[32,256]{1,0:T(8,128)S(1)}, f32[32,128]{1,0:T(8,128)S(1)}) custom-call(s32[5]{0:T(128)S(1)} %stack.38.place_ref, f32[32,384]{1,0:T(8,128)S(1)} %pad_maximum_fusion.1.refs_0_, f32[32,384]{1,0:T(8,128)S(1)} %collective-permute-done.11.refs_1_, f32[32,384]{1,0:T(8,128)S(1)} %collective-permute-done.12.refs_2_, ...), custom_call_target="tpu_custom_call" | custom-call | tf_op jit(solution)/shard_map/products/pallas_call | solution.py:179
  45.3 13.9 %all_to_all.5.products_ref = f32[16,32,128]{2,1,0:T(8,128)S(1)} all-to-all(f32[16,32,128]{2,1,0:T(8,128)S(1)} %broadcast_in_dim.3), channel_id=1, replica_groups=mesh['x'=4,'y'=4,'zh'=2,'zl'=2,'core'=2] {'x','y'}, dimensions={0} | all-to-all | bytes 524288 | tf_op jit(solution)/shard_map/all_to_all | solution.py:276
  59.2 2.8 %final.1 = (f32[32,64]{1,0:T(8,128)}, f32[32,32]{1,0:T(8,128)}, f32[32,32]{1,0:T(8,128)}) custom-call(s32[5]{0:T(128)S(1)} %stack.38.place_ref, f32[16,32,128]{2,1,0:T(8,128)S(1)} %all_to_all.5.products_ref, f32[32,256]{1,0:T(8,128)S(1)} %get-tuple-element.18.image_ref, f32[32,64]{1,0:T(8,128)S(1)} %copy-done.1), custom_call_target="tpu_custom_call" | custom-call | tf_op jit(solution)/shard_map/final/pallas_call | solution.py:241
  (20 shorter events, 0.7 us)
Async XLA Ops:
  0.6 6.9 %collective-permute-start.2 = (f32[128,128]{1,0:T(8,128)}, f32[128,128]{1,0:T(8,128)S(1)}, u32[]{:S(2)}, u32[]{:S(2)}) collective-permute-start(f32[128,128]{1,0:T(8,128)} %bitcast.11), channel_id=1, source_target_pairs={{24,0},{97,1},{26,2},{99,3},{28,4},{101,5},{30,6},{103,7},{0,8},{1... | collective-permute-start | bytes 196616 | tf_op jit(solution)/shard_map/ppermute | solution.py:65
  2.4 6.1 %collective-permute-start.1 = (f32[128,128]{1,0:T(8,128)}, f32[128,128]{1,0:T(8,128)S(1)}, u32[]{:S(2)}, u32[]{:S(2)}) collective-permute-start(f32[128,128]{1,0:T(8,128)} %bitcast.12), channel_id=1, source_target_pairs={{16,0},{65,1},{18,2},{67,3},{20,4},{69,5},{22,6},{71,7},{24,8},{73... | collective-permute-start | bytes 196616 | tf_op jit(solution)/shard_map/ppermute | solution.py:65
  5.3 4.5 %collective-permute-start = (f32[128,128]{1,0:T(8,128)}, f32[128,128]{1,0:T(8,128)S(1)}, u32[]{:S(2)}, u32[]{:S(2)}) collective-permute-start(f32[128,128]{1,0:T(8,128)} %bitcast.13), channel_id=1, source_target_pairs={{8,0},{33,1},{10,2},{35,3},{12,4},{37,5},{14,6},{39,7},{16,8},{41,... | collective-permute-start | bytes 196616 | tf_op jit(solution)/shard_map/ppermute | solution.py:65
  6.6 0.9 %copy-start = (f32[8,1,2048]{2,1,0:T(1,128)S(1)}, f32[8,1,2048]{2,1,0:T(1,128)}, u32[]{:S(2)}) copy-start(f32[8,1,2048]{2,1,0:T(1,128)} %param.4) | copy-start | bytes 196612
  9.8 10.2 %collective-permute-start.6 = (f32[4,128,128]{2,1,0:T(8,128)S(1)}, f32[4,128,128]{2,1,0:T(8,128)S(1)}, u32[]{:S(2)}, u32[]{:S(2)}) collective-permute-start(f32[4,128,128]{2,1,0:T(8,128)S(1)} %pad_maximum_fusion.refs_0_), channel_id=1, source_target_pairs={{4,0},{5,1},{6,2},{7,3},{0,4},{1,5},{2,6},{3,7},{12,8},{13,9},{14,... | collective-permute-start | bytes 786440 | tf_op jit(solution)/shard_map/ppermute | solution.py:65
  13.7 9.5 %collective-permute-start.4 = (f32[4,128,128]{2,1,0:T(8,128)S(1)}, f32[4,128,128]{2,1,0:T(8,128)S(1)}, u32[]{:S(2)}, u32[]{:S(2)}) collective-permute-start(f32[4,128,128]{2,1,0:T(8,128)S(1)} %pad_maximum_fusion.refs_0_), channel_id=1, source_target_pairs={{64,0},{17,1},{66,2},{19,3},{68,4},{21,5},{70,6},{23,7},{72,8},{25... | collective-permute-start | bytes 786440 | tf_op jit(solution)/shard_map/ppermute | solution.py:65
  16.7 14.0 %collective-permute-start.5 = (f32[4,128,128]{2,1,0:T(8,128)S(1)}, f32[4,128,128]{2,1,0:T(8,128)S(1)}, u32[]{:S(2)}, u32[]{:S(2)}) collective-permute-start(f32[4,128,128]{2,1,0:T(8,128)S(1)} %pad_maximum_fusion.refs_0_), channel_id=1, source_target_pairs={{96,0},{25,1},{98,2},{27,3},{100,4},{29,5},{102,6},{31,7},{104,8},... | collective-permute-start | bytes 786440 | tf_op jit(solution)/shard_map/ppermute | solution.py:65
  17.3 13.4 %collective-permute-start.3 = (f32[4,128,128]{2,1,0:T(8,128)S(1)}, f32[4,128,128]{2,1,0:T(8,128)S(1)}, u32[]{:S(2)}, u32[]{:S(2)}) collective-permute-start(f32[4,128,128]{2,1,0:T(8,128)S(1)} %pad_maximum_fusion.refs_0_), channel_id=1, source_target_pairs={{32,0},{9,1},{34,2},{11,3},{36,4},{13,5},{38,6},{15,7},{40,8},{17,... | collective-permute-start | bytes 786440 | tf_op jit(solution)/shard_map/ppermute | solution.py:65
  20.0 10.8 %collective-permute-start.9 = (f32[4,128,128]{2,1,0:T(8,128)S(1)}, f32[4,128,128]{2,1,0:T(8,128)S(1)}, u32[]{:S(2)}, u32[]{:S(2)}) collective-permute-start(f32[4,128,128]{2,1,0:T(8,128)S(1)} %collective-permute-done.6.refs_4_), channel_id=1, source_target_pairs={{96,0},{25,1},{98,2},{27,3},{100,4},{29,5},{102,6},{31,7},{104,8},... | collective-permute-start | bytes 786440 | tf_op jit(solution)/shard_map/ppermute | solution.py:65
  20.0 10.8 %collective-permute-start.7 = (f32[4,128,128]{2,1,0:T(8,128)S(1)}, f32[4,128,128]{2,1,0:T(8,128)S(1)}, u32[]{:S(2)}, u32[]{:S(2)}) collective-permute-start(f32[4,128,128]{2,1,0:T(8,128)S(1)} %collective-permute-done.6.refs_4_), channel_id=1, source_target_pairs={{32,0},{9,1},{34,2},{11,3},{36,4},{13,5},{38,6},{15,7},{40,8},{17,... | collective-permute-start | bytes 786440 | tf_op jit(solution)/shard_map/ppermute | solution.py:65
  23.2 7.9 %collective-permute-start.8 = (f32[4,128,128]{2,1,0:T(8,128)S(1)}, f32[4,128,128]{2,1,0:T(8,128)S(1)}, u32[]{:S(2)}, u32[]{:S(2)}) collective-permute-start(f32[4,128,128]{2,1,0:T(8,128)S(1)} %collective-permute-done.4.refs_2_), channel_id=1, source_target_pairs={{4,0},{5,1},{6,2},{7,3},{0,4},{1,5},{2,6},{3,7},{12,8},{13,9},{14,... | collective-permute-start | bytes 786440 | tf_op jit(solution)/shard_map/ppermute | solution.py:65
  24.9 6.2 %copy-start.1 = (f32[32,64]{1,0:T(8,128)S(1)}, f32[32,64]{1,0:T(8,128)}, u32[]{:S(2)}) copy-start(f32[32,64]{1,0:T(8,128)} %basis_ref.1) | copy-start | bytes 24580
  36.3 1.3 %collective-permute-start.10 = (f32[32,384]{1,0:T(8,128)S(1)}, f32[32,384]{1,0:T(8,128)S(1)}, u32[]{:S(2)}, u32[]{:S(2)}) collective-permute-start(f32[32,384]{1,0:T(8,128)S(1)} %image.1), channel_id=1, source_target_pairs={{1,0},{0,1},{3,2},{2,3},{5,4},{4,5},{7,6},{6,7},{9,8},{8,9},{11,10... | collective-permute-start | bytes 147464 | tf_op jit(solution)/shard_map/ppermute | solution.py:65
  37.7 4.9 %collective-permute-start.13 = (f32[32,384]{1,0:T(8,128)S(1)}, f32[32,384]{1,0:T(8,128)S(1)}, u32[]{:S(2)}, u32[]{:S(2)}) collective-permute-start(f32[32,384]{1,0:T(8,128)S(1)} %pad_maximum_fusion.1.refs_0_), channel_id=1, source_target_pairs={{7,0},{6,1},{1,2},{0,3},{3,4},{2,5},{5,6},{4,7},{15,8},{14,9},{9,1... | collective-permute-start | bytes 147464 | tf_op jit(solution)/shard_map/ppermute | solution.py:65
  38.5 5.0 %collective-permute-start.12 = (f32[32,384]{1,0:T(8,128)S(1)}, f32[32,384]{1,0:T(8,128)S(1)}, u32[]{:S(2)}, u32[]{:S(2)}) collective-permute-start(f32[32,384]{1,0:T(8,128)S(1)} %pad_maximum_fusion.1.refs_0_), channel_id=1, source_target_pairs={{5,0},{4,1},{7,2},{6,3},{1,4},{0,5},{3,6},{2,7},{13,8},{12,9},{15,... | collective-permute-start | bytes 147464 | tf_op jit(solution)/shard_map/ppermute | solution.py:65
  40.6 3.7 %collective-permute-start.11 = (f32[32,384]{1,0:T(8,128)S(1)}, f32[32,384]{1,0:T(8,128)S(1)}, u32[]{:S(2)}, u32[]{:S(2)}) collective-permute-start(f32[32,384]{1,0:T(8,128)S(1)} %pad_maximum_fusion.1.refs_0_), channel_id=1, source_target_pairs={{3,0},{2,1},{5,2},{4,3},{7,4},{6,5},{1,6},{0,7},{11,8},{10,9},{13,... | collective-permute-start | bytes 147464 | tf_op jit(solution)/shard_map/ppermute | solution.py:65

commit v8 on v7

--- a/solution.py
+++ b/solution.py
@@ -193,17 +193,17 @@
 def eliminate(work):
     lane = lax.broadcasted_iota(jnp.int32, (1, 4 * R), 1)
     done = []
-    for k in range(0, R, 8):
-        columns = [jnp.broadcast_to(work[:, k + m : k + m + 1], work.shape) for m in range(8)]
-        rows = [work[k + m : k + m + 1, :] for m in range(8)]
+    for k in range(0, R, 16):
+        columns = [jnp.broadcast_to(work[:, k + m : k + m + 1], work.shape) for m in range(16)]
+        rows = [work[k + m : k + m + 1, :] for m in range(16)]
         update = jnp.zeros_like(work)
-        for m in range(8):
+        for m in range(16):
             at = k + m
             scale = lax.rsqrt(columns[m][at : at + 1, :])
             unit = rows[m] * scale
             column = columns[m] * scale
             done.append(jnp.where(lane >= at, unit, 0.0))
-            for t in range(m + 1, 8):
+            for t in range(m + 1, 16):
                 factor = columns[t][at : at + 1, :] * scale
                 rows[t] = rows[t] - column[k + t : k + t + 1, :] * unit
                 columns[t] = columns[t] - column * factor

time: 62.1 us -> 62 us (level)
  no operation moved by 1% of the time
where the time goes in v8:
time: 62 us; the launch traced here: 61.8 us
  starting transfers between devices  24.9 us (40%)
  Pallas kernels  14.6 us (24%)
  blocking collectives  13.9 us (22%)
  waiting for transfers between devices  6.68 us (11%)
  local copies, waits for them, and re-layouts  0.98 us (2%)
  between operations  0.73 us (1%)
    ppermute x14, starting transfers between devices, move(): return lax.ppermute(value, AXES, pairs)  24.9 us
    all_to_all x1, blocking collectives, body(): total = lax.all_to_all(total, ('x', 'y'), 0, 0, tiled=True)  13.9 us
    ppermute x14, waiting for transfers between devices, move(): return lax.ppermute(value, AXES, pairs)  6.68 us
    pallas_call x1, Pallas kernels, load(): pl.pallas_call(load_kernel, in_specs=[pl.BlockSpec(memory_space=pltpu.HBM...  5.79 us
    pallas_call x1, Pallas kernels, image_part(): pl.pallas_call(image_kernel, in_specs=[SM] + [VM] * (len(pieces) + 2), ou...  5.16 us
    pallas_call x1, Pallas kernels, final(): pl.pallas_call(final_kernel, in_specs=[SM] + [VM] * 3, out_specs=[VM] * 3...  2.67 us
  transfers between devices with their start and end apart: 14, of which 7 were waited for; matrix products, arithmetic and copies ran while one was open for 0% of the time, Pallas kernels for 9%

profile of v8, /device:TPU:0, one launch (start us, length us, event | category | flops | bytes accessed | tf_op | source)
XLA Modules:
  0.0 61.8 jit_solution(10963609046346203329)
XLA Ops:
  0.6 1.7 %collective-permute-start.2 = (f32[128,128]{1,0:T(8,128)}, f32[128,128]{1,0:T(8,128)S(1)}, u32[]{:S(2)}, u32[]{:S(2)}) collective-permute-start(f32[128,128]{1,0:T(8,128)} %bitcast.11), channel_id=1, source_target_pairs={{24,0},{97,1},{26,2},{99,3},{28,4},{101,5},{30,6},{103,7},{0,8},{1... | collective-permute-start | bytes 196616 | tf_op jit(solution)/shard_map/ppermute | solution.py:65
  2.4 2.9 %collective-permute-start.1 = (f32[128,128]{1,0:T(8,128)}, f32[128,128]{1,0:T(8,128)S(1)}, u32[]{:S(2)}, u32[]{:S(2)}) collective-permute-start(f32[128,128]{1,0:T(8,128)} %bitcast.12), channel_id=1, source_target_pairs={{16,0},{65,1},{18,2},{67,3},{20,4},{69,5},{22,6},{71,7},{24,8},{73... | collective-permute-start | bytes 196616 | tf_op jit(solution)/shard_map/ppermute | solution.py:65
  5.3 1.3 %collective-permute-start = (f32[128,128]{1,0:T(8,128)}, f32[128,128]{1,0:T(8,128)S(1)}, u32[]{:S(2)}, u32[]{:S(2)}) collective-permute-start(f32[128,128]{1,0:T(8,128)} %bitcast.13), channel_id=1, source_target_pairs={{8,0},{33,1},{10,2},{35,3},{12,4},{37,5},{14,6},{39,7},{16,8},{41,... | collective-permute-start | bytes 196616 | tf_op jit(solution)/shard_map/ppermute | solution.py:65
  6.6 0.9 %copy-done = f32[8,1,2048]{2,1,0:T(1,128)S(1)} copy-done((f32[8,1,2048]{2,1,0:T(1,128)S(1)}, f32[8,1,2048]{2,1,0:T(1,128)}, u32[]{:S(2)}) %copy-start) | copy-done | bytes 65560
  7.6 0.9 %collective-permute-done.1 = f32[128,128]{1,0:T(8,128)S(1)} collective-permute-done((f32[128,128]{1,0:T(8,128)}, f32[128,128]{1,0:T(8,128)S(1)}, u32[]{:S(2)}, u32[]{:S(2)}) %collective-permute-start.1) | collective-permute-done | bytes 65568 | tf_op jit(solution)/shard_map/ppermute | solution.py:65
  8.4 1.3 %collective-permute-done = f32[128,128]{1,0:T(8,128)S(1)} collective-permute-done((f32[128,128]{1,0:T(8,128)}, f32[128,128]{1,0:T(8,128)S(1)}, u32[]{:S(2)}, u32[]{:S(2)}) %collective-permute-start) | collective-permute-done | bytes 65568 | tf_op jit(solution)/shard_map/ppermute | solution.py:65
  9.8 4.0 %collective-permute-start.6 = (f32[4,128,128]{2,1,0:T(8,128)S(1)}, f32[4,128,128]{2,1,0:T(8,128)S(1)}, u32[]{:S(2)}, u32[]{:S(2)}) collective-permute-start(f32[4,128,128]{2,1,0:T(8,128)S(1)} %pad_maximum_fusion.refs_0_), channel_id=1, source_target_pairs={{4,0},{5,1},{6,2},{7,3},{0,4},{1,5},{2,6},{3,7},{12,8},{13,9},{14,... | collective-permute-start | bytes 786440 | tf_op jit(solution)/shard_map/ppermute | solution.py:65
  13.7 3.0 %collective-permute-start.4 = (f32[4,128,128]{2,1,0:T(8,128)S(1)}, f32[4,128,128]{2,1,0:T(8,128)S(1)}, u32[]{:S(2)}, u32[]{:S(2)}) collective-permute-start(f32[4,128,128]{2,1,0:T(8,128)S(1)} %pad_maximum_fusion.refs_0_), channel_id=1, source_target_pairs={{64,0},{17,1},{66,2},{19,3},{68,4},{21,5},{70,6},{23,7},{72,8},{25... | collective-permute-start | bytes 786440 | tf_op jit(solution)/shard_map/ppermute | solution.py:65
  16.7 0.6 collective-permute-start.5
  17.3 2.6 %collective-permute-start.3 = (f32[4,128,128]{2,1,0:T(8,128)S(1)}, f32[4,128,128]{2,1,0:T(8,128)S(1)}, u32[]{:S(2)}, u32[]{:S(2)}) collective-permute-start(f32[4,128,128]{2,1,0:T(8,128)S(1)} %pad_maximum_fusion.refs_0_), channel_id=1, source_target_pairs={{32,0},{9,1},{34,2},{11,3},{36,4},{13,5},{38,6},{15,7},{40,8},{17,... | collective-permute-start | bytes 786440 | tf_op jit(solution)/shard_map/ppermute | solution.py:65
  20.0 3.2 %collective-permute-start.7 = (f32[4,128,128]{2,1,0:T(8,128)S(1)}, f32[4,128,128]{2,1,0:T(8,128)S(1)}, u32[]{:S(2)}, u32[]{:S(2)}) collective-permute-start(f32[4,128,128]{2,1,0:T(8,128)S(1)} %collective-permute-done.6.refs_4_), channel_id=1, source_target_pairs={{32,0},{9,1},{34,2},{11,3},{36,4},{13,5},{38,6},{15,7},{40,8},{17,... | collective-permute-start | bytes 786440 | tf_op jit(solution)/shard_map/ppermute | solution.py:65
  23.2 1.6 %collective-permute-start.8 = (f32[4,128,128]{2,1,0:T(8,128)S(1)}, f32[4,128,128]{2,1,0:T(8,128)S(1)}, u32[]{:S(2)}, u32[]{:S(2)}) collective-permute-start(f32[4,128,128]{2,1,0:T(8,128)S(1)} %collective-permute-done.4.refs_2_), channel_id=1, source_target_pairs={{4,0},{5,1},{6,2},{7,3},{0,4},{1,5},{2,6},{3,7},{12,8},{13,9},{14,... | collective-permute-start | bytes 786440 | tf_op jit(solution)/shard_map/ppermute | solution.py:65
  24.9 5.8 %load.1.refs_8_ = f32[8,256,2048]{2,1,0:T(8,128)S(1)} custom-call(f32[8,256,2048]{2,1,0:T(8,128)} %source_ref), custom_call_target="tpu_custom_call" | custom-call | tf_op jit(solution)/shard_map/load/pallas_call | solution.py:99
  31.1 5.2 %image.1 = f32[32,384]{1,0:T(8,128)S(1)} custom-call(s32[5]{0:T(128)S(1)} %stack.38.place_ref, f32[4,128,128]{2,1,0:T(8,128)S(1)} %pad_maximum_fusion.refs_0_, f32[4,128,128]{2,1,0:T(8,128)S(1)} %collective-permute-done.3.refs_1_, f32[4,128,128]{2,1,0:T(8,128)S(1)} %collective-permute-done.4.refs_2_, f32[4,128,128]{2,1,0:T(8,128)S(1)} %collective-permute-done.5.refs_3_, ...), custom_call_target="tpu_custom_call" | custom-call | tf_op jit(solution)/shard_map/image/pallas_call | solution.py:142
  36.4 1.2 %collective-permute-done.10 = f32[32,384]{1,0:T(8,128)S(1)} collective-permute-done((f32[32,384]{1,0:T(8,128)S(1)}, f32[32,384]{1,0:T(8,128)S(1)}, u32[]{:S(2)}, u32[]{:S(2)}) %collective-permute-start.10) | collective-permute-done | bytes 49184 | tf_op jit(solution)/shard_map/ppermute | solution.py:65
  37.7 0.8 %collective-permute-start.13 = (f32[32,384]{1,0:T(8,128)S(1)}, f32[32,384]{1,0:T(8,128)S(1)}, u32[]{:S(2)}, u32[]{:S(2)}) collective-permute-start(f32[32,384]{1,0:T(8,128)S(1)} %pad_maximum_fusion.1.refs_0_), channel_id=1, source_target_pairs={{7,0},{6,1},{1,2},{0,3},{3,4},{2,5},{5,6},{4,7},{15,8},{14,9},{9,1... | collective-permute-start | bytes 147464 | tf_op jit(solution)/shard_map/ppermute | solution.py:65
  38.5 2.2 %collective-permute-start.12 = (f32[32,384]{1,0:T(8,128)S(1)}, f32[32,384]{1,0:T(8,128)S(1)}, u32[]{:S(2)}, u32[]{:S(2)}) collective-permute-start(f32[32,384]{1,0:T(8,128)S(1)} %pad_maximum_fusion.1.refs_0_), channel_id=1, source_target_pairs={{5,0},{4,1},{7,2},{6,3},{1,4},{0,5},{3,6},{2,7},{13,8},{12,9},{15,... | collective-permute-start | bytes 147464 | tf_op jit(solution)/shard_map/ppermute | solution.py:65
  40.6 0.8 %collective-permute-start.11 = (f32[32,384]{1,0:T(8,128)S(1)}, f32[32,384]{1,0:T(8,128)S(1)}, u32[]{:S(2)}, u32[]{:S(2)}) collective-permute-start(f32[32,384]{1,0:T(8,128)S(1)} %pad_maximum_fusion.1.refs_0_), channel_id=1, source_target_pairs={{3,0},{2,1},{5,2},{4,3},{7,4},{6,5},{1,6},{0,7},{11,8},{10,9},{13,... | collective-permute-start | bytes 147464 | tf_op jit(solution)/shard_map/ppermute | solution.py:65
  41.4 1.2 %collective-permute-done.13.refs_3_ = f32[32,384]{1,0:T(8,128)S(1)} collective-permute-done((f32[32,384]{1,0:T(8,128)S(1)}, f32[32,384]{1,0:T(8,128)S(1)}, u32[]{:S(2)}, u32[]{:S(2)}) %collective-permute-start.13) | collective-permute-done | bytes 49184 | tf_op jit(solution)/shard_map/ppermute | solution.py:65
  42.6 0.9 %collective-permute-done.12.refs_2_ = f32[32,384]{1,0:T(8,128)S(1)} collective-permute-done((f32[32,384]{1,0:T(8,128)S(1)}, f32[32,384]{1,0:T(8,128)S(1)}, u32[]{:S(2)}, u32[]{:S(2)}) %collective-permute-start.12) | collective-permute-done | bytes 49184 | tf_op jit(solution)/shard_map/ppermute | solution.py:65
  43.5 0.9 %collective-permute-done.11.refs_1_ = f32[32,384]{1,0:T(8,128)S(1)} collective-permute-done((f32[32,384]{1,0:T(8,128)S(1)}, f32[32,384]{1,0:T(8,128)S(1)}, u32[]{:S(2)}, u32[]{:S(2)}) %collective-permute-start.11) | collective-permute-done | bytes 49184 | tf_op jit(solution)/shard_map/ppermute | solution.py:65
  44.3 0.9 %products.1 = (f32[32,256]{1,0:T(8,128)S(1)}, f32[32,128]{1,0:T(8,128)S(1)}) custom-call(s32[5]{0:T(128)S(1)} %stack.38.place_ref, f32[32,384]{1,0:T(8,128)S(1)} %pad_maximum_fusion.1.refs_0_, f32[32,384]{1,0:T(8,128)S(1)} %collective-permute-done.11.refs_1_, f32[32,384]{1,0:T(8,128)S(1)} %collective-permute-done.12.refs_2_, ...), custom_call_target="tpu_custom_call" | custom-call | tf_op jit(solution)/shard_map/products/pallas_call | solution.py:179
  45.3 13.9 %all_to_all.5.products_ref = f32[16,32,128]{2,1,0:T(8,128)S(1)} all-to-all(f32[16,32,128]{2,1,0:T(8,128)S(1)} %broadcast_in_dim.3), channel_id=1, replica_groups=mesh['x'=4,'y'=4,'zh'=2,'zl'=2,'core'=2] {'x','y'}, dimensions={0} | all-to-all | bytes 524288 | tf_op jit(solution)/shard_map/all_to_all | solution.py:276
  59.2 2.7 %final.1 = (f32[32,64]{1,0:T(8,128)}, f32[32,32]{1,0:T(8,128)}, f32[32,32]{1,0:T(8,128)}) custom-call(s32[5]{0:T(128)S(1)} %stack.38.place_ref, f32[16,32,128]{2,1,0:T(8,128)S(1)} %all_to_all.5.products_ref, f32[32,256]{1,0:T(8,128)S(1)} %get-tuple-element.18.image_ref, f32[32,64]{1,0:T(8,128)S(1)} %copy-done.1), custom_call_target="tpu_custom_call" | custom-call | tf_op jit(solution)/shard_map/final/pallas_call | solution.py:241
  (20 shorter events, 0.7 us)
Async XLA Ops:
  0.6 6.9 %collective-permute-start.2 = (f32[128,128]{1,0:T(8,128)}, f32[128,128]{1,0:T(8,128)S(1)}, u32[]{:S(2)}, u32[]{:S(2)}) collective-permute-start(f32[128,128]{1,0:T(8,128)} %bitcast.11), channel_id=1, source_target_pairs={{24,0},{97,1},{26,2},{99,3},{28,4},{101,5},{30,6},{103,7},{0,8},{1... | collective-permute-start | bytes 196616 | tf_op jit(solution)/shard_map/ppermute | solution.py:65
  2.4 6.1 %collective-permute-start.1 = (f32[128,128]{1,0:T(8,128)}, f32[128,128]{1,0:T(8,128)S(1)}, u32[]{:S(2)}, u32[]{:S(2)}) collective-permute-start(f32[128,128]{1,0:T(8,128)} %bitcast.12), channel_id=1, source_target_pairs={{16,0},{65,1},{18,2},{67,3},{20,4},{69,5},{22,6},{71,7},{24,8},{73... | collective-permute-start | bytes 196616 | tf_op jit(solution)/shard_map/ppermute | solution.py:65
  5.3 4.5 %collective-permute-start = (f32[128,128]{1,0:T(8,128)}, f32[128,128]{1,0:T(8,128)S(1)}, u32[]{:S(2)}, u32[]{:S(2)}) collective-permute-start(f32[128,128]{1,0:T(8,128)} %bitcast.13), channel_id=1, source_target_pairs={{8,0},{33,1},{10,2},{35,3},{12,4},{37,5},{14,6},{39,7},{16,8},{41,... | collective-permute-start | bytes 196616 | tf_op jit(solution)/shard_map/ppermute | solution.py:65
  6.6 0.9 %copy-start = (f32[8,1,2048]{2,1,0:T(1,128)S(1)}, f32[8,1,2048]{2,1,0:T(1,128)}, u32[]{:S(2)}) copy-start(f32[8,1,2048]{2,1,0:T(1,128)} %param.4) | copy-start | bytes 196612
  9.8 10.2 %collective-permute-start.6 = (f32[4,128,128]{2,1,0:T(8,128)S(1)}, f32[4,128,128]{2,1,0:T(8,128)S(1)}, u32[]{:S(2)}, u32[]{:S(2)}) collective-permute-start(f32[4,128,128]{2,1,0:T(8,128)S(1)} %pad_maximum_fusion.refs_0_), channel_id=1, source_target_pairs={{4,0},{5,1},{6,2},{7,3},{0,4},{1,5},{2,6},{3,7},{12,8},{13,9},{14,... | collective-permute-start | bytes 786440 | tf_op jit(solution)/shard_map/ppermute | solution.py:65
  13.7 9.5 %collective-permute-start.4 = (f32[4,128,128]{2,1,0:T(8,128)S(1)}, f32[4,128,128]{2,1,0:T(8,128)S(1)}, u32[]{:S(2)}, u32[]{:S(2)}) collective-permute-start(f32[4,128,128]{2,1,0:T(8,128)S(1)} %pad_maximum_fusion.refs_0_), channel_id=1, source_target_pairs={{64,0},{17,1},{66,2},{19,3},{68,4},{21,5},{70,6},{23,7},{72,8},{25... | collective-permute-start | bytes 786440 | tf_op jit(solution)/shard_map/ppermute | solution.py:65
  16.7 14.0 %collective-permute-start.5 = (f32[4,128,128]{2,1,0:T(8,128)S(1)}, f32[4,128,128]{2,1,0:T(8,128)S(1)}, u32[]{:S(2)}, u32[]{:S(2)}) collective-permute-start(f32[4,128,128]{2,1,0:T(8,128)S(1)} %pad_maximum_fusion.refs_0_), channel_id=1, source_target_pairs={{96,0},{25,1},{98,2},{27,3},{100,4},{29,5},{102,6},{31,7},{104,8},... | collective-permute-start | bytes 786440 | tf_op jit(solution)/shard_map/ppermute | solution.py:65
  17.3 13.4 %collective-permute-start.3 = (f32[4,128,128]{2,1,0:T(8,128)S(1)}, f32[4,128,128]{2,1,0:T(8,128)S(1)}, u32[]{:S(2)}, u32[]{:S(2)}) collective-permute-start(f32[4,128,128]{2,1,0:T(8,128)S(1)} %pad_maximum_fusion.refs_0_), channel_id=1, source_target_pairs={{32,0},{9,1},{34,2},{11,3},{36,4},{13,5},{38,6},{15,7},{40,8},{17,... | collective-permute-start | bytes 786440 | tf_op jit(solution)/shard_map/ppermute | solution.py:65
  20.0 10.8 %collective-permute-start.9 = (f32[4,128,128]{2,1,0:T(8,128)S(1)}, f32[4,128,128]{2,1,0:T(8,128)S(1)}, u32[]{:S(2)}, u32[]{:S(2)}) collective-permute-start(f32[4,128,128]{2,1,0:T(8,128)S(1)} %collective-permute-done.6.refs_4_), channel_id=1, source_target_pairs={{96,0},{25,1},{98,2},{27,3},{100,4},{29,5},{102,6},{31,7},{104,8},... | collective-permute-start | bytes 786440 | tf_op jit(solution)/shard_map/ppermute | solution.py:65
  20.0 10.8 %collective-permute-start.7 = (f32[4,128,128]{2,1,0:T(8,128)S(1)}, f32[4,128,128]{2,1,0:T(8,128)S(1)}, u32[]{:S(2)}, u32[]{:S(2)}) collective-permute-start(f32[4,128,128]{2,1,0:T(8,128)S(1)} %collective-permute-done.6.refs_4_), channel_id=1, source_target_pairs={{32,0},{9,1},{34,2},{11,3},{36,4},{13,5},{38,6},{15,7},{40,8},{17,... | collective-permute-start | bytes 786440 | tf_op jit(solution)/shard_map/ppermute | solution.py:65
  23.2 7.9 %collective-permute-start.8 = (f32[4,128,128]{2,1,0:T(8,128)S(1)}, f32[4,128,128]{2,1,0:T(8,128)S(1)}, u32[]{:S(2)}, u32[]{:S(2)}) collective-permute-start(f32[4,128,128]{2,1,0:T(8,128)S(1)} %collective-permute-done.4.refs_2_), channel_id=1, source_target_pairs={{4,0},{5,1},{6,2},{7,3},{0,4},{1,5},{2,6},{3,7},{12,8},{13,9},{14,... | collective-permute-start | bytes 786440 | tf_op jit(solution)/shard_map/ppermute | solution.py:65
  24.9 6.2 %copy-start.1 = (f32[32,64]{1,0:T(8,128)S(1)}, f32[32,64]{1,0:T(8,128)}, u32[]{:S(2)}) copy-start(f32[32,64]{1,0:T(8,128)} %basis_ref.1) | copy-start | bytes 24580
  36.3 1.3 %collective-permute-start.10 = (f32[32,384]{1,0:T(8,128)S(1)}, f32[32,384]{1,0:T(8,128)S(1)}, u32[]{:S(2)}, u32[]{:S(2)}) collective-permute-start(f32[32,384]{1,0:T(8,128)S(1)} %image.1), channel_id=1, source_target_pairs={{1,0},{0,1},{3,2},{2,3},{5,4},{4,5},{7,6},{6,7},{9,8},{8,9},{11,10... | collective-permute-start | bytes 147464 | tf_op jit(solution)/shard_map/ppermute | solution.py:65
  37.7 4.9 %collective-permute-start.13 = (f32[32,384]{1,0:T(8,128)S(1)}, f32[32,384]{1,0:T(8,128)S(1)}, u32[]{:S(2)}, u32[]{:S(2)}) collective-permute-start(f32[32,384]{1,0:T(8,128)S(1)} %pad_maximum_fusion.1.refs_0_), channel_id=1, source_target_pairs={{7,0},{6,1},{1,2},{0,3},{3,4},{2,5},{5,6},{4,7},{15,8},{14,9},{9,1... | collective-permute-start | bytes 147464 | tf_op jit(solution)/shard_map/ppermute | solution.py:65
  38.5 5.0 %collective-permute-start.12 = (f32[32,384]{1,0:T(8,128)S(1)}, f32[32,384]{1,0:T(8,128)S(1)}, u32[]{:S(2)}, u32[]{:S(2)}) collective-permute-start(f32[32,384]{1,0:T(8,128)S(1)} %pad_maximum_fusion.1.refs_0_), channel_id=1, source_target_pairs={{5,0},{4,1},{7,2},{6,3},{1,4},{0,5},{3,6},{2,7},{13,8},{12,9},{15,... | collective-permute-start | bytes 147464 | tf_op jit(solution)/shard_map/ppermute | solution.py:65
  40.6 3.7 %collective-permute-start.11 = (f32[32,384]{1,0:T(8,128)S(1)}, f32[32,384]{1,0:T(8,128)S(1)}, u32[]{:S(2)}, u32[]{:S(2)}) collective-permute-start(f32[32,384]{1,0:T(8,128)S(1)} %pad_maximum_fusion.1.refs_0_), channel_id=1, source_target_pairs={{3,0},{2,1},{5,2},{4,3},{7,4},{6,5},{1,6},{0,7},{11,8},{10,9},{13,... | collective-permute-start | bytes 147464 | tf_op jit(solution)/shard_map/ppermute | solution.py:65
